TPU v7x, 256 devices: a whole 4x4x8 slice. The times are simulated.
256 devices in a mesh: gx: 4 (over z_hi), gy: 8 (over x, z_lo), gz: 8 (over y, core).
Axes of the slice: x: 4, y: 4, z: 8 (z_hi: 4, z_lo: 2; z = z_hi * 2 + z_lo), core: 2. Of those that a mesh axis runs over, the one named last changes fastest.
Arguments:
- weights: bfloat16 [32, 32, 32, 2, 8, 512], P('gx', 'gy', 'gz'), may hold values from -6 to 6
- angles: float32 [3, 32, 32, 32, 512], P(None, 'gx', 'gy', 'gz'), may hold values from -3.140625 to 3.140625
- translation: bfloat16 [8, 512, 512], replicated, may hold values from -0.09375 to 0.09375
Outputs:
- transformed: bfloat16 [32, 32, 32, 2, 8, 512], P('gx', 'gy', 'gz')
All inputs are finite; a program needn't handle non-finite values.
Results may differ from a plain program's by a relative error of at most 0.025.
Values may be sent and summed in bfloat16 or wider, within the bound.
No kernel may reach another device: no remote copies, remote signals or barrier semaphores. Data moves between devices by JAX's collectives and lax.ppermute only.
A program may use at most 64 MiB of HBM per device.

v0:
```python
import jax
import jax.numpy as jnp
import numpy as np
from jax import lax
from jax.experimental import pallas as pl
from jax.experimental.pallas import tpu as pltpu
from jax.sharding import Mesh
from jax.sharding import PartitionSpec as P

BITS = ("x4", "x3", "y4", "y3", "y2", "z4", "z3", "z2")
CHEB = 512
HALF = 256
BF = jnp.bfloat16
F32 = jnp.float32

SIN = (1.0, -0.1666666567325592, 0.00833332072943449, -0.00019840527966152877, 2.753572516667191e-06,
       -2.472758353633253e-08, 1.3608578153245787e-10)
COS = (1.0, -0.49999988079071045, 0.04166648909449577, -0.0013887794921174645, 2.4769700758042745e-05,
       -2.707722615014063e-07, 1.7238451777146224e-09)


def sin_cos(angle):
    square = angle * angle
    sine, cosine = jnp.full_like(square, SIN[-1]), jnp.full_like(square, COS[-1])
    for s, c in zip(SIN[-2::-1], COS[-2::-1]):
        sine, cosine = sine * square + s, cosine * square + c
    return sine * angle, cosine


def selection(source, count):
    source = np.asarray(source).reshape(-1)
    matrix = np.zeros((source.size, count), np.float32)
    matrix[np.arange(source.size), source] = 1
    return matrix


def rows(dims, order):
    return np.arange(int(np.prod(dims))).reshape(dims).transpose(order)


MIX = selection(rows((2, 8, 2, 4, 2), (1, 3, 0, 2, 4)), 256)
SEND_PHASE = selection(rows((2, 2, 2, 16), (3, 1, 2, 0)), 128)
ENTER = selection(rows((8, 4, 2, 2, 2), (0, 3, 4, 1, 2)), 256)
TURN = selection(rows((8, 2, 2, 8), (3, 1, 2, 0)), 256)
LEAVE = selection(rows((2, 2, 2, 2, 2, 2), (4, 5, 3, 1, 2, 0)), 64)


def phase_picks():
    first, second = [], []
    at = np.arange(256).reshape(4, 8, 2, 2, 2)
    for own in range(4):
        near = at[[yz ^ own for yz in range(4)]]
        first.append(selection(near[:, :, 0].transpose(3, 1, 0, 2), 256))
        second.append(selection(near[:, :, 1].transpose(3, 0, 2, 1), 256))
    return np.stack(first), np.stack(second)


def final_picks():
    at = np.arange(256).reshape(4, 8, 2, 2, 2)
    return np.stack(
        [
            selection(at[[yz ^ own for yz in range(4)]].transpose(4, 1, 2, 0, 3), 256)
            for own in range(4)
        ]
    )


FIRST, SECOND = phase_picks()
FINAL = final_picks()


def dot(a, b):
    return jnp.dot(a, b, preferred_element_type=F32)


def params():
    return pltpu.CompilerParams(vmem_limit_bytes=48 * 1024 * 1024)


def rotate_kernel(place, w_ref, a_ref, mix_ref, order_ref, send0, keep0, send1, keep1, phases, angle, mixed):
    step = pl.program_id(0)
    for level in range(3):
        for x2 in range(2):
            for y in range(4):
                angle[level, x2, 4 * y : 4 * y + 4, :] = a_ref[level, x2, 0, y]
    for x2 in range(2):
        sine, cosine = sin_cos(angle[0, x2])
        angle[0, x2] = sine
        for low in range(16):
            block = w_ref[x2, 0, 16 * low : 16 * low + 16, :].astype(F32)
            re, im = block[:8], block[8:]
            s, c = angle[0, x2, low : low + 1, :], cosine[low : low + 1]
            turned = jnp.concatenate([re * c - im * s, re * s + im * c], axis=0)
            at = 128 * x2 + 16 * (low % 8)
            mixed[low // 8, at : at + 16, :] = turned.astype(BF)
    far = angle[1:3].reshape(64, CHEB).astype(BF)
    far = jnp.concatenate([far[:, :HALF], far[:, HALF:]], axis=0)
    far = dot(order_ref[...], far).astype(BF)
    for high in range(2):
        phases[high, 0] = far[64 * high : 64 * high + 64]
    first = dot(mix_ref[...], mixed[0]).astype(BF)
    second = dot(mix_ref[...], mixed[1]).astype(BF)

    @pl.when(step < 2)
    def _():
        send0[0] = first

    @pl.when(step >= 2)
    def _():
        keep0[0] = first

    @pl.when(step % 2 == 0)
    def _():
        send1[0] = second

    @pl.when(step % 2 == 1)
    def _():
        keep1[0] = second


def rotate(place, weights, angles):
    def block(i, place):
        return (place[0] ^ (1 - i // 2)) * 2 + (place[1] ^ (1 - i % 2))

    piece = jax.ShapeDtypeStruct((2, 256, CHEB), BF)
    spec = pltpu.PrefetchScalarGridSpec(
        num_scalar_prefetch=1,
        grid=(4,),
        in_specs=[
            pl.BlockSpec((2, 1, 256, CHEB), lambda i, p: (0, block(i, p), 0, 0)),
            pl.BlockSpec((3, 2, 1, 4, 4, CHEB), lambda i, p: (0, 0, block(i, p), 0, 0, 0)),
            pl.BlockSpec((256, 256), lambda i, p: (0, 0)),
            pl.BlockSpec((128, 128), lambda i, p: (0, 0)),
        ],
        out_specs=[
            pl.BlockSpec((1, 256, CHEB), lambda i, p: (jnp.minimum(i, 1), 0, 0)),
            pl.BlockSpec((1, 256, CHEB), lambda i, p: (jnp.maximum(i - 2, 0), 0, 0)),
            pl.BlockSpec((1, 256, CHEB), lambda i, p: (i // 2, 0, 0)),
            pl.BlockSpec((1, 256, CHEB), lambda i, p: (i // 2, 0, 0)),
            pl.BlockSpec((2, 1, 64, HALF), lambda i, p: (0, block(i, p), 0, 0)),
        ],
        scratch_shapes=[pltpu.VMEM((3, 2, 16, CHEB), F32), pltpu.VMEM((2, 256, CHEB), BF)],
    )
    return pl.pallas_call(
        rotate_kernel,
        grid_spec=spec,
        out_shape=[piece] * 4 + [jax.ShapeDtypeStruct((2, 4, 64, HALF), BF)],
        compiler_params=params(),
        name="rotate",
    )(
        place,
        weights.reshape(2, 4, 256, CHEB),
        angles.reshape(3, 2, 4, 4, 4, CHEB),
        jnp.asarray(MIX, BF),
        jnp.asarray(SEND_PHASE, BF),
    )


def levels_kernel(place, x_ref, t_ref, *refs):
    near1, near2 = refs[0:4], refs[4:8]
    enter_ref, first_ref, second_ref, turn_ref, leave_ref, out_ref, left, middle, product, angle = refs[8:]
    step = pl.program_id(0)

    @pl.when(step == 0)
    def _():
        total = (x_ref[0].astype(F32) + x_ref[1].astype(F32)).astype(BF)
        left[...] = dot(enter_ref[...], total).astype(BF)

    @pl.when(step == 8)
    def _():
        left[...] = dot(turn_ref[...], middle[...]).astype(BF)

    @pl.when(step < 8)
    def _():
        held = jnp.concatenate([r[0] for r in near1], axis=0)
        angle[...] = dot(first_ref[0], held)

    @pl.when(step >= 8)
    def _():
        held = jnp.concatenate([r[...].astype(F32).reshape(64, HALF) for r in near2], axis=0)
        angle[...] = dot(second_ref[0], held.astype(BF))

    product[...] = dot(left[...], t_ref[0])
    total = [jnp.zeros((8, CHEB), F32)] * 4
    for outer in range(8):
        at = 8 * outer
        theta = jnp.concatenate([angle[at : at + 8], angle[64 + at : 72 + at]], axis=1)
        sine, cosine = sin_cos(theta)
        at = 32 * outer
        for r in range(2):
            re = product[at + 8 * r : at + 8 * r + 8]
            im = product[at + 16 + 8 * r : at + 24 + 8 * r]
            total[r] = total[r] + (re * cosine - im * sine)
            total[2 + r] = total[2 + r] + (re * sine + im * cosine)
    summed = jnp.concatenate(total, axis=0)

    @pl.when(step < 8)
    def _():
        middle[pl.ds(pl.multiple_of(step * 32, 32), 32), :] = summed.astype(BF)

    @pl.when(step >= 8)
    def _():
        value = summed.astype(BF)
        value = jnp.concatenate([value[:, :HALF], value[:, HALF:]], axis=0)
        value = dot(leave_ref[...], value)
        for t4 in range(8):
            out_ref[t4] = value[8 * t4 : 8 * t4 + 8].astype(BF)


def levels(place, share, translation, near):
    def const(*shape):
        return pl.BlockSpec(shape, lambda i, p: (0,) * len(shape))

    def own(*shape):
        return pl.BlockSpec((1, *shape), lambda i, p: (p[2],) + (0,) * len(shape))

    spec = pltpu.PrefetchScalarGridSpec(
        num_scalar_prefetch=1,
        grid=(16,),
        in_specs=[const(2, 256, CHEB), pl.BlockSpec((1, CHEB, CHEB), lambda i, p: (i % 8, 0, 0))]
        + [pl.BlockSpec((1, 64, HALF), lambda i, p: (jnp.minimum(i, 7), 0, 0))] * 4
        + [pl.BlockSpec((8, 8, HALF), lambda i, p: (0, jnp.maximum(i - 8, 0), 0))] * 4
        + [const(256, 256), own(128, 256), own(128, 256), const(256, 256), const(64, 64)],
        out_specs=pl.BlockSpec((8, 8, HALF), lambda i, p: (0, jnp.maximum(i - 8, 0), 0)),
        scratch_shapes=[
            pltpu.VMEM((256, CHEB), BF),
            pltpu.VMEM((256, CHEB), BF),
            pltpu.VMEM((256, CHEB), F32),
            pltpu.VMEM((128, HALF), F32),
        ],
    )
    return pl.pallas_call(
        levels_kernel,
        grid_spec=spec,
        out_shape=jax.ShapeDtypeStruct((8, 64, HALF), BF),
        compiler_params=params(),
        name="levels",
    )(
        place,
        share,
        translation,
        *near,
        *near,
        jnp.asarray(ENTER, BF),
        jnp.asarray(FIRST, BF),
        jnp.asarray(SECOND, BF),
        jnp.asarray(TURN, BF),
        jnp.asarray(LEAVE, BF),
    )


def final_kernel(place, n0, n1, n2, n3, pick_ref, t_ref, out_ref, left):
    for high in range(2):
        held = jnp.concatenate([r[64 * high : 64 * high + 64] for r in (n0, n1, n2, n3)], axis=0)
        value = dot(pick_ref[0], held)
        value = jnp.concatenate([value[:128], value[128:]], axis=1)
        left[128 * high : 128 * high + 128, :] = value.astype(BF)
    for x2 in range(2):
        out_ref[x2, 0] = dot(left[...], t_ref[x2, 0]).astype(BF)


def final(place, near, translation):
    spec = pltpu.PrefetchScalarGridSpec(
        num_scalar_prefetch=1,
        grid=(4,),
        in_specs=[pl.BlockSpec((128, HALF), lambda i, p: (i, 0))] * 4
        + [
            pl.BlockSpec((1, 256, 256), lambda i, p: (p[2], 0, 0)),
            pl.BlockSpec((2, 1, CHEB, CHEB), lambda i, p: (0, p[2], 0, 0)),
        ],
        out_specs=pl.BlockSpec((2, 1, 256, CHEB), lambda i, p: (0, i, 0, 0)),
        scratch_shapes=[pltpu.VMEM((256, CHEB), BF)],
    )
    return pl.pallas_call(
        final_kernel,
        grid_spec=spec,
        out_shape=jax.ShapeDtypeStruct((2, 4, 256, CHEB), BF),
        compiler_params=params(),
        name="final",
    )(place, *near, jnp.asarray(FINAL, BF), translation.reshape(2, 4, CHEB, CHEB))


def swap(value, axis):
    return lax.ppermute(value, axis, [(0, 1), (1, 0)])


def add(a, b):
    return (a.astype(F32) + b.astype(F32)).astype(BF)


def four(value):
    other = swap(value, "y2")
    return value, swap(value, "z2"), other, swap(other, "z2")


def exchange(value, axes):
    return lax.all_to_all(value, axes, split_axis=0, concat_axis=0, tiled=True)


def shards(weights, angles, translation):
    bit = lax.axis_index
    place = jnp.stack([bit("y4"), bit("z4"), 2 * bit("y2") + bit("z2")]).astype(jnp.int32)
    send0, keep0, send1, keep1, phases = rotate(place, weights, angles)
    come0, come1 = swap(send0, "y4"), swap(send1, "z4")
    again0, again1 = add(keep0[0], come0[0]), add(keep1[0], come1[0])
    come0, again0 = add(keep0[1], come0[1]), swap(again0, "z4")
    come1, again1 = add(keep1[1], come1[1]), swap(again1, "y4")
    share = jnp.stack([add(come0, again0), add(come1, again1)])
    share = exchange(share.reshape(64, 8, CHEB), ("x4", "x3", "y3", "z3", "y2", "z2"))
    phases = exchange(phases.reshape(64, 8, HALF), ("x4", "y4", "z4", "x3", "y3", "z3"))
    near = four(phases.reshape(8, 64, HALF))
    done = levels(place, share.reshape(2, 256, CHEB), translation, near)
    done = exchange(done.reshape(64, 8, HALF), ("y4", "z4", "x4", "x3", "y3", "z3"))
    near = four(done.reshape(512, HALF))
    return final(place, near, translation).reshape(weights.shape)


def solution(mesh):
    fine = Mesh(mesh.devices.reshape((2,) * len(BITS)), BITS)
    x, y, z = BITS[:2], BITS[2:5], BITS[5:]
    return jax.shard_map(
        shards,
        mesh=fine,
        in_specs=(P(x, y, z, None, None, None), P(None, x, y, z, None), P()),
        out_specs=P(x, y, z, None, None, None),
        check_vma=False,
    )
```

profile of v0, /device:TPU:1, one launch (start us, length us, event | category | flops | bytes accessed | tf_op | source)
XLA Modules:
  0.0 134.4 jit_solution(9368821589581552350)
XLA Ops:
  0.0 0.1 pad_add_fusion.place
  0.1 1.6 %copy-done.1 = bf16[8,4,4,2,8,512]{5,4,3,2,1,0:T(8,128)(2,1)S(1)} copy-done((bf16[8,4,4,2,8,512]{5,4,3,2,1,0:T(8,128)(2,1)S(1)}, bf16[8,4,4,2,8,512]{5,4,3,2,1,0:T(8,128)(2,1)}, u32[]{:S(2)}) %copy-start.1) | copy-done | bytes 2097176
  1.7 1.1 copy-done.2
  2.8 0.9 copy-done.8
  3.7 0.8 copy-done.9
  4.5 3.7 %rotate.1 = (bf16[2,256,512]{2,1,0:T(8,128)(2,1)S(1)}, bf16[2,256,512]{2,1,0:T(8,128)(2,1)S(1)}, bf16[2,256,512]{2,1,0:T(8,128)(2,1)S(1)}, bf16[2,256,512]{2,1,0:T(8,128)(2,1)S(1)}, bf16[2,4,64,256]{3,2,1,0:T(8,128)(2,1)}) custom-call(s32[3]{0:T(128)S(1)} %pad_add_fusion.place, bf16[2,4,256,512]{3,2,1,0:T(8,128)(2,1)S(1)} %bitcast.41, ...), custom_call_target="tpu_custom_call" | custom-call | tf_op jit(solution)/shard_map/rotate/pallas_call | solution.py:144
  8.2 3.6 %collective-permute-start = (bf16[2,256,512]{2,1,0:T(8,128)(2,1)S(1)}, bf16[2,256,512]{2,1,0:T(8,128)(2,1)S(1)}, u32[]{:S(2)}, u32[]{:S(2)}) collective-permute-start(bf16[2,256,512]{2,1,0:T(8,128)(2,1)S(1)} %get-tuple-element.11), channel_id=1, source_target_pairs={{0,32},{32,0},{1,33},{33,1},{2,34},{34,2},{3,35},{35,3},{4,36},{36... | collective-permute-start | bytes 1572872 | tf_op jit(solution)/shard_map/ppermute | solution.py:284
  11.8 2.9 %collective-permute-start.2 = (bf16[2,256,512]{2,1,0:T(8,128)(2,1)S(1)}, bf16[2,256,512]{2,1,0:T(8,128)(2,1)S(1)}, u32[]{:S(2)}, u32[]{:S(2)}) collective-permute-start(bf16[2,256,512]{2,1,0:T(8,128)(2,1)S(1)} %get-tuple-element.13), channel_id=1, source_target_pairs={{0,4},{4,0},{1,5},{5,1},{2,6},{6,2},{3,7},{7,3},{8,12},{12,8},{9,1... | collective-permute-start | bytes 1572872 | tf_op jit(solution)/shard_map/ppermute | solution.py:284
  14.7 7.7 %collective-permute-done = bf16[2,256,512]{2,1,0:T(8,128)(2,1)S(1)} collective-permute-done((bf16[2,256,512]{2,1,0:T(8,128)(2,1)S(1)}, bf16[2,256,512]{2,1,0:T(8,128)(2,1)S(1)}, u32[]{:S(2)}, u32[]{:S(2)}) %collective-permute-start) | collective-permute-done | bytes 524320 | tf_op jit(solution)/shard_map/ppermute | solution.py:284
  22.4 0.8 fusion.3
  23.1 3.9 %collective-permute-start.1 = (bf16[256,512]{1,0:T(8,128)(2,1)}, bf16[256,512]{1,0:T(8,128)(2,1)}, u32[]{:S(2)}, u32[]{:S(2)}) collective-permute-start(bf16[256,512]{1,0:T(8,128)(2,1)} %fusion.3), channel_id=1, source_target_pairs={{0,4},{4,0},{1,5},{5,1},{2,6},{6,2},{3,7},{7,3},{8,12},{12,8},{9,1... | collective-permute-start | bytes 786440 | tf_op jit(solution)/shard_map/ppermute | solution.py:284
  27.0 0.8 fusion.5
  27.8 2.8 %collective-permute-start.3 = (bf16[256,512]{1,0:T(8,128)(2,1)}, bf16[256,512]{1,0:T(8,128)(2,1)}, u32[]{:S(2)}, u32[]{:S(2)}) collective-permute-start(bf16[256,512]{1,0:T(8,128)(2,1)} %fusion.5), channel_id=1, source_target_pairs={{0,32},{32,0},{1,33},{33,1},{2,34},{34,2},{3,35},{35,3},{4,36},{36... | collective-permute-start | bytes 786440 | tf_op jit(solution)/shard_map/ppermute | solution.py:284
  30.5 10.5 %all-to-all-start.1 = ((bf16[64,8,256]{2,1,0:T(8,128)(2,1)}), bf16[64,8,256]{2,1,0:T(8,128)(2,1)S(1)}, u32[]{:S(2)}, u32[]{:S(2)}) async-start(bf16[64,8,256]{2,1,0:T(8,128)(2,1)} %bitcast.13), calls=%async_computation.1 | async-start | bytes 524288 | tf_op jit(solution)/shard_map/all_to_all | solution.py:297
  41.1 1.1 fusion.6
  42.3 1.1 fusion.7
  43.3 0.8 pad_maximum_fusion
  44.2 9.5 %all-to-all-done.1 = bf16[64,8,256]{2,1,0:T(8,128)(2,1)S(1)} async-done(((bf16[64,8,256]{2,1,0:T(8,128)(2,1)}), bf16[64,8,256]{2,1,0:T(8,128)(2,1)S(1)}, u32[]{:S(2)}, u32[]{:S(2)}) %all-to-all-start.1) | async-done | bytes 262176 | tf_op jit(solution)/shard_map/all_to_all | solution.py:297
  53.7 7.7 %all-to-all-start = ((bf16[64,8,512]{2,1,0:T(8,128)(2,1)}), bf16[64,8,512]{2,1,0:T(8,128)(2,1)S(1)}, u32[]{:S(2)}, u32[]{:S(2)}) async-start(bf16[64,8,512]{2,1,0:T(8,128)(2,1)} %bitcast.11), calls=%async_computation | async-start | bytes 1048576 | tf_op jit(solution)/shard_map/all_to_all | solution.py:297
  61.4 1.5 %collective-permute-start.5 = (bf16[8,64,256]{2,1,0:T(8,128)(2,1)S(1)}, bf16[8,64,256]{2,1,0:T(8,128)(2,1)S(1)}, u32[]{:S(2)}, u32[]{:S(2)}) collective-permute-start(bf16[8,64,256]{2,1,0:T(8,128)(2,1)S(1)} %bitcast.36), channel_id=1, source_target_pairs={{0,8},{8,0},{1,9},{9,1},{2,10},{10,2},{3,11},{11,3},{4,12},{12,4},... | collective-permute-start | bytes 786440 | tf_op jit(solution)/shard_map/ppermute | solution.py:284
  62.9 0.6 collective-permute-start.4
  63.5 16.7 %collective-permute-done.5.refs_2_.refs_6_ = bf16[8,64,256]{2,1,0:T(8,128)(2,1)S(1)} collective-permute-done((bf16[8,64,256]{2,1,0:T(8,128)(2,1)S(1)}, bf16[8,64,256]{2,1,0:T(8,128)(2,1)S(1)}, u32[]{:S(2)}, u32[]{:S(2)}) %collective-permute-start.5) | collective-permute-done | bytes 262176 | tf_op jit(solution)/shard_map/ppermute | solution.py:284
  80.3 0.9 collective-permute-start.6
  81.1 1.2 collective-permute-done.6.refs_3_.refs_7_
  82.3 15.4 %levels.1 = bf16[8,64,256]{2,1,0:T(8,128)(2,1)S(1)} custom-call(s32[3]{0:T(128)S(1)} %pad_add_fusion.place, bf16[2,256,512]{2,1,0:T(8,128)(2,1)S(1)} %bitcast.40, bf16[8,512,512]{2,1,0:T(8,128)(2,1)} %t_ref.1, bf16[8,64,256]{2,1,0:T(8,128)(2,1)S(1)} %bitcast.38, bf16[8,64,256]{2,1,0:T(8,128)(2,1)S(1)} %collective-permute-done.4.refs_1_.refs_5_, ...), custom_call_target="tpu_custom_call" | custom-call | tf_op jit(solution)/shard_map/levels/pallas_call | solution.py:232
  97.8 21.9 %all_to_all.15 = bf16[64,8,256]{2,1,0:T(8,128)(2,1)S(1)} all-to-all(bf16[64,8,256]{2,1,0:T(8,128)(2,1)S(1)} %bitcast.45), channel_id=1, replica_groups=mesh['x4'=2,'x3'=2,'y4'=2,'y3'=2,'y2'=2,'z4'=2,'z3'=2,'z2'=2] {'y4','z4'..., dimensions={0} | all-to-all | bytes 524288 | tf_op jit(solution)/shard_map/all_to_all | solution.py:297
  119.7 1.8 %collective-permute-start.8 = (bf16[512,256]{1,0:T(8,128)(2,1)S(1)}, bf16[512,256]{1,0:T(8,128)(2,1)S(1)}, u32[]{:S(2)}, u32[]{:S(2)}) collective-permute-start(bf16[512,256]{1,0:T(8,128)(2,1)S(1)} %bitcast.42), channel_id=1, source_target_pairs={{0,8},{8,0},{1,9},{9,1},{2,10},{10,2},{3,11},{11,3},{4,12},{12,4},... | collective-permute-start | bytes 786440 | tf_op jit(solution)/shard_map/ppermute | solution.py:284
  121.5 2.4 %collective-permute-start.7 = (bf16[512,256]{1,0:T(8,128)(2,1)S(1)}, bf16[512,256]{1,0:T(8,128)(2,1)S(1)}, u32[]{:S(2)}, u32[]{:S(2)}) collective-permute-start(bf16[512,256]{1,0:T(8,128)(2,1)S(1)} %bitcast.43), channel_id=1, source_target_pairs={{0,1},{1,0},{2,3},{3,2},{4,5},{5,4},{6,7},{7,6},{8,9},{9,8},{10,11... | collective-permute-start | bytes 786440 | tf_op jit(solution)/shard_map/ppermute | solution.py:284
  123.8 1.4 %collective-permute-done.8.n2 = bf16[512,256]{1,0:T(8,128)(2,1)S(1)} collective-permute-done((bf16[512,256]{1,0:T(8,128)(2,1)S(1)}, bf16[512,256]{1,0:T(8,128)(2,1)S(1)}, u32[]{:S(2)}, u32[]{:S(2)}) %collective-permute-start.8) | collective-permute-done | bytes 262176 | tf_op jit(solution)/shard_map/ppermute | solution.py:284
  125.2 4.1 %collective-permute-start.9 = (bf16[512,256]{1,0:T(8,128)(2,1)S(1)}, bf16[512,256]{1,0:T(8,128)(2,1)S(1)}, u32[]{:S(2)}, u32[]{:S(2)}) collective-permute-start(bf16[512,256]{1,0:T(8,128)(2,1)S(1)} %collective-permute-done.8.n2), channel_id=1, source_target_pairs={{0,1},{1,0},{2,3},{3,2},{4,5},{5,4},{6,7},{7,6},{8,9},{9,8},{10,11... | collective-permute-start | bytes 786440 | tf_op jit(solution)/shard_map/ppermute | solution.py:284
  129.3 1.2 collective-permute-done.9.n3
  130.5 4.0 %final.1 = bf16[2,4,256,512]{3,2,1,0:T(8,128)(2,1)} custom-call(s32[3]{0:T(128)S(1)} %pad_add_fusion.place, bf16[512,256]{1,0:T(8,128)(2,1)S(1)} %bitcast.44, bf16[512,256]{1,0:T(8,128)(2,1)S(1)} %collective-permute-done.7.n1, bf16[512,256]{1,0:T(8,128)(2,1)S(1)} %collective-permute-done.8.n2, bf16[512,256]{1,0:T(8,128)(2,1)S(1)} %collective-permute-done.9.n3, ...), custom_call_target="tpu_custom_call" | custom-call | tf_op jit(solution)/shard_map/final/pallas_call | solution.py:274
  (24 shorter events, 0.1 us)
Async XLA Ops:
  0.1 1.6 %copy-start.1 = (bf16[8,4,4,2,8,512]{5,4,3,2,1,0:T(8,128)(2,1)S(1)}, bf16[8,4,4,2,8,512]{5,4,3,2,1,0:T(8,128)(2,1)}, u32[]{:S(2)}) copy-start(bf16[8,4,4,2,8,512]{5,4,3,2,1,0:T(8,128)(2,1)} %param.11) | copy-start | bytes 6291460
  1.7 1.1 copy-start.2
  2.8 0.9 copy-start.8
  3.7 0.8 copy-start.9
  8.2 14.2 %collective-permute-start = (bf16[2,256,512]{2,1,0:T(8,128)(2,1)S(1)}, bf16[2,256,512]{2,1,0:T(8,128)(2,1)S(1)}, u32[]{:S(2)}, u32[]{:S(2)}) collective-permute-start(bf16[2,256,512]{2,1,0:T(8,128)(2,1)S(1)} %get-tuple-element.11), channel_id=1, source_target_pairs={{0,32},{32,0},{1,33},{33,1},{2,34},{34,2},{3,35},{35,3},{4,36},{36... | collective-permute-start | bytes 1572872 | tf_op jit(solution)/shard_map/ppermute | solution.py:284
  11.8 15.2 %collective-permute-start.2 = (bf16[2,256,512]{2,1,0:T(8,128)(2,1)S(1)}, bf16[2,256,512]{2,1,0:T(8,128)(2,1)S(1)}, u32[]{:S(2)}, u32[]{:S(2)}) collective-permute-start(bf16[2,256,512]{2,1,0:T(8,128)(2,1)S(1)} %get-tuple-element.13), channel_id=1, source_target_pairs={{0,4},{4,0},{1,5},{5,1},{2,6},{6,2},{3,7},{7,3},{8,12},{12,8},{9,1... | collective-permute-start | bytes 1572872 | tf_op jit(solution)/shard_map/ppermute | solution.py:284
  23.1 18.0 %collective-permute-start.1 = (bf16[256,512]{1,0:T(8,128)(2,1)}, bf16[256,512]{1,0:T(8,128)(2,1)}, u32[]{:S(2)}, u32[]{:S(2)}) collective-permute-start(bf16[256,512]{1,0:T(8,128)(2,1)} %fusion.3), channel_id=1, source_target_pairs={{0,4},{4,0},{1,5},{5,1},{2,6},{6,2},{3,7},{7,3},{8,12},{12,8},{9,1... | collective-permute-start | bytes 786440 | tf_op jit(solution)/shard_map/ppermute | solution.py:284
  27.8 14.5 %collective-permute-start.3 = (bf16[256,512]{1,0:T(8,128)(2,1)}, bf16[256,512]{1,0:T(8,128)(2,1)}, u32[]{:S(2)}, u32[]{:S(2)}) collective-permute-start(bf16[256,512]{1,0:T(8,128)(2,1)} %fusion.5), channel_id=1, source_target_pairs={{0,32},{32,0},{1,33},{33,1},{2,34},{34,2},{3,35},{35,3},{4,36},{36... | collective-permute-start | bytes 786440 | tf_op jit(solution)/shard_map/ppermute | solution.py:284
  30.5 23.1 %all-to-all-start.1 = ((bf16[64,8,256]{2,1,0:T(8,128)(2,1)}), bf16[64,8,256]{2,1,0:T(8,128)(2,1)S(1)}, u32[]{:S(2)}, u32[]{:S(2)}) async-start(bf16[64,8,256]{2,1,0:T(8,128)(2,1)} %bitcast.13), calls=%async_computation.1 | async-start | bytes 524288 | tf_op jit(solution)/shard_map/all_to_all | solution.py:297
  41.1 41.2 %copy-start.4 = (bf16[4,128,256]{2,1,0:T(8,128)(2,1)S(1)}, bf16[4,128,256]{2,1,0:T(8,128)(2,1)}, u32[]{:S(2)}) copy-start(bf16[4,128,256]{2,1,0:T(8,128)(2,1)} %constant.37.clone.refs_9_) | copy-start | bytes 786436
  41.1 41.2 %copy-start.5 = (bf16[4,128,256]{2,1,0:T(8,128)(2,1)S(1)}, bf16[4,128,256]{2,1,0:T(8,128)(2,1)}, u32[]{:S(2)}) copy-start(bf16[4,128,256]{2,1,0:T(8,128)(2,1)} %constant.38.clone.refs_10_) | copy-start | bytes 786436
  41.1 41.2 %copy-start.6 = (bf16[256,256]{1,0:T(8,128)(2,1)S(1)}, bf16[256,256]{1,0:T(8,128)(2,1)}, u32[]{:S(2)}) copy-start(bf16[256,256]{1,0:T(8,128)(2,1)} %constant.36.clone.refs_8_) | copy-start | bytes 393220
  41.1 41.2 %copy-start.7 = (bf16[256,256]{1,0:T(8,128)(2,1)S(1)}, bf16[256,256]{1,0:T(8,128)(2,1)}, u32[]{:S(2)}) copy-start(bf16[256,256]{1,0:T(8,128)(2,1)} %constant.39.clone.refs_11_) | copy-start | bytes 393220
  41.1 41.2 %copy-start.10 = (bf16[64,64]{1,0:T(8,128)(2,1)S(1)}, bf16[64,64]{1,0:T(8,128)(2,1)}, u32[]{:S(2)}) copy-start(bf16[64,64]{1,0:T(8,128)(2,1)} %constant.40.clone.refs_12_) | copy-start | bytes 24580
  53.7 28.6 %all-to-all-start = ((bf16[64,8,512]{2,1,0:T(8,128)(2,1)}), bf16[64,8,512]{2,1,0:T(8,128)(2,1)S(1)}, u32[]{:S(2)}, u32[]{:S(2)}) async-start(bf16[64,8,512]{2,1,0:T(8,128)(2,1)} %bitcast.11), calls=%async_computation | async-start | bytes 1048576 | tf_op jit(solution)/shard_map/all_to_all | solution.py:297
  61.4 18.9 %collective-permute-start.5 = (bf16[8,64,256]{2,1,0:T(8,128)(2,1)S(1)}, bf16[8,64,256]{2,1,0:T(8,128)(2,1)S(1)}, u32[]{:S(2)}, u32[]{:S(2)}) collective-permute-start(bf16[8,64,256]{2,1,0:T(8,128)(2,1)S(1)} %bitcast.36), channel_id=1, source_target_pairs={{0,8},{8,0},{1,9},{9,1},{2,10},{10,2},{3,11},{11,3},{4,12},{12,4},... | collective-permute-start | bytes 786440 | tf_op jit(solution)/shard_map/ppermute | solution.py:284
  62.9 18.3 %collective-permute-start.4 = (bf16[8,64,256]{2,1,0:T(8,128)(2,1)S(1)}, bf16[8,64,256]{2,1,0:T(8,128)(2,1)S(1)}, u32[]{:S(2)}, u32[]{:S(2)}) collective-permute-start(bf16[8,64,256]{2,1,0:T(8,128)(2,1)S(1)} %bitcast.37), channel_id=1, source_target_pairs={{0,1},{1,0},{2,3},{3,2},{4,5},{5,4},{6,7},{7,6},{8,9},{9,8},{10,11... | collective-permute-start | bytes 786440 | tf_op jit(solution)/shard_map/ppermute | solution.py:284
  80.3 2.0 %collective-permute-start.6 = (bf16[8,64,256]{2,1,0:T(8,128)(2,1)S(1)}, bf16[8,64,256]{2,1,0:T(8,128)(2,1)S(1)}, u32[]{:S(2)}, u32[]{:S(2)}) collective-permute-start(bf16[8,64,256]{2,1,0:T(8,128)(2,1)S(1)} %collective-permute-done.5.refs_2_.refs_6_), channel_id=1, source_target_pairs={{0,1},{1,0},{2,3},{3,2},{4,5},{5,4},{6,7},{7,6},{8,9},{9,8},{10,11... | collective-permute-start | bytes 786440 | tf_op jit(solution)/shard_map/ppermute | solution.py:284
  82.3 48.1 %copy-start = (bf16[8,512,512]{2,1,0:T(8,128)(2,1)S(1)}, bf16[8,512,512]{2,1,0:T(8,128)(2,1)}, u32[]{:S(2)}) copy-start(bf16[8,512,512]{2,1,0:T(8,128)(2,1)} %t_ref.1) | copy-start | bytes 12582916
  82.3 48.1 %copy-start.3 = (bf16[4,256,256]{2,1,0:T(8,128)(2,1)S(1)}, bf16[4,256,256]{2,1,0:T(8,128)(2,1)}, u32[]{:S(2)}) copy-start(bf16[4,256,256]{2,1,0:T(8,128)(2,1)} %constant.41.clone.pick_ref) | copy-start | bytes 1572868
  119.7 5.5 %collective-permute-start.8 = (bf16[512,256]{1,0:T(8,128)(2,1)S(1)}, bf16[512,256]{1,0:T(8,128)(2,1)S(1)}, u32[]{:S(2)}, u32[]{:S(2)}) collective-permute-start(bf16[512,256]{1,0:T(8,128)(2,1)S(1)} %bitcast.42), channel_id=1, source_target_pairs={{0,8},{8,0},{1,9},{9,1},{2,10},{10,2},{3,11},{11,3},{4,12},{12,4},... | collective-permute-start | bytes 786440 | tf_op jit(solution)/shard_map/ppermute | solution.py:284
  121.5 7.8 %collective-permute-start.7 = (bf16[512,256]{1,0:T(8,128)(2,1)S(1)}, bf16[512,256]{1,0:T(8,128)(2,1)S(1)}, u32[]{:S(2)}, u32[]{:S(2)}) collective-permute-start(bf16[512,256]{1,0:T(8,128)(2,1)S(1)} %bitcast.43), channel_id=1, source_target_pairs={{0,1},{1,0},{2,3},{3,2},{4,5},{5,4},{6,7},{7,6},{8,9},{9,8},{10,11... | collective-permute-start | bytes 786440 | tf_op jit(solution)/shard_map/ppermute | solution.py:284
  125.2 5.2 %collective-permute-start.9 = (bf16[512,256]{1,0:T(8,128)(2,1)S(1)}, bf16[512,256]{1,0:T(8,128)(2,1)S(1)}, u32[]{:S(2)}, u32[]{:S(2)}) collective-permute-start(bf16[512,256]{1,0:T(8,128)(2,1)S(1)} %collective-permute-done.8.n2), channel_id=1, source_target_pairs={{0,1},{1,0},{2,3},{3,2},{4,5},{5,4},{6,7},{7,6},{8,9},{9,8},{10,11... | collective-permute-start | bytes 786440 | tf_op jit(solution)/shard_map/ppermute | solution.py:284
where the time goes:
time: 135 us; the launch traced here: 134 us
  starting transfers between devices  42.6 us (32%)
  waiting for transfers between devices  37.6 us (28%)
  Pallas kernels  23.1 us (17%)
  blocking collectives  21.9 us (16%)
  other arithmetic  4.61 us (3%)
  local copies, waits for them, and re-layouts  4.43 us (3%)
    ppermute x10, waiting for transfers between devices, swap(): return lax.ppermute(value, axis, [(0, 1), (1, 0)])  28.1 us
    ppermute x10, starting transfers between devices, swap(): return lax.ppermute(value, axis, [(0, 1), (1, 0)])  24.3 us
    all_to_all x1, blocking collectives, exchange(): return lax.all_to_all(value, axes, split_axis=0, concat_axis=0, tiled=True)  21.9 us
    all_to_all x2, starting transfers between devices, exchange(): return lax.all_to_all(value, axes, split_axis=0, concat_axis=0, tiled=True)  18.2 us
    pallas_call x1, Pallas kernels, levels(): pl.pallas_call(levels_kernel, grid_spec=spec, out_shape=jax.ShapeDtypeStr...  15.4 us
    all_to_all x2, waiting for transfers between devices, exchange(): return lax.all_to_all(value, axes, split_axis=0, concat_axis=0, tiled=True)  9.52 us
    unnamed x22, local copies, waits for them, and re-layouts  4.43 us
    pallas_call x1, Pallas kernels, final(): pl.pallas_call(final_kernel, grid_spec=spec, out_shape=jax.ShapeDtypeStru...  3.97 us
  transfers between devices with their start and end apart: 12, of which 6 were waited for; matrix products, arithmetic and copies ran while one was open for 3% of the time, Pallas kernels for 0%

commit v1 on v0

v1 whole, which is shorter than its diff:
```python
import jax
import jax.numpy as jnp
import numpy as np
from jax import lax
from jax.experimental import pallas as pl
from jax.experimental.pallas import tpu as pltpu
from jax.sharding import Mesh
from jax.sharding import PartitionSpec as P

BITS = ("x4", "x3", "y4", "y3", "y2", "z4", "z3", "z2")
CHEB = 512
HALF = 256
BF = jnp.bfloat16
F32 = jnp.float32

SIN = (1.0, -0.1666666567325592, 0.00833332072943449, -0.00019840527966152877, 2.753572516667191e-06,
       -2.472758353633253e-08, 1.3608578153245787e-10)
COS = (1.0, -0.49999988079071045, 0.04166648909449577, -0.0013887794921174645, 2.4769700758042745e-05,
       -2.707722615014063e-07, 1.7238451777146224e-09)


def sin_cos(angle):
    square = angle * angle
    sine, cosine = jnp.full_like(square, SIN[-1]), jnp.full_like(square, COS[-1])
    for s, c in zip(SIN[-2::-1], COS[-2::-1]):
        sine, cosine = sine * square + s, cosine * square + c
    return sine * angle, cosine


def selection(source, count):
    source = np.asarray(source).reshape(-1)
    matrix = np.zeros((source.size, count), np.float32)
    matrix[np.arange(source.size), source] = 1
    return matrix


def rows(dims, order):
    return np.arange(int(np.prod(dims))).reshape(dims).transpose(order)


MIX = selection(rows((2, 8, 2, 4, 2), (1, 3, 0, 2, 4)), 256)
SEND_PHASE = selection(rows((2, 2, 2, 16), (3, 1, 2, 0)), 128)
ENTER = selection(rows((8, 4, 2, 2, 2), (0, 3, 4, 1, 2)), 256)
TURN = selection(rows((8, 2, 2, 8), (3, 1, 2, 0)), 256)
LEAVE = selection(rows((2, 2, 2, 2, 2, 2), (4, 5, 3, 1, 2, 0)), 64)


def phase_picks():
    first, second = [], []
    at = np.arange(256).reshape(4, 8, 2, 2, 2)
    for own in range(4):
        near = at[[yz ^ own for yz in range(4)]]
        first.append(selection(near[:, :, 0].transpose(3, 1, 0, 2), 256))
        second.append(selection(near[:, :, 1].transpose(3, 0, 2, 1), 256))
    return np.stack(first), np.stack(second)


def final_picks():
    at = np.arange(256).reshape(4, 8, 2, 2, 2)
    return np.stack(
        [
            selection(at[[yz ^ own for yz in range(4)]].transpose(4, 1, 2, 0, 3), 256)
            for own in range(4)
        ]
    )


FIRST, SECOND = phase_picks()
FINAL = final_picks()


def dot(a, b):
    return jnp.dot(a, b, preferred_element_type=F32)


def in_hbm(value):
    return pltpu.with_memory_space_constraint(value, pltpu.HBM)


def params(mebibytes):
    return pltpu.CompilerParams(vmem_limit_bytes=mebibytes * 1024 * 1024)


def rotate_half(w_ref, a_ref, mix_ref, first, second, angle, mixed):
    step = pl.program_id(0)
    for x2 in range(2):
        for y in range(2):
            angle[x2, 4 * y : 4 * y + 4, :] = a_ref[0, x2, 0, y]
        sine, cosine = sin_cos(angle[x2])
        for low in range(8):
            block = w_ref[x2, 0, 16 * low : 16 * low + 16, :].astype(F32)
            re, im = block[:8], block[8:]
            s, c = sine[low : low + 1], cosine[low : low + 1]
            turned = jnp.concatenate([re * c - im * s, re * s + im * c], axis=0)
            at = 128 * x2 + 16 * low
            mixed[at : at + 16, :] = turned.astype(BF)
    value = dot(mix_ref[...], mixed[...]).astype(BF)

    @pl.when(step < 2)
    def _():
        first[0] = value

    @pl.when(step >= 2)
    def _():
        second[0] = value


def send_kernel(place, w_ref, a_ref, mix_ref, first, second, angle, mixed):
    rotate_half(w_ref, a_ref, mix_ref, first, second, angle, mixed)


def keep_kernel(place, w_ref, a_ref, mix_ref, a1_ref, a2_ref, order_ref, first, second, phases, angle, mixed, far):
    rotate_half(w_ref, a_ref, mix_ref, first, second, angle, mixed)
    for level, ref in enumerate((a1_ref, a2_ref)):
        for x2 in range(2):
            for y in range(4):
                at = 32 * level + 16 * x2 + 4 * y
                far[at : at + 4, :] = ref[0, x2, 0, y]
    value = far[...].astype(BF)
    value = jnp.concatenate([value[:, :HALF], value[:, HALF:]], axis=0)
    value = dot(order_ref[...], value).astype(BF)
    for high in range(2):
        phases[high, 0] = value[64 * high : 64 * high + 64]


def rotate(place, weights, angles, keep):
    def block(j, place):
        if keep:
            y, z = jnp.where(j == 2, 0, 1), jnp.where(j == 0, 0, 1)
        else:
            y, z = jnp.where(j == 3, 1, 0), jnp.where(j == 1, 1, 0)
        return (place[0] ^ (1 - y)) * 2 + (place[1] ^ (1 - z))

    piece = jax.ShapeDtypeStruct((2, 256, CHEB), BF)
    in_specs = [
        pl.BlockSpec((2, 1, 128, CHEB), lambda j, p: (0, block(j, p), j // 2, 0)),
        pl.BlockSpec((1, 2, 1, 2, 4, CHEB), lambda j, p: (0, 0, block(j, p), j // 2, 0, 0)),
        pl.BlockSpec((256, 256), lambda j, p: (0, 0)),
    ]
    out_specs = [
        pl.BlockSpec((1, 256, CHEB), lambda j, p: (jnp.minimum(j, 1), 0, 0)),
        pl.BlockSpec((1, 256, CHEB), lambda j, p: (jnp.maximum(j - 2, 0), 0, 0)),
    ]
    out_shape = [piece] * 2
    scratch = [pltpu.VMEM((2, 8, CHEB), F32), pltpu.VMEM((256, CHEB), BF)]
    args = [weights, angles, jnp.asarray(MIX, BF)]
    if keep:
        in_specs += [
            pl.BlockSpec((1, 2, 1, 4, 4, CHEB), lambda j, p: (1, 0, j, 0, 0, 0)),
            pl.BlockSpec((1, 2, 1, 4, 4, CHEB), lambda j, p: (2, 0, j, 0, 0, 0)),
            pl.BlockSpec((128, 128), lambda j, p: (0, 0)),
        ]
        out_specs.append(pl.BlockSpec((2, 1, 64, HALF), lambda j, p: (0, j, 0, 0)))
        out_shape.append(jax.ShapeDtypeStruct((2, 4, 64, HALF), BF))
        scratch.append(pltpu.VMEM((64, CHEB), F32))
        args += [angles, angles, jnp.asarray(SEND_PHASE, BF)]
    spec = pltpu.PrefetchScalarGridSpec(
        num_scalar_prefetch=1, grid=(4,), in_specs=in_specs, out_specs=out_specs, scratch_shapes=scratch
    )
    return pl.pallas_call(
        keep_kernel if keep else send_kernel,
        grid_spec=spec,
        out_shape=out_shape,
        compiler_params=params(12),
        name="rotate_kept" if keep else "rotate_sent",
    )(place, *args)


def add(a, b):
    return (a.astype(F32) + b.astype(F32)).astype(BF)


def sum_kernel(keep0, come0, again0, keep1, come1, again1, out_ref):
    for half, (kept, come, again) in enumerate(((keep0, come0, again0), (keep1, come1, again1))):
        out_ref[half] = add(add(kept[1], come[1]), again[...])


def sums(*args):
    return pl.pallas_call(
        sum_kernel,
        out_shape=jax.ShapeDtypeStruct((2, 256, CHEB), BF),
        in_specs=[pl.BlockSpec(memory_space=pltpu.VMEM)] * 6,
        out_specs=pl.BlockSpec(memory_space=pltpu.VMEM),
        compiler_params=params(8),
        name="sums",
    )(*args)


def trig_kernel(place, *refs):
    near1, near2 = refs[0:4], refs[4:8]
    first_ref, second_ref, out_ref, angle = refs[8:]
    step = pl.program_id(0)

    @pl.when(step < 8)
    def _():
        held = jnp.concatenate([r[0] for r in near1], axis=0)
        angle[...] = dot(first_ref[0], held)

    @pl.when(step >= 8)
    def _():
        held = jnp.concatenate([r[...].astype(F32).reshape(64, HALF) for r in near2], axis=0)
        angle[...] = dot(second_ref[0], held.astype(BF))

    for half in range(2):
        for at in range(0, 64, 16):
            sine, cosine = sin_cos(angle[64 * half + at : 64 * half + at + 16])
            out_ref[0, 0, at : at + 16, HALF * half : HALF * half + HALF] = sine
            out_ref[0, 1, at : at + 16, HALF * half : HALF * half + HALF] = cosine


def trig(place, near):
    def own(*shape):
        return pl.BlockSpec((1, *shape), lambda i, p: (p[2],) + (0,) * len(shape))

    spec = pltpu.PrefetchScalarGridSpec(
        num_scalar_prefetch=1,
        grid=(16,),
        in_specs=[pl.BlockSpec((1, 64, HALF), lambda i, p: (jnp.minimum(i, 7), 0, 0))] * 4
        + [pl.BlockSpec((8, 8, HALF), lambda i, p: (0, jnp.maximum(i - 8, 0), 0))] * 4
        + [own(128, 256), own(128, 256)],
        out_specs=pl.BlockSpec((1, 2, 64, CHEB), lambda i, p: (i, 0, 0, 0)),
        scratch_shapes=[pltpu.VMEM((128, HALF), F32)],
    )
    return pl.pallas_call(
        trig_kernel,
        grid_spec=spec,
        out_shape=pltpu.HBM((16, 2, 64, CHEB), F32),
        compiler_params=params(10),
        name="trig",
    )(place, *near, *near, jnp.asarray(FIRST, BF), jnp.asarray(SECOND, BF))


def levels_kernel(x_ref, t_ref, trig_ref, enter_ref, turn_ref, leave_ref, out_ref, left, middle, even, odd):
    step = pl.program_id(0)

    @pl.when(step == 0)
    def _():
        total = (x_ref[0].astype(F32) + x_ref[1].astype(F32)).astype(BF)
        left[...] = dot(enter_ref[...], total).astype(BF)

    @pl.when(step == 2)
    def _():
        left[...] = dot(turn_ref[...], middle[...]).astype(BF)

    def turn_and_sum(product, at):
        total = [jnp.zeros((8, CHEB), F32)] * 4
        for outer in range(8):
            sine = trig_ref[at, 0, 8 * outer : 8 * outer + 8, :]
            cosine = trig_ref[at, 1, 8 * outer : 8 * outer + 8, :]
            for r in range(2):
                row = 32 * outer + 8 * r
                re = product[row : row + 8, :]
                im = product[row + 16 : row + 24, :]
                total[r] = total[r] + (re * cosine - im * sine)
                total[2 + r] = total[2 + r] + (re * sine + im * cosine)
        return jnp.concatenate(total, axis=0).astype(BF)

    def four_orientations(put):
        even[...] = dot(left[...], t_ref[0])
        for t in range(4):
            if t < 3:
                (odd, even)[t % 2][...] = dot(left[...], t_ref[t + 1])
            put(t, turn_and_sum((even, odd)[t % 2], t))

    @pl.when(step < 2)
    def _():
        def put(t, value):
            row = pl.multiple_of(128 * step + 32 * t, 32)
            middle[pl.ds(row, 32), :] = value

        four_orientations(put)

    @pl.when(step >= 2)
    def _():
        def put(t, value):
            value = jnp.concatenate([value[:, :HALF], value[:, HALF:]], axis=0)
            value = dot(leave_ref[...], value)
            for t4 in range(8):
                out_ref[t4, t] = value[8 * t4 : 8 * t4 + 8].astype(BF)

        four_orientations(put)


def levels(share, translation, waves):
    def const(*shape):
        return pl.BlockSpec(shape, lambda i: (0,) * len(shape))

    return pl.pallas_call(
        levels_kernel,
        grid=(4,),
        out_shape=jax.ShapeDtypeStruct((8, 8, 8, HALF), BF),
        in_specs=[
            const(2, 256, CHEB),
            pl.BlockSpec((4, CHEB, CHEB), lambda i: (i % 2, 0, 0)),
            pl.BlockSpec((4, 2, 64, CHEB), lambda i: (i, 0, 0, 0)),
            const(256, 256),
            const(256, 256),
            const(64, 64),
        ],
        out_specs=pl.BlockSpec((8, 4, 8, HALF), lambda i: (0, jnp.maximum(i - 2, 0), 0, 0)),
        scratch_shapes=[
            pltpu.VMEM((256, CHEB), BF),
            pltpu.VMEM((256, CHEB), BF),
            pltpu.VMEM((256, CHEB), F32),
            pltpu.VMEM((256, CHEB), F32),
        ],
        compiler_params=params(20),
        name="levels",
    )(share, in_hbm(translation), in_hbm(waves), jnp.asarray(ENTER, BF), jnp.asarray(TURN, BF), jnp.asarray(LEAVE, BF))


def final_kernel(place, n0, n1, n2, n3, pick_ref, t_ref, out_ref, left):
    for high in range(2):
        held = jnp.concatenate([r[64 * high : 64 * high + 64] for r in (n0, n1, n2, n3)], axis=0)
        value = dot(pick_ref[0], held)
        value = jnp.concatenate([value[:128], value[128:]], axis=1)
        left[128 * high : 128 * high + 128, :] = value.astype(BF)
    for x2 in range(2):
        out_ref[x2, 0] = dot(left[...], t_ref[4 * x2 + place[2]]).astype(BF)


def final(place, near, translation):
    spec = pltpu.PrefetchScalarGridSpec(
        num_scalar_prefetch=1,
        grid=(4,),
        in_specs=[pl.BlockSpec((128, HALF), lambda i, p: (i, 0))] * 4
        + [
            pl.BlockSpec((1, 256, 256), lambda i, p: (p[2], 0, 0)),
            pl.BlockSpec(memory_space=pltpu.VMEM),
        ],
        out_specs=pl.BlockSpec((2, 1, 256, CHEB), lambda i, p: (0, i, 0, 0)),
        scratch_shapes=[pltpu.VMEM((256, CHEB), BF)],
    )
    return pl.pallas_call(
        final_kernel,
        grid_spec=spec,
        out_shape=jax.ShapeDtypeStruct((2, 4, 256, CHEB), BF),
        compiler_params=params(14),
        name="final",
    )(place, *near, jnp.asarray(FINAL, BF), translation)


def swap(value, axis):
    return lax.ppermute(value, axis, [(0, 1), (1, 0)])


def four(value):
    other = swap(value, "y2")
    return value, swap(value, "z2"), other, swap(other, "z2")


def exchange(value, axes):
    return lax.all_to_all(value, axes, split_axis=0, concat_axis=0, tiled=True)


def shards(weights, angles, translation):
    bit = lax.axis_index
    place = jnp.stack([bit("y4"), bit("z4"), 2 * bit("y2") + bit("z2")]).astype(jnp.int32)
    shape = weights.shape
    weights = in_hbm(weights.reshape(2, 4, 256, CHEB))
    angles = in_hbm(angles.reshape(3, 2, 4, 4, 4, CHEB))
    send0, send1 = rotate(place, weights, angles, False)
    come0, come1 = swap(send0, "y4"), swap(send1, "z4")
    keep0, keep1, phases = rotate(place, weights, angles, True)
    phases = exchange(phases.reshape(64, 8, HALF), ("x4", "y4", "z4", "x3", "y3", "z3"))
    again0, again1 = add(keep0[0], come0[0]), add(keep1[0], come1[0])
    phases, _, _ = lax.optimization_barrier((phases, again0, again1))
    near = four(phases.reshape(8, 64, HALF))
    again0, again1 = swap(again0, "z4"), swap(again1, "y4")
    share = sums(keep0, come0, again0, keep1, come1, again1)
    share = exchange(share.reshape(64, 8, CHEB), ("x4", "x3", "y3", "z3", "y2", "z2"))
    waves = trig(place, near)
    done = levels(share.reshape(2, 256, CHEB), translation, waves)
    done = exchange(done.reshape(64, 8, HALF), ("y4", "z4", "x4", "x3", "y3", "z3"))
    near = four(done.reshape(512, HALF))
    return final(place, near, translation).reshape(shape)


def solution(mesh):
    fine = Mesh(mesh.devices.reshape((2,) * len(BITS)), BITS)
    x, y, z = BITS[:2], BITS[2:5], BITS[5:]
    return jax.shard_map(
        shards,
        mesh=fine,
        in_specs=(P(x, y, z, None, None, None), P(None, x, y, z, None), P()),
        out_specs=P(x, y, z, None, None, None),
        check_vma=False,
    )
```

time: 135 us -> 127 us (0.941)
  waiting for transfers between devices: 37.6 us -> 27.3 us
  Pallas kernels: 23.1 us -> 30.7 us
  other arithmetic: 4.61 us -> 0.21 us
  local copies, waits for them, and re-layouts: 4.43 us -> 1.69 us
    all_to_all x2, waiting for transfers between devices: 9.52 us -> 0.01 us  [exchange(): return lax.all_to_all(value, axes, split_axis=0, concat_axis=0, tiled=True)]
    pallas_call x2 -> x5, Pallas kernels: 19.2 us -> 26.8 us  [the longest x2 9.36 us: rotate(): pl.pallas_call(keep_kernel if keep else send_kernel, grid_spec=spec, out_...]
    another operation x3 -> x0, other arithmetic: 3.01 us -> none  [shards(): share = jnp.stack([add(come0, again0), add(come1, again1)])]
    unnamed x22 -> x18, local copies, waits for them, and re-layouts: 4.43 us -> 1.69 us
    all_to_all x2, starting transfers between devices: 18.2 us -> 20.7 us  [exchange(): return lax.all_to_all(value, axes, split_axis=0, concat_axis=0, tiled=True)]
    convert_element_type x2, other arithmetic: 1.53 us -> 0.13 us  [add(): return (a.astype(F32) + b.astype(F32)).astype(BF)]
  transfers between devices with their start and end apart: 12 -> 12, of which waited for: 6 -> 6; matrix products, arithmetic and copies ran while one was open for 3% -> 0% of each run, Pallas kernels for 0% -> 12%
where the time goes in v1:
time: 127 us
  starting transfers between devices  43.8 us (34%)
  Pallas kernels  30.7 us (24%)
  waiting for transfers between devices  27.3 us (21%)
  blocking collectives  22.9 us (18%)
  local copies, waits for them, and re-layouts  1.69 us (1%)
    ppermute x10, waiting for transfers between devices, swap(): return lax.ppermute(value, axis, [(0, 1), (1, 0)])  27.3 us
    ppermute x10, starting transfers between devices, swap(): return lax.ppermute(value, axis, [(0, 1), (1, 0)])  23.1 us
    all_to_all x1, blocking collectives, exchange(): return lax.all_to_all(value, axes, split_axis=0, concat_axis=0, tiled=True)  22.9 us
    all_to_all x2, starting transfers between devices, exchange(): return lax.all_to_all(value, axes, split_axis=0, concat_axis=0, tiled=True)  20.7 us
    pallas_call x2, Pallas kernels, rotate(): pl.pallas_call(keep_kernel if keep else send_kernel, grid_spec=spec, out_...  9.36 us
    pallas_call x1, Pallas kernels, trig(): pl.pallas_call(trig_kernel, grid_spec=spec, out_shape=pltpu.HBM((16, 2, 6...  8.98 us
    pallas_call x1, Pallas kernels, levels(): pl.pallas_call(levels_kernel, grid=(4,), out_shape=jax.ShapeDtypeStruct((...  7.44 us
    pallas_call x1, Pallas kernels, final(): pl.pallas_call(final_kernel, grid_spec=spec, out_shape=jax.ShapeDtypeStru...  3.88 us
  transfers between devices with their start and end apart: 12, of which 6 were waited for; matrix products, arithmetic and copies ran while one was open for 0% of the time, Pallas kernels for 12%

profile of v1, /device:TPU:1, one launch (start us, length us, event | category | flops | bytes accessed | tf_op | source)
XLA Modules:
  0.0 126.7 jit_solution(15123663056117466839)
XLA Ops:
  0.0 0.1 pad_add_fusion.place
  0.1 0.9 copy-done.2
  1.0 4.5 %rotate_sent.1 = (bf16[2,256,512]{2,1,0:T(8,128)(2,1)S(1)}, bf16[2,256,512]{2,1,0:T(8,128)(2,1)}) custom-call(s32[3]{0:T(128)S(1)} %pad_add_fusion.place, bf16[2,4,256,512]{3,2,1,0:T(8,128)(2,1)} %bitcast.29, f32[3,2,4,4,4,512]{5,4,3,2,1,0:T(4,128)} %bitcast.25, bf16[256,256]{1,0:T(8,128)(2,1)S(1)} %copy-done.2), custom_call_target="tpu_custom_call" | custom-call | tf_op jit(solution)/shard_map/rotate_sent/pallas_call | solution.py:160
  5.4 3.7 %collective-permute-start.2 = (bf16[2,256,512]{2,1,0:T(8,128)(2,1)}, bf16[2,256,512]{2,1,0:T(8,128)(2,1)S(1)}, u32[]{:S(2)}, u32[]{:S(2)}) collective-permute-start(bf16[2,256,512]{2,1,0:T(8,128)(2,1)} %get-tuple-element.14), channel_id=1, source_target_pairs={{0,4},{4,0},{1,5},{5,1},{2,6},{6,2},{3,7},{7,3},{8,12},{12,8},{9,1... | collective-permute-start | bytes 1572872 | tf_op jit(solution)/shard_map/ppermute | solution.py:344
  9.2 2.7 %collective-permute-start = (bf16[2,256,512]{2,1,0:T(8,128)(2,1)S(1)}, bf16[2,256,512]{2,1,0:T(8,128)(2,1)S(1)}, u32[]{:S(2)}, u32[]{:S(2)}) collective-permute-start(bf16[2,256,512]{2,1,0:T(8,128)(2,1)S(1)} %get-tuple-element.12), channel_id=1, source_target_pairs={{0,32},{32,0},{1,33},{33,1},{2,34},{34,2},{3,35},{35,3},{4,36},{36... | collective-permute-start | bytes 1572872 | tf_op jit(solution)/shard_map/ppermute | solution.py:344
  11.9 0.8 copy-done.7
  12.7 4.9 %rotate_kept.1 = (bf16[2,256,512]{2,1,0:T(8,128)(2,1)S(1)}, bf16[2,256,512]{2,1,0:T(8,128)(2,1)S(1)}, bf16[2,4,64,256]{3,2,1,0:T(8,128)(2,1)}) custom-call(s32[3]{0:T(128)S(1)} %pad_add_fusion.place, bf16[2,4,256,512]{3,2,1,0:T(8,128)(2,1)} %bitcast.30, f32[3,2,4,4,4,512]{5,4,3,2,1,0:T(4,128)} %bitcast.26, bf16[256,256]{1,0:T(8,128)(2,1)S(1)} %copy-done.2, ...), custom_call_target="tpu_custom_call" | custom-call | tf_op jit(solution)/shard_map/rotate_kept/pallas_call | solution.py:160
  17.6 10.4 %all-to-all-start.1 = ((bf16[64,8,256]{2,1,0:T(8,128)(2,1)}), bf16[64,8,256]{2,1,0:T(8,128)(2,1)S(1)}, u32[]{:S(2)}, u32[]{:S(2)}) async-start(bf16[64,8,256]{2,1,0:T(8,128)(2,1)} %bitcast.9), calls=%async_computation.1 | async-start | bytes 524288 | tf_op jit(solution)/shard_map/all_to_all | solution.py:353
  28.0 0.1 fusion.1
  28.1 2.6 %collective-permute-start.3 = (bf16[256,512]{1,0:T(8,128)(2,1)S(1)}, bf16[256,512]{1,0:T(8,128)(2,1)S(1)}, u32[]{:S(2)}, u32[]{:S(2)}) collective-permute-start(bf16[256,512]{1,0:T(8,128)(2,1)S(1)} %fusion.1), channel_id=1, source_target_pairs={{0,32},{32,0},{1,33},{33,1},{2,34},{34,2},{3,35},{35,3},{4,36},{36... | collective-permute-start | bytes 786440 | tf_op jit(solution)/shard_map/ppermute | solution.py:344
  30.7 0.1 fusion
  30.8 2.8 %collective-permute-start.1 = (bf16[256,512]{1,0:T(8,128)(2,1)S(1)}, bf16[256,512]{1,0:T(8,128)(2,1)S(1)}, u32[]{:S(2)}, u32[]{:S(2)}) collective-permute-start(bf16[256,512]{1,0:T(8,128)(2,1)S(1)} %fusion), channel_id=1, source_target_pairs={{0,4},{4,0},{1,5},{5,1},{2,6},{6,2},{3,7},{7,3},{8,12},{12,8},{9,1... | collective-permute-start | bytes 786440 | tf_op jit(solution)/shard_map/ppermute | solution.py:344
  33.6 4.9 %collective-permute-done.3.again1 = bf16[256,512]{1,0:T(8,128)(2,1)S(1)} collective-permute-done((bf16[256,512]{1,0:T(8,128)(2,1)S(1)}, bf16[256,512]{1,0:T(8,128)(2,1)S(1)}, u32[]{:S(2)}, u32[]{:S(2)}) %collective-permute-start.3) | collective-permute-done | bytes 262176 | tf_op jit(solution)/shard_map/ppermute | solution.py:344
  38.5 2.0 %collective-permute-done.1.again0 = bf16[256,512]{1,0:T(8,128)(2,1)S(1)} collective-permute-done((bf16[256,512]{1,0:T(8,128)(2,1)S(1)}, bf16[256,512]{1,0:T(8,128)(2,1)S(1)}, u32[]{:S(2)}, u32[]{:S(2)}) %collective-permute-start.1) | collective-permute-done | bytes 262176 | tf_op jit(solution)/shard_map/ppermute | solution.py:344
  40.4 1.0 sums.1
  41.5 10.3 %all-to-all-start = ((bf16[64,8,512]{2,1,0:T(8,128)(2,1)}), bf16[64,8,512]{2,1,0:T(8,128)(2,1)S(1)}, u32[]{:S(2)}, u32[]{:S(2)}) async-start(bf16[64,8,512]{2,1,0:T(8,128)(2,1)} %bitcast.7), calls=%async_computation | async-start | bytes 1048576 | tf_op jit(solution)/shard_map/all_to_all | solution.py:353
  51.8 1.5 %collective-permute-start.5 = (bf16[8,64,256]{2,1,0:T(8,128)(2,1)S(1)}, bf16[8,64,256]{2,1,0:T(8,128)(2,1)S(1)}, u32[]{:S(2)}, u32[]{:S(2)}) collective-permute-start(bf16[8,64,256]{2,1,0:T(8,128)(2,1)S(1)} %bitcast.16), channel_id=1, source_target_pairs={{0,8},{8,0},{1,9},{9,1},{2,10},{10,2},{3,11},{11,3},{4,12},{12,4},... | collective-permute-start | bytes 786440 | tf_op jit(solution)/shard_map/ppermute | solution.py:344
  53.3 0.6 collective-permute-start.4
  53.9 16.7 %collective-permute-done.5.refs_2_.refs_6_ = bf16[8,64,256]{2,1,0:T(8,128)(2,1)S(1)} collective-permute-done((bf16[8,64,256]{2,1,0:T(8,128)(2,1)S(1)}, bf16[8,64,256]{2,1,0:T(8,128)(2,1)S(1)}, u32[]{:S(2)}, u32[]{:S(2)}) %collective-permute-start.5) | collective-permute-done | bytes 262176 | tf_op jit(solution)/shard_map/ppermute | solution.py:344
  70.6 0.9 collective-permute-start.6
  71.5 1.2 collective-permute-done.6.refs_3_.refs_7_
  72.7 9.0 %trig.1.trig_ref = f32[16,2,64,512]{3,2,1,0:T(8,128)} custom-call(s32[3]{0:T(128)S(1)} %pad_add_fusion.place, bf16[8,64,256]{2,1,0:T(8,128)(2,1)S(1)} %bitcast.18, bf16[8,64,256]{2,1,0:T(8,128)(2,1)S(1)} %collective-permute-done.4.refs_1_.refs_5_, bf16[8,64,256]{2,1,0:T(8,128)(2,1)S(1)} %collective-permute-done.5.refs_2_.refs_6_, ...), custom_call_target="tpu_custom_call" | custom-call | tf_op jit(solution)/shard_map/trig/pallas_call | solution.py:224
  81.7 0.0 copy-start
  81.7 0.0 copy-start.1
  81.7 7.4 %levels.1 = bf16[8,8,8,256]{3,2,1,0:T(8,128)(2,1)S(1)} custom-call(bf16[2,256,512]{2,1,0:T(8,128)(2,1)S(1)} %bitcast.20, bf16[8,512,512]{2,1,0:T(8,128)(2,1)} %t_ref.3, f32[16,2,64,512]{3,2,1,0:T(8,128)} %trig.1.trig_ref, bf16[256,256]{1,0:T(8,128)(2,1)S(1)} %copy-done.6, bf16[256,256]{1,0:T(8,128)(2,1)S(1)} %copy-done.5, bf16[64,64]{1,0:T(8,128)(2,1)S(1)} %copy-done.8), custom_call_target="tpu_custom_call" | custom-call | tf_op jit(solution)/shard_map/levels/pallas_call | solution.py:288
  89.2 22.9 %all_to_all.15 = bf16[64,8,256]{2,1,0:T(8,128)(2,1)S(1)} all-to-all(bf16[64,8,256]{2,1,0:T(8,128)(2,1)S(1)} %bitcast.24), channel_id=1, replica_groups=mesh['x4'=2,'x3'=2,'y4'=2,'y3'=2,'y2'=2,'z4'=2,'z3'=2,'z2'=2] {'y4','z4'..., dimensions={0} | all-to-all | bytes 524288 | tf_op jit(solution)/shard_map/all_to_all | solution.py:353
  112.1 1.8 %collective-permute-start.8 = (bf16[512,256]{1,0:T(8,128)(2,1)S(1)}, bf16[512,256]{1,0:T(8,128)(2,1)S(1)}, u32[]{:S(2)}, u32[]{:S(2)}) collective-permute-start(bf16[512,256]{1,0:T(8,128)(2,1)S(1)} %bitcast.21), channel_id=1, source_target_pairs={{0,8},{8,0},{1,9},{9,1},{2,10},{10,2},{3,11},{11,3},{4,12},{12,4},... | collective-permute-start | bytes 786440 | tf_op jit(solution)/shard_map/ppermute | solution.py:344
  113.8 2.4 %collective-permute-start.7 = (bf16[512,256]{1,0:T(8,128)(2,1)S(1)}, bf16[512,256]{1,0:T(8,128)(2,1)S(1)}, u32[]{:S(2)}, u32[]{:S(2)}) collective-permute-start(bf16[512,256]{1,0:T(8,128)(2,1)S(1)} %bitcast.22), channel_id=1, source_target_pairs={{0,1},{1,0},{2,3},{3,2},{4,5},{5,4},{6,7},{7,6},{8,9},{9,8},{10,11... | collective-permute-start | bytes 786440 | tf_op jit(solution)/shard_map/ppermute | solution.py:344
  116.2 1.4 %collective-permute-done.8.n2 = bf16[512,256]{1,0:T(8,128)(2,1)S(1)} collective-permute-done((bf16[512,256]{1,0:T(8,128)(2,1)S(1)}, bf16[512,256]{1,0:T(8,128)(2,1)S(1)}, u32[]{:S(2)}, u32[]{:S(2)}) %collective-permute-start.8) | collective-permute-done | bytes 262176 | tf_op jit(solution)/shard_map/ppermute | solution.py:344
  117.6 4.1 %collective-permute-start.9 = (bf16[512,256]{1,0:T(8,128)(2,1)S(1)}, bf16[512,256]{1,0:T(8,128)(2,1)S(1)}, u32[]{:S(2)}, u32[]{:S(2)}) collective-permute-start(bf16[512,256]{1,0:T(8,128)(2,1)S(1)} %collective-permute-done.8.n2), channel_id=1, source_target_pairs={{0,1},{1,0},{2,3},{3,2},{4,5},{5,4},{6,7},{7,6},{8,9},{9,8},{10,11... | collective-permute-start | bytes 786440 | tf_op jit(solution)/shard_map/ppermute | solution.py:344
  121.7 1.2 collective-permute-done.9.n3
  122.8 3.9 %final.1 = bf16[2,4,256,512]{3,2,1,0:T(8,128)(2,1)} custom-call(s32[3]{0:T(128)S(1)} %pad_add_fusion.place, bf16[512,256]{1,0:T(8,128)(2,1)S(1)} %bitcast.23, bf16[512,256]{1,0:T(8,128)(2,1)S(1)} %collective-permute-done.7.n1, bf16[512,256]{1,0:T(8,128)(2,1)S(1)} %collective-permute-done.8.n2, bf16[512,256]{1,0:T(8,128)(2,1)S(1)} %collective-permute-done.9.n3, ...), custom_call_target="tpu_custom_call" | custom-call | tf_op jit(solution)/shard_map/final/pallas_call | solution.py:334
  (20 shorter events, 0.0 us)
Async XLA Ops:
  0.1 0.9 copy-start.2
  5.4 22.6 %collective-permute-start.2 = (bf16[2,256,512]{2,1,0:T(8,128)(2,1)}, bf16[2,256,512]{2,1,0:T(8,128)(2,1)S(1)}, u32[]{:S(2)}, u32[]{:S(2)}) collective-permute-start(bf16[2,256,512]{2,1,0:T(8,128)(2,1)} %get-tuple-element.14), channel_id=1, source_target_pairs={{0,4},{4,0},{1,5},{5,1},{2,6},{6,2},{3,7},{7,3},{8,12},{12,8},{9,1... | collective-permute-start | bytes 1572872 | tf_op jit(solution)/shard_map/ppermute | solution.py:344
  9.2 21.5 %collective-permute-start = (bf16[2,256,512]{2,1,0:T(8,128)(2,1)S(1)}, bf16[2,256,512]{2,1,0:T(8,128)(2,1)S(1)}, u32[]{:S(2)}, u32[]{:S(2)}) collective-permute-start(bf16[2,256,512]{2,1,0:T(8,128)(2,1)S(1)} %get-tuple-element.12), channel_id=1, source_target_pairs={{0,32},{32,0},{1,33},{33,1},{2,34},{34,2},{3,35},{35,3},{4,36},{36... | collective-permute-start | bytes 1572872 | tf_op jit(solution)/shard_map/ppermute | solution.py:344
  11.9 0.8 copy-start.7
  17.6 55.1 %copy-start.3 = (bf16[4,128,256]{2,1,0:T(8,128)(2,1)S(1)}, bf16[4,128,256]{2,1,0:T(8,128)(2,1)}, u32[]{:S(2)}) copy-start(bf16[4,128,256]{2,1,0:T(8,128)(2,1)} %constant.37.clone.refs_9_) | copy-start | bytes 786436
  17.6 55.1 %copy-start.4 = (bf16[4,128,256]{2,1,0:T(8,128)(2,1)S(1)}, bf16[4,128,256]{2,1,0:T(8,128)(2,1)}, u32[]{:S(2)}) copy-start(bf16[4,128,256]{2,1,0:T(8,128)(2,1)} %constant.36.clone.refs_8_) | copy-start | bytes 786436
  17.6 23.9 %all-to-all-start.1 = ((bf16[64,8,256]{2,1,0:T(8,128)(2,1)}), bf16[64,8,256]{2,1,0:T(8,128)(2,1)S(1)}, u32[]{:S(2)}, u32[]{:S(2)}) async-start(bf16[64,8,256]{2,1,0:T(8,128)(2,1)} %bitcast.9), calls=%async_computation.1 | async-start | bytes 524288 | tf_op jit(solution)/shard_map/all_to_all | solution.py:353
  28.1 10.4 %collective-permute-start.3 = (bf16[256,512]{1,0:T(8,128)(2,1)S(1)}, bf16[256,512]{1,0:T(8,128)(2,1)S(1)}, u32[]{:S(2)}, u32[]{:S(2)}) collective-permute-start(bf16[256,512]{1,0:T(8,128)(2,1)S(1)} %fusion.1), channel_id=1, source_target_pairs={{0,32},{32,0},{1,33},{33,1},{2,34},{34,2},{3,35},{35,3},{4,36},{36... | collective-permute-start | bytes 786440 | tf_op jit(solution)/shard_map/ppermute | solution.py:344
  30.8 9.7 %collective-permute-start.1 = (bf16[256,512]{1,0:T(8,128)(2,1)S(1)}, bf16[256,512]{1,0:T(8,128)(2,1)S(1)}, u32[]{:S(2)}, u32[]{:S(2)}) collective-permute-start(bf16[256,512]{1,0:T(8,128)(2,1)S(1)} %fusion), channel_id=1, source_target_pairs={{0,4},{4,0},{1,5},{5,1},{2,6},{6,2},{3,7},{7,3},{8,12},{12,8},{9,1... | collective-permute-start | bytes 786440 | tf_op jit(solution)/shard_map/ppermute | solution.py:344
  41.5 40.2 %copy-start.5 = (bf16[256,256]{1,0:T(8,128)(2,1)S(1)}, bf16[256,256]{1,0:T(8,128)(2,1)}, u32[]{:S(2)}) copy-start(bf16[256,256]{1,0:T(8,128)(2,1)} %constant.39.clone.turn_ref) | copy-start | bytes 393220
  41.5 40.2 %copy-start.6 = (bf16[256,256]{1,0:T(8,128)(2,1)S(1)}, bf16[256,256]{1,0:T(8,128)(2,1)}, u32[]{:S(2)}) copy-start(bf16[256,256]{1,0:T(8,128)(2,1)} %constant.38.clone.enter_ref) | copy-start | bytes 393220
  41.5 40.2 %copy-start.8 = (bf16[64,64]{1,0:T(8,128)(2,1)S(1)}, bf16[64,64]{1,0:T(8,128)(2,1)}, u32[]{:S(2)}) copy-start(bf16[64,64]{1,0:T(8,128)(2,1)} %constant.40.clone.leave_ref) | copy-start | bytes 24580
  41.5 40.2 %all-to-all-start = ((bf16[64,8,512]{2,1,0:T(8,128)(2,1)}), bf16[64,8,512]{2,1,0:T(8,128)(2,1)S(1)}, u32[]{:S(2)}, u32[]{:S(2)}) async-start(bf16[64,8,512]{2,1,0:T(8,128)(2,1)} %bitcast.7), calls=%async_computation | async-start | bytes 1048576 | tf_op jit(solution)/shard_map/all_to_all | solution.py:353
  51.8 18.8 %collective-permute-start.5 = (bf16[8,64,256]{2,1,0:T(8,128)(2,1)S(1)}, bf16[8,64,256]{2,1,0:T(8,128)(2,1)S(1)}, u32[]{:S(2)}, u32[]{:S(2)}) collective-permute-start(bf16[8,64,256]{2,1,0:T(8,128)(2,1)S(1)} %bitcast.16), channel_id=1, source_target_pairs={{0,8},{8,0},{1,9},{9,1},{2,10},{10,2},{3,11},{11,3},{4,12},{12,4},... | collective-permute-start | bytes 786440 | tf_op jit(solution)/shard_map/ppermute | solution.py:344
  53.3 18.3 %collective-permute-start.4 = (bf16[8,64,256]{2,1,0:T(8,128)(2,1)S(1)}, bf16[8,64,256]{2,1,0:T(8,128)(2,1)S(1)}, u32[]{:S(2)}, u32[]{:S(2)}) collective-permute-start(bf16[8,64,256]{2,1,0:T(8,128)(2,1)S(1)} %bitcast.17), channel_id=1, source_target_pairs={{0,1},{1,0},{2,3},{3,2},{4,5},{5,4},{6,7},{7,6},{8,9},{9,8},{10,11... | collective-permute-start | bytes 786440 | tf_op jit(solution)/shard_map/ppermute | solution.py:344
  70.6 2.0 %collective-permute-start.6 = (bf16[8,64,256]{2,1,0:T(8,128)(2,1)S(1)}, bf16[8,64,256]{2,1,0:T(8,128)(2,1)S(1)}, u32[]{:S(2)}, u32[]{:S(2)}) collective-permute-start(bf16[8,64,256]{2,1,0:T(8,128)(2,1)S(1)} %collective-permute-done.5.refs_2_.refs_6_), channel_id=1, source_target_pairs={{0,1},{1,0},{2,3},{3,2},{4,5},{5,4},{6,7},{7,6},{8,9},{9,8},{10,11... | collective-permute-start | bytes 786440 | tf_op jit(solution)/shard_map/ppermute | solution.py:344
  81.7 41.1 %copy-start = (bf16[8,512,512]{2,1,0:T(8,128)(2,1)S(1)}, bf16[8,512,512]{2,1,0:T(8,128)(2,1)}, u32[]{:S(2)}) copy-start(bf16[8,512,512]{2,1,0:T(8,128)(2,1)} %t_ref.3) | copy-start | bytes 12582916
  81.7 41.1 %copy-start.1 = (bf16[4,256,256]{2,1,0:T(8,128)(2,1)S(1)}, bf16[4,256,256]{2,1,0:T(8,128)(2,1)}, u32[]{:S(2)}) copy-start(bf16[4,256,256]{2,1,0:T(8,128)(2,1)} %constant.41.clone.pick_ref) | copy-start | bytes 1572868
  112.1 5.5 %collective-permute-start.8 = (bf16[512,256]{1,0:T(8,128)(2,1)S(1)}, bf16[512,256]{1,0:T(8,128)(2,1)S(1)}, u32[]{:S(2)}, u32[]{:S(2)}) collective-permute-start(bf16[512,256]{1,0:T(8,128)(2,1)S(1)} %bitcast.21), channel_id=1, source_target_pairs={{0,8},{8,0},{1,9},{9,1},{2,10},{10,2},{3,11},{11,3},{4,12},{12,4},... | collective-permute-start | bytes 786440 | tf_op jit(solution)/shard_map/ppermute | solution.py:344
  113.8 7.8 %collective-permute-start.7 = (bf16[512,256]{1,0:T(8,128)(2,1)S(1)}, bf16[512,256]{1,0:T(8,128)(2,1)S(1)}, u32[]{:S(2)}, u32[]{:S(2)}) collective-permute-start(bf16[512,256]{1,0:T(8,128)(2,1)S(1)} %bitcast.22), channel_id=1, source_target_pairs={{0,1},{1,0},{2,3},{3,2},{4,5},{5,4},{6,7},{7,6},{8,9},{9,8},{10,11... | collective-permute-start | bytes 786440 | tf_op jit(solution)/shard_map/ppermute | solution.py:344
  117.6 5.2 %collective-permute-start.9 = (bf16[512,256]{1,0:T(8,128)(2,1)S(1)}, bf16[512,256]{1,0:T(8,128)(2,1)S(1)}, u32[]{:S(2)}, u32[]{:S(2)}) collective-permute-start(bf16[512,256]{1,0:T(8,128)(2,1)S(1)} %collective-permute-done.8.n2), channel_id=1, source_target_pairs={{0,1},{1,0},{2,3},{3,2},{4,5},{5,4},{6,7},{7,6},{8,9},{9,8},{10,11... | collective-permute-start | bytes 786440 | tf_op jit(solution)/shard_map/ppermute | solution.py:344

commit v2 on v1

--- a/solution.py
+++ b/solution.py
@@ -81,89 +81,84 @@
     return pltpu.CompilerParams(vmem_limit_bytes=mebibytes * 1024 * 1024)
 
 
-def rotate_half(w_ref, a_ref, mix_ref, first, second, angle, mixed):
-    step = pl.program_id(0)
-    for x2 in range(2):
-        for y in range(2):
-            angle[x2, 4 * y : 4 * y + 4, :] = a_ref[0, x2, 0, y]
-        sine, cosine = sin_cos(angle[x2])
-        for low in range(8):
-            block = w_ref[x2, 0, 16 * low : 16 * low + 16, :].astype(F32)
-            re, im = block[:8], block[8:]
-            s, c = sine[low : low + 1], cosine[low : low + 1]
-            turned = jnp.concatenate([re * c - im * s, re * s + im * c], axis=0)
-            at = 128 * x2 + 16 * low
-            mixed[at : at + 16, :] = turned.astype(BF)
-    value = dot(mix_ref[...], mixed[...]).astype(BF)
-
-    @pl.when(step < 2)
-    def _():
-        first[0] = value
-
-    @pl.when(step >= 2)
-    def _():
-        second[0] = value
-
-
-def send_kernel(place, w_ref, a_ref, mix_ref, first, second, angle, mixed):
-    rotate_half(w_ref, a_ref, mix_ref, first, second, angle, mixed)
-
-
-def keep_kernel(place, w_ref, a_ref, mix_ref, a1_ref, a2_ref, order_ref, first, second, phases, angle, mixed, far):
-    rotate_half(w_ref, a_ref, mix_ref, first, second, angle, mixed)
-    for level, ref in enumerate((a1_ref, a2_ref)):
+def rotate_kernel(place, *refs):
+    blocks, angles = refs[0:4], refs[4:8]
+    mix_ref, first, second, angle, mixed = refs[8:]
+    for j in range(4):
         for x2 in range(2):
-            for y in range(4):
-                at = 32 * level + 16 * x2 + 4 * y
-                far[at : at + 4, :] = ref[0, x2, 0, y]
-    value = far[...].astype(BF)
-    value = jnp.concatenate([value[:, :HALF], value[:, HALF:]], axis=0)
-    value = dot(order_ref[...], value).astype(BF)
-    for high in range(2):
-        phases[high, 0] = value[64 * high : 64 * high + 64]
+            for y in range(2):
+                angle[j, x2, 4 * y : 4 * y + 4, :] = angles[j][0, x2, 0, y]
+            sine, cosine = sin_cos(angle[j, x2])
+            for low in range(8):
+                block = blocks[j][x2, 0, 16 * low : 16 * low + 16, :].astype(F32)
+                re, im = block[:8], block[8:]
+                s, c = sine[low : low + 1], cosine[low : low + 1]
+                turned = jnp.concatenate([re * c - im * s, re * s + im * c], axis=0)
+                at = 128 * x2 + 16 * low
+                mixed[j, at : at + 16, :] = turned.astype(BF)
+        (first, second)[j // 2][j % 2] = dot(mix_ref[...], mixed[j]).astype(BF)
 
 
 def rotate(place, weights, angles, keep):
-    def block(j, place):
-        if keep:
-            y, z = jnp.where(j == 2, 0, 1), jnp.where(j == 0, 0, 1)
-        else:
-            y, z = jnp.where(j == 3, 1, 0), jnp.where(j == 1, 1, 0)
-        return (place[0] ^ (1 - y)) * 2 + (place[1] ^ (1 - z))
-
-    piece = jax.ShapeDtypeStruct((2, 256, CHEB), BF)
-    in_specs = [
-        pl.BlockSpec((2, 1, 128, CHEB), lambda j, p: (0, block(j, p), j // 2, 0)),
-        pl.BlockSpec((1, 2, 1, 2, 4, CHEB), lambda j, p: (0, 0, block(j, p), j // 2, 0, 0)),
-        pl.BlockSpec((256, 256), lambda j, p: (0, 0)),
-    ]
-    out_specs = [
-        pl.BlockSpec((1, 256, CHEB), lambda j, p: (jnp.minimum(j, 1), 0, 0)),
-        pl.BlockSpec((1, 256, CHEB), lambda j, p: (jnp.maximum(j - 2, 0), 0, 0)),
-    ]
-    out_shape = [piece] * 2
-    scratch = [pltpu.VMEM((2, 8, CHEB), F32), pltpu.VMEM((256, CHEB), BF)]
-    args = [weights, angles, jnp.asarray(MIX, BF)]
-    if keep:
-        in_specs += [
-            pl.BlockSpec((1, 2, 1, 4, 4, CHEB), lambda j, p: (1, 0, j, 0, 0, 0)),
-            pl.BlockSpec((1, 2, 1, 4, 4, CHEB), lambda j, p: (2, 0, j, 0, 0, 0)),
-            pl.BlockSpec((128, 128), lambda j, p: (0, 0)),
-        ]
-        out_specs.append(pl.BlockSpec((2, 1, 64, HALF), lambda j, p: (0, j, 0, 0)))
-        out_shape.append(jax.ShapeDtypeStruct((2, 4, 64, HALF), BF))
-        scratch.append(pltpu.VMEM((64, CHEB), F32))
-        args += [angles, angles, jnp.asarray(SEND_PHASE, BF)]
+    def block(j):
+        y, z = ((1, 0), (1, 1), (0, 1), (1, 1))[j] if keep else ((0, 0), (0, 1), (0, 0), (1, 0))[j]
+        return lambda p: (p[0] ^ (1 - y)) * 2 + (p[1] ^ (1 - z))
+
+    def weight(j):
+        at = block(j)
+        return pl.BlockSpec((2, 1, 128, CHEB), lambda i, p: (0, at(p), j // 2, 0))
+
+    def phase(j):
+        at = block(j)
+        return pl.BlockSpec((1, 2, 1, 2, 4, CHEB), lambda i, p: (0, 0, at(p), j // 2, 0, 0))
+
     spec = pltpu.PrefetchScalarGridSpec(
-        num_scalar_prefetch=1, grid=(4,), in_specs=in_specs, out_specs=out_specs, scratch_shapes=scratch
-    )
-    return pl.pallas_call(
-        keep_kernel if keep else send_kernel,
+        num_scalar_prefetch=1,
+        grid=(1,),
+        in_specs=[weight(j) for j in range(4)]
+        + [phase(j) for j in range(4)]
+        + [pl.BlockSpec((256, 256), lambda i, p: (0, 0))],
+        out_specs=[pl.BlockSpec((2, 256, CHEB), lambda i, p: (0, 0, 0))] * 2,
+        scratch_shapes=[pltpu.VMEM((4, 2, 8, CHEB), F32), pltpu.VMEM((4, 256, CHEB), BF)],
+    )
+    return pl.pallas_call(
+        rotate_kernel,
         grid_spec=spec,
-        out_shape=out_shape,
+        out_shape=[jax.ShapeDtypeStruct((2, 256, CHEB), BF)] * 2,
         compiler_params=params(12),
         name="rotate_kept" if keep else "rotate_sent",
-    )(place, *args)
+    )(place, *[weights] * 4, *[angles] * 4, in_hbm(jnp.asarray(MIX, BF)))
+
+
+def phase_kernel(a1_ref, a2_ref, order_ref, phases, far):
+    for block in range(4):
+        for level, ref in enumerate((a1_ref, a2_ref)):
+            for x2 in range(2):
+                for y in range(4):
+                    at = 32 * level + 16 * x2 + 4 * y
+                    far[block, at : at + 4, :] = ref[0, x2, block, y]
+        value = far[block].astype(BF)
+        value = jnp.concatenate([value[:, :HALF], value[:, HALF:]], axis=0)
+        value = dot(order_ref[...], value).astype(BF)
+        for high in range(2):
+            phases[high, block] = value[64 * high : 64 * high + 64]
+
+
+def far_phases(angles):
+    return pl.pallas_call(
+        phase_kernel,
+        grid=(1,),
+        in_specs=[
+            pl.BlockSpec((1, 2, 4, 4, 4, CHEB), lambda i: (1, 0, 0, 0, 0, 0)),
+            pl.BlockSpec((1, 2, 4, 4, 4, CHEB), lambda i: (2, 0, 0, 0, 0, 0)),
+            pl.BlockSpec((128, 128), lambda i: (0, 0)),
+        ],
+        out_specs=pl.BlockSpec((2, 4, 64, HALF), lambda i: (0, 0, 0, 0)),
+        out_shape=jax.ShapeDtypeStruct((2, 4, 64, HALF), BF),
+        scratch_shapes=[pltpu.VMEM((4, 64, CHEB), F32)],
+        compiler_params=params(8),
+        name="far_phases",
+    )(angles, angles, in_hbm(jnp.asarray(SEND_PHASE, BF)))
 
 
 def add(a, b):
@@ -188,24 +183,27 @@
 
 def trig_kernel(place, *refs):
     near1, near2 = refs[0:4], refs[4:8]
-    first_ref, second_ref, out_ref, angle = refs[8:]
+    first_ref, second_ref, out_ref = refs[8:]
     step = pl.program_id(0)
 
-    @pl.when(step < 8)
-    def _():
-        held = jnp.concatenate([r[0] for r in near1], axis=0)
-        angle[...] = dot(first_ref[0], held)
-
-    @pl.when(step >= 8)
-    def _():
-        held = jnp.concatenate([r[...].astype(F32).reshape(64, HALF) for r in near2], axis=0)
-        angle[...] = dot(second_ref[0], held.astype(BF))
-
-    for half in range(2):
-        for at in range(0, 64, 16):
-            sine, cosine = sin_cos(angle[64 * half + at : 64 * half + at + 16])
-            out_ref[0, 0, at : at + 16, HALF * half : HALF * half + HALF] = sine
-            out_ref[0, 1, at : at + 16, HALF * half : HALF * half + HALF] = cosine
+    def write(t, angle):
+        for half in range(2):
+            for at in range(0, 64, 8):
+                sine, cosine = sin_cos(angle[64 * half + at : 64 * half + at + 8])
+                out_ref[t, 0, at : at + 8, HALF * half : HALF * half + HALF] = sine
+                out_ref[t, 1, at : at + 8, HALF * half : HALF * half + HALF] = cosine
+
+    @pl.when(step < 2)
+    def _():
+        for t in range(4):
+            held = jnp.concatenate([r[t] for r in near1], axis=0)
+            write(t, dot(first_ref[0], held))
+
+    @pl.when(step >= 2)
+    def _():
+        for t in range(4):
+            held = [r[:, 8 * t : 8 * t + 8, :].astype(F32).reshape(64, HALF) for r in near2]
+            write(t, dot(second_ref[0], jnp.concatenate(held, axis=0).astype(BF)))
 
 
 def trig(place, near):
@@ -214,18 +212,17 @@
 
     spec = pltpu.PrefetchScalarGridSpec(
         num_scalar_prefetch=1,
-        grid=(16,),
-        in_specs=[pl.BlockSpec((1, 64, HALF), lambda i, p: (jnp.minimum(i, 7), 0, 0))] * 4
-        + [pl.BlockSpec((8, 8, HALF), lambda i, p: (0, jnp.maximum(i - 8, 0), 0))] * 4
+        grid=(4,),
+        in_specs=[pl.BlockSpec((4, 64, HALF), lambda i, p: (jnp.minimum(i, 1), 0, 0))] * 4
+        + [pl.BlockSpec((8, 32, HALF), lambda i, p: (0, jnp.maximum(i - 2, 0), 0))] * 4
         + [own(128, 256), own(128, 256)],
-        out_specs=pl.BlockSpec((1, 2, 64, CHEB), lambda i, p: (i, 0, 0, 0)),
-        scratch_shapes=[pltpu.VMEM((128, HALF), F32)],
+        out_specs=pl.BlockSpec((4, 2, 64, CHEB), lambda i, p: (i, 0, 0, 0)),
     )
     return pl.pallas_call(
         trig_kernel,
         grid_spec=spec,
         out_shape=pltpu.HBM((16, 2, 64, CHEB), F32),
-        compiler_params=params(10),
+        compiler_params=params(12),
         name="trig",
     )(place, *near, *near, jnp.asarray(FIRST, BF), jnp.asarray(SECOND, BF))
 
@@ -361,13 +358,14 @@
     angles = in_hbm(angles.reshape(3, 2, 4, 4, 4, CHEB))
     send0, send1 = rotate(place, weights, angles, False)
     come0, come1 = swap(send0, "y4"), swap(send1, "z4")
-    keep0, keep1, phases = rotate(place, weights, angles, True)
-    phases = exchange(phases.reshape(64, 8, HALF), ("x4", "y4", "z4", "x3", "y3", "z3"))
+    keep0, keep1 = rotate(place, weights, angles, True)
+    phases = exchange(far_phases(angles).reshape(64, 8, HALF), ("x4", "y4", "z4", "x3", "y3", "z3"))
     again0, again1 = add(keep0[0], come0[0]), add(keep1[0], come1[0])
     phases, _, _ = lax.optimization_barrier((phases, again0, again1))
     near = four(phases.reshape(8, 64, HALF))
     again0, again1 = swap(again0, "z4"), swap(again1, "y4")
     share = sums(keep0, come0, again0, keep1, come1, again1)
+    share, near = lax.optimization_barrier((share, near))
     share = exchange(share.reshape(64, 8, CHEB), ("x4", "x3", "y3", "z3", "y2", "z2"))
     waves = trig(place, near)
     done = levels(share.reshape(2, 256, CHEB), translation, waves)

time: 127 us -> 114 us (0.90)
  Pallas kernels: 30.7 us -> 24.9 us
  starting transfers between devices: 43.8 us -> 39.9 us
  waiting for transfers between devices: 27.3 us -> 24.3 us
  blocking collectives: 22.9 us -> 21.3 us
  other arithmetic: 0.21 us -> 1.61 us
    ppermute x10, waiting for transfers between devices: 27.3 us -> 3.79 us  [swap(): return lax.ppermute(value, axis, [(0, 1), (1, 0)])]
    all_to_all x2, waiting for transfers between devices: 0.01 us -> 20.6 us  [exchange(): return lax.all_to_all(value, axes, split_axis=0, concat_axis=0, tiled=True)]
    pallas_call x1, Pallas kernels: 8.98 us -> 4.54 us  [trig(): pl.pallas_call(trig_kernel, grid_spec=spec, out_shape=pltpu.HBM((16, 2, 6...]
    all_to_all x2, starting transfers between devices: 20.7 us -> 18.1 us  [exchange(): return lax.all_to_all(value, axes, split_axis=0, concat_axis=0, tiled=True)]
    all_to_all x1, blocking collectives: 22.9 us -> 21.3 us  [exchange(): return lax.all_to_all(value, axes, split_axis=0, concat_axis=0, tiled=True)]
    convert_element_type x2, other arithmetic: 0.13 us -> 1.53 us  [add(): return (a.astype(F32) + b.astype(F32)).astype(BF)]
    ppermute x10, starting transfers between devices: 23.1 us -> 21.8 us  [swap(): return lax.ppermute(value, axis, [(0, 1), (1, 0)])]
    pallas_call x2 -> x3, Pallas kernels: 9.36 us -> 8.06 us  [the longest x2 6.06 us: rotate(): pl.pallas_call(rotate_kernel, grid_spec=spec, out_shape=[jax.ShapeDtypeSt...]
  transfers between devices with their start and end apart: 12 -> 12, of which waited for: 6 -> 5; matrix products, arithmetic and copies ran while one was open for 0% -> 1% of each run, Pallas kernels for 12% -> 9%
where the time goes in v2:
time: 114 us; the launch traced here: 113 us
  starting transfers between devices  39.9 us (35%)
  Pallas kernels  24.9 us (22%)
  waiting for transfers between devices  24.3 us (21%)
  blocking collectives  21.3 us (19%)
  other arithmetic  1.61 us (1%)
    ppermute x10, starting transfers between devices, swap(): return lax.ppermute(value, axis, [(0, 1), (1, 0)])  21.8 us
    all_to_all x1, blocking collectives, exchange(): return lax.all_to_all(value, axes, split_axis=0, concat_axis=0, tiled=True)  21.3 us
    all_to_all x2, waiting for transfers between devices, exchange(): return lax.all_to_all(value, axes, split_axis=0, concat_axis=0, tiled=True)  20.6 us
    all_to_all x2, starting transfers between devices, exchange(): return lax.all_to_all(value, axes, split_axis=0, concat_axis=0, tiled=True)  18.1 us
    pallas_call x1, Pallas kernels, levels(): pl.pallas_call(levels_kernel, grid=(4,), out_shape=jax.ShapeDtypeStruct((...  7.43 us
    pallas_call x2, Pallas kernels, rotate(): pl.pallas_call(rotate_kernel, grid_spec=spec, out_shape=[jax.ShapeDtypeSt...  6.06 us
    pallas_call x1, Pallas kernels, trig(): pl.pallas_call(trig_kernel, grid_spec=spec, out_shape=pltpu.HBM((16, 2, 6...  4.54 us
    pallas_call x1, Pallas kernels, final(): pl.pallas_call(final_kernel, grid_spec=spec, out_shape=jax.ShapeDtypeStru...  3.87 us
  transfers between devices with their start and end apart: 12, of which 5 were waited for; matrix products, arithmetic and copies ran while one was open for 1% of the time, Pallas kernels for 9%

profile of v2, /device:TPU:1, one launch (start us, length us, event | category | flops | bytes accessed | tf_op | source)
XLA Modules:
  0.0 113.2 jit_solution(10086772156955204167)
XLA Ops:
  0.0 0.1 pad_add_fusion.place
  0.1 3.3 %rotate_sent.1 = (bf16[2,256,512]{2,1,0:T(8,128)(2,1)}, bf16[2,256,512]{2,1,0:T(8,128)(2,1)S(1)}) custom-call(s32[3]{0:T(128)S(1)} %pad_add_fusion.place, bf16[2,4,256,512]{3,2,1,0:T(8,128)(2,1)} %bitcast.25, bf16[2,4,256,512]{3,2,1,0:T(8,128)(2,1)} %bitcast.26, bf16[2,4,256,512]{3,2,1,0:T(8,128)(2,1)} %bitcast.27, bf16[2,4,256,512]{3,2,1,0:T(8,128)(2,1)} %bitcast.28, ...), custom_call_target="tpu_custom_call" | custom-call | tf_op jit(solution)/shard_map/rotate_sent/pallas_call | solution.py:124
  3.4 3.6 %collective-permute-start = (bf16[2,256,512]{2,1,0:T(8,128)(2,1)}, bf16[2,256,512]{2,1,0:T(8,128)(2,1)S(1)}, u32[]{:S(2)}, u32[]{:S(2)}) collective-permute-start(bf16[2,256,512]{2,1,0:T(8,128)(2,1)} %get-tuple-element.16), channel_id=1, source_target_pairs={{0,32},{32,0},{1,33},{33,1},{2,34},{34,2},{3,35},{35,3},{4,36},{36... | collective-permute-start | bytes 1572872 | tf_op jit(solution)/shard_map/ppermute | solution.py:341
  7.0 2.9 %collective-permute-start.2 = (bf16[2,256,512]{2,1,0:T(8,128)(2,1)S(1)}, bf16[2,256,512]{2,1,0:T(8,128)(2,1)S(1)}, u32[]{:S(2)}, u32[]{:S(2)}) collective-permute-start(bf16[2,256,512]{2,1,0:T(8,128)(2,1)S(1)} %get-tuple-element.18), channel_id=1, source_target_pairs={{0,4},{4,0},{1,5},{5,1},{2,6},{6,2},{3,7},{7,3},{8,12},{12,8},{9,1... | collective-permute-start | bytes 1572872 | tf_op jit(solution)/shard_map/ppermute | solution.py:341
  9.9 2.0 %far_phases.1 = bf16[2,4,64,256]{3,2,1,0:T(8,128)(2,1)} custom-call(f32[3,2,4,4,4,512]{5,4,3,2,1,0:T(4,128)} %bitcast.37, f32[3,2,4,4,4,512]{5,4,3,2,1,0:T(4,128)} %bitcast.38, bf16[128,128]{1,0:T(8,128)(2,1)} %constant.35.clone.order_ref), custom_call_target="tpu_custom_call" | custom-call | tf_op jit(solution)/shard_map/far_phases/pallas_call | solution.py:148
  11.9 10.3 %all-to-all-start = ((bf16[64,8,256]{2,1,0:T(8,128)(2,1)}), bf16[64,8,256]{2,1,0:T(8,128)(2,1)S(1)}, u32[]{:S(2)}, u32[]{:S(2)}) async-start(bf16[64,8,256]{2,1,0:T(8,128)(2,1)} %bitcast.7), calls=%async_computation | async-start | bytes 524288 | tf_op jit(solution)/shard_map/all_to_all | solution.py:350
  22.2 2.7 %rotate_kept.1 = (bf16[2,256,512]{2,1,0:T(8,128)(2,1)S(1)}, bf16[2,256,512]{2,1,0:T(8,128)(2,1)S(1)}) custom-call(s32[3]{0:T(128)S(1)} %pad_add_fusion.place, bf16[2,4,256,512]{3,2,1,0:T(8,128)(2,1)} %bitcast.29, bf16[2,4,256,512]{3,2,1,0:T(8,128)(2,1)} %bitcast.30, bf16[2,4,256,512]{3,2,1,0:T(8,128)(2,1)} %bitcast.31, bf16[2,4,256,512]{3,2,1,0:T(8,128)(2,1)} %bitcast.32, ...), custom_call_target="tpu_custom_call" | custom-call | tf_op jit(solution)/shard_map/rotate_kept/pallas_call | solution.py:124
  24.9 0.0 copy-start.2
  24.9 0.0 collective-permute-done.come0
  24.9 0.8 fusion
  25.7 0.8 fusion.1
  26.5 9.1 %all-to-all-done = bf16[64,8,256]{2,1,0:T(8,128)(2,1)S(1)} async-done(((bf16[64,8,256]{2,1,0:T(8,128)(2,1)}), bf16[64,8,256]{2,1,0:T(8,128)(2,1)S(1)}, u32[]{:S(2)}, u32[]{:S(2)}) %all-to-all-start) | async-done | bytes 262176 | tf_op jit(solution)/shard_map/all_to_all | solution.py:350
  35.5 0.6 collective-permute-start.5
  36.1 1.6 %collective-permute-start.1 = (bf16[256,512]{1,0:T(8,128)(2,1)}, bf16[256,512]{1,0:T(8,128)(2,1)S(1)}, u32[]{:S(2)}, u32[]{:S(2)}) collective-permute-start(bf16[256,512]{1,0:T(8,128)(2,1)} %fusion), channel_id=1, source_target_pairs={{0,4},{4,0},{1,5},{5,1},{2,6},{6,2},{3,7},{7,3},{8,12},{12,8},{9,1... | collective-permute-start | bytes 786440 | tf_op jit(solution)/shard_map/ppermute | solution.py:341
  37.7 3.9 %collective-permute-start.4 = (bf16[8,64,256]{2,1,0:T(8,128)(2,1)S(1)}, bf16[8,64,256]{2,1,0:T(8,128)(2,1)S(1)}, u32[]{:S(2)}, u32[]{:S(2)}) collective-permute-start(bf16[8,64,256]{2,1,0:T(8,128)(2,1)S(1)} %bitcast.17), channel_id=1, source_target_pairs={{0,1},{1,0},{2,3},{3,2},{4,5},{5,4},{6,7},{7,6},{8,9},{9,8},{10,11... | collective-permute-start | bytes 786440 | tf_op jit(solution)/shard_map/ppermute | solution.py:341
  41.6 3.0 %collective-permute-start.6 = (bf16[8,64,256]{2,1,0:T(8,128)(2,1)S(1)}, bf16[8,64,256]{2,1,0:T(8,128)(2,1)S(1)}, u32[]{:S(2)}, u32[]{:S(2)}) collective-permute-start(bf16[8,64,256]{2,1,0:T(8,128)(2,1)S(1)} %collective-permute-done.5.refs_2_.refs_6_), channel_id=1, source_target_pairs={{0,1},{1,0},{2,3},{3,2},{4,5},{5,4},{6,7},{7,6},{8,9},{9,8},{10,11... | collective-permute-start | bytes 786440 | tf_op jit(solution)/shard_map/ppermute | solution.py:341
  44.6 1.0 sums.1
  45.7 0.1 collective-permute-done.6.refs_3_.refs_7_
  45.8 7.9 %all-to-all-start.1 = ((bf16[64,8,512]{2,1,0:T(8,128)(2,1)}), bf16[64,8,512]{2,1,0:T(8,128)(2,1)S(1)}, u32[]{:S(2)}, u32[]{:S(2)}) async-start(bf16[64,8,512]{2,1,0:T(8,128)(2,1)} %bitcast.9), calls=%async_computation.1 | async-start | bytes 1048576 | tf_op jit(solution)/shard_map/all_to_all | solution.py:350
  53.7 0.0 copy-start.3
  53.7 0.9 copy-done.3
  54.6 4.5 %trig.1.trig_ref = f32[16,2,64,512]{3,2,1,0:T(8,128)} custom-call(s32[3]{0:T(128)S(1)} %pad_add_fusion.place, bf16[8,64,256]{2,1,0:T(8,128)(2,1)S(1)} %bitcast.18, bf16[8,64,256]{2,1,0:T(8,128)(2,1)S(1)} %collective-permute-done.4.refs_1_.refs_5_, bf16[8,64,256]{2,1,0:T(8,128)(2,1)S(1)} %collective-permute-done.5.refs_2_.refs_6_, ...), custom_call_target="tpu_custom_call" | custom-call | tf_op jit(solution)/shard_map/trig/pallas_call | solution.py:221
  59.2 11.5 %all-to-all-done.1 = bf16[64,8,512]{2,1,0:T(8,128)(2,1)S(1)} async-done(((bf16[64,8,512]{2,1,0:T(8,128)(2,1)}), bf16[64,8,512]{2,1,0:T(8,128)(2,1)S(1)}, u32[]{:S(2)}, u32[]{:S(2)}) %all-to-all-start.1) | async-done | bytes 524320 | tf_op jit(solution)/shard_map/all_to_all | solution.py:350
  70.7 0.0 copy-start
  70.7 0.0 copy-start.1
  70.7 7.4 %levels.1 = bf16[8,8,8,256]{3,2,1,0:T(8,128)(2,1)S(1)} custom-call(bf16[2,256,512]{2,1,0:T(8,128)(2,1)S(1)} %bitcast.20, bf16[8,512,512]{2,1,0:T(8,128)(2,1)} %t_ref.3, f32[16,2,64,512]{3,2,1,0:T(8,128)} %trig.1.trig_ref, bf16[256,256]{1,0:T(8,128)(2,1)S(1)} %copy-done.5, bf16[256,256]{1,0:T(8,128)(2,1)S(1)} %copy-done.4, bf16[64,64]{1,0:T(8,128)(2,1)S(1)} %copy-done.6), custom_call_target="tpu_custom_call" | custom-call | tf_op jit(solution)/shard_map/levels/pallas_call | solution.py:285
  78.1 21.3 %all_to_all.15 = bf16[64,8,256]{2,1,0:T(8,128)(2,1)S(1)} all-to-all(bf16[64,8,256]{2,1,0:T(8,128)(2,1)S(1)} %bitcast.24), channel_id=1, replica_groups=mesh['x4'=2,'x3'=2,'y4'=2,'y3'=2,'y2'=2,'z4'=2,'z3'=2,'z2'=2] {'y4','z4'..., dimensions={0} | all-to-all | bytes 524288 | tf_op jit(solution)/shard_map/all_to_all | solution.py:350
  99.5 3.3 %collective-permute-start.7 = (bf16[512,256]{1,0:T(8,128)(2,1)S(1)}, bf16[512,256]{1,0:T(8,128)(2,1)S(1)}, u32[]{:S(2)}, u32[]{:S(2)}) collective-permute-start(bf16[512,256]{1,0:T(8,128)(2,1)S(1)} %bitcast.22), channel_id=1, source_target_pairs={{0,1},{1,0},{2,3},{3,2},{4,5},{5,4},{6,7},{7,6},{8,9},{9,8},{10,11... | collective-permute-start | bytes 786440 | tf_op jit(solution)/shard_map/ppermute | solution.py:341
  102.8 2.5 %collective-permute-done.8.n2 = bf16[512,256]{1,0:T(8,128)(2,1)S(1)} collective-permute-done((bf16[512,256]{1,0:T(8,128)(2,1)S(1)}, bf16[512,256]{1,0:T(8,128)(2,1)S(1)}, u32[]{:S(2)}, u32[]{:S(2)}) %collective-permute-start.8) | collective-permute-done | bytes 262176 | tf_op jit(solution)/shard_map/ppermute | solution.py:341
  105.3 2.9 %collective-permute-start.9 = (bf16[512,256]{1,0:T(8,128)(2,1)S(1)}, bf16[512,256]{1,0:T(8,128)(2,1)S(1)}, u32[]{:S(2)}, u32[]{:S(2)}) collective-permute-start(bf16[512,256]{1,0:T(8,128)(2,1)S(1)} %collective-permute-done.8.n2), channel_id=1, source_target_pairs={{0,1},{1,0},{2,3},{3,2},{4,5},{5,4},{6,7},{7,6},{8,9},{9,8},{10,11... | collective-permute-start | bytes 786440 | tf_op jit(solution)/shard_map/ppermute | solution.py:341
  108.2 1.2 %collective-permute-done.9.n3 = bf16[512,256]{1,0:T(8,128)(2,1)S(1)} collective-permute-done((bf16[512,256]{1,0:T(8,128)(2,1)S(1)}, bf16[512,256]{1,0:T(8,128)(2,1)S(1)}, u32[]{:S(2)}, u32[]{:S(2)}) %collective-permute-start.9) | collective-permute-done | bytes 262176 | tf_op jit(solution)/shard_map/ppermute | solution.py:341
  109.4 3.9 %final.1 = bf16[2,4,256,512]{3,2,1,0:T(8,128)(2,1)} custom-call(s32[3]{0:T(128)S(1)} %pad_add_fusion.place, bf16[512,256]{1,0:T(8,128)(2,1)S(1)} %bitcast.23, bf16[512,256]{1,0:T(8,128)(2,1)S(1)} %collective-permute-done.7.n1, bf16[512,256]{1,0:T(8,128)(2,1)S(1)} %collective-permute-done.8.n2, bf16[512,256]{1,0:T(8,128)(2,1)S(1)} %collective-permute-done.9.n3, ...), custom_call_target="tpu_custom_call" | custom-call | tf_op jit(solution)/shard_map/final/pallas_call | solution.py:331
  (17 shorter events, 0.0 us)
Async XLA Ops:
  3.4 21.5 %collective-permute-start = (bf16[2,256,512]{2,1,0:T(8,128)(2,1)}, bf16[2,256,512]{2,1,0:T(8,128)(2,1)S(1)}, u32[]{:S(2)}, u32[]{:S(2)}) collective-permute-start(bf16[2,256,512]{2,1,0:T(8,128)(2,1)} %get-tuple-element.16), channel_id=1, source_target_pairs={{0,32},{32,0},{1,33},{33,1},{2,34},{34,2},{3,35},{35,3},{4,36},{36... | collective-permute-start | bytes 1572872 | tf_op jit(solution)/shard_map/ppermute | solution.py:341
  7.0 18.7 %collective-permute-start.2 = (bf16[2,256,512]{2,1,0:T(8,128)(2,1)S(1)}, bf16[2,256,512]{2,1,0:T(8,128)(2,1)S(1)}, u32[]{:S(2)}, u32[]{:S(2)}) collective-permute-start(bf16[2,256,512]{2,1,0:T(8,128)(2,1)S(1)} %get-tuple-element.18), channel_id=1, source_target_pairs={{0,4},{4,0},{1,5},{5,1},{2,6},{6,2},{3,7},{7,3},{8,12},{12,8},{9,1... | collective-permute-start | bytes 1572872 | tf_op jit(solution)/shard_map/ppermute | solution.py:341
  11.9 23.6 %all-to-all-start = ((bf16[64,8,256]{2,1,0:T(8,128)(2,1)}), bf16[64,8,256]{2,1,0:T(8,128)(2,1)S(1)}, u32[]{:S(2)}, u32[]{:S(2)}) async-start(bf16[64,8,256]{2,1,0:T(8,128)(2,1)} %bitcast.7), calls=%async_computation | async-start | bytes 524288 | tf_op jit(solution)/shard_map/all_to_all | solution.py:350
  24.9 28.8 %copy-start.2 = (bf16[4,128,256]{2,1,0:T(8,128)(2,1)S(1)}, bf16[4,128,256]{2,1,0:T(8,128)(2,1)}, u32[]{:S(2)}) copy-start(bf16[4,128,256]{2,1,0:T(8,128)(2,1)} %constant.37.clone.refs_9_) | copy-start | bytes 786436
  35.5 6.1 %collective-permute-start.5 = (bf16[8,64,256]{2,1,0:T(8,128)(2,1)S(1)}, bf16[8,64,256]{2,1,0:T(8,128)(2,1)S(1)}, u32[]{:S(2)}, u32[]{:S(2)}) collective-permute-start(bf16[8,64,256]{2,1,0:T(8,128)(2,1)S(1)} %bitcast.16), channel_id=1, source_target_pairs={{0,8},{8,0},{1,9},{9,1},{2,10},{10,2},{3,11},{11,3},{4,12},{12,4},... | collective-permute-start | bytes 786440 | tf_op jit(solution)/shard_map/ppermute | solution.py:341
  36.1 8.5 %collective-permute-start.3 = (bf16[256,512]{1,0:T(8,128)(2,1)}, bf16[256,512]{1,0:T(8,128)(2,1)S(1)}, u32[]{:S(2)}, u32[]{:S(2)}) collective-permute-start(bf16[256,512]{1,0:T(8,128)(2,1)} %fusion.1), channel_id=1, source_target_pairs={{0,32},{32,0},{1,33},{33,1},{2,34},{34,2},{3,35},{35,3},{4,36},{36... | collective-permute-start | bytes 786440 | tf_op jit(solution)/shard_map/ppermute | solution.py:341
  36.1 8.5 %collective-permute-start.1 = (bf16[256,512]{1,0:T(8,128)(2,1)}, bf16[256,512]{1,0:T(8,128)(2,1)S(1)}, u32[]{:S(2)}, u32[]{:S(2)}) collective-permute-start(bf16[256,512]{1,0:T(8,128)(2,1)} %fusion), channel_id=1, source_target_pairs={{0,4},{4,0},{1,5},{5,1},{2,6},{6,2},{3,7},{7,3},{8,12},{12,8},{9,1... | collective-permute-start | bytes 786440 | tf_op jit(solution)/shard_map/ppermute | solution.py:341
  37.7 7.9 %collective-permute-start.4 = (bf16[8,64,256]{2,1,0:T(8,128)(2,1)S(1)}, bf16[8,64,256]{2,1,0:T(8,128)(2,1)S(1)}, u32[]{:S(2)}, u32[]{:S(2)}) collective-permute-start(bf16[8,64,256]{2,1,0:T(8,128)(2,1)S(1)} %bitcast.17), channel_id=1, source_target_pairs={{0,1},{1,0},{2,3},{3,2},{4,5},{5,4},{6,7},{7,6},{8,9},{9,8},{10,11... | collective-permute-start | bytes 786440 | tf_op jit(solution)/shard_map/ppermute | solution.py:341
  41.6 4.2 %collective-permute-start.6 = (bf16[8,64,256]{2,1,0:T(8,128)(2,1)S(1)}, bf16[8,64,256]{2,1,0:T(8,128)(2,1)S(1)}, u32[]{:S(2)}, u32[]{:S(2)}) collective-permute-start(bf16[8,64,256]{2,1,0:T(8,128)(2,1)S(1)} %collective-permute-done.5.refs_2_.refs_6_), channel_id=1, source_target_pairs={{0,1},{1,0},{2,3},{3,2},{4,5},{5,4},{6,7},{7,6},{8,9},{9,8},{10,11... | collective-permute-start | bytes 786440 | tf_op jit(solution)/shard_map/ppermute | solution.py:341
  45.7 25.0 %copy-start.4 = (bf16[256,256]{1,0:T(8,128)(2,1)S(1)}, bf16[256,256]{1,0:T(8,128)(2,1)}, u32[]{:S(2)}) copy-start(bf16[256,256]{1,0:T(8,128)(2,1)} %constant.39.clone.turn_ref) | copy-start | bytes 393220
  45.7 25.0 %copy-start.5 = (bf16[256,256]{1,0:T(8,128)(2,1)S(1)}, bf16[256,256]{1,0:T(8,128)(2,1)}, u32[]{:S(2)}) copy-start(bf16[256,256]{1,0:T(8,128)(2,1)} %constant.38.clone.enter_ref) | copy-start | bytes 393220
  45.7 25.0 %copy-start.6 = (bf16[64,64]{1,0:T(8,128)(2,1)S(1)}, bf16[64,64]{1,0:T(8,128)(2,1)}, u32[]{:S(2)}) copy-start(bf16[64,64]{1,0:T(8,128)(2,1)} %constant.40.clone.leave_ref) | copy-start | bytes 24580
  45.8 24.9 %all-to-all-start.1 = ((bf16[64,8,512]{2,1,0:T(8,128)(2,1)}), bf16[64,8,512]{2,1,0:T(8,128)(2,1)S(1)}, u32[]{:S(2)}, u32[]{:S(2)}) async-start(bf16[64,8,512]{2,1,0:T(8,128)(2,1)} %bitcast.9), calls=%async_computation.1 | async-start | bytes 1048576 | tf_op jit(solution)/shard_map/all_to_all | solution.py:350
  53.7 1.0 copy-start.3
  70.7 38.7 %copy-start = (bf16[8,512,512]{2,1,0:T(8,128)(2,1)S(1)}, bf16[8,512,512]{2,1,0:T(8,128)(2,1)}, u32[]{:S(2)}) copy-start(bf16[8,512,512]{2,1,0:T(8,128)(2,1)} %t_ref.3) | copy-start | bytes 12582916
  70.7 38.7 %copy-start.1 = (bf16[4,256,256]{2,1,0:T(8,128)(2,1)S(1)}, bf16[4,256,256]{2,1,0:T(8,128)(2,1)}, u32[]{:S(2)}) copy-start(bf16[4,256,256]{2,1,0:T(8,128)(2,1)} %constant.41.clone.pick_ref) | copy-start | bytes 1572868
  99.5 5.8 %collective-permute-start.8 = (bf16[512,256]{1,0:T(8,128)(2,1)S(1)}, bf16[512,256]{1,0:T(8,128)(2,1)S(1)}, u32[]{:S(2)}, u32[]{:S(2)}) collective-permute-start(bf16[512,256]{1,0:T(8,128)(2,1)S(1)} %bitcast.21), channel_id=1, source_target_pairs={{0,8},{8,0},{1,9},{9,1},{2,10},{10,2},{3,11},{11,3},{4,12},{12,4},... | collective-permute-start | bytes 786440 | tf_op jit(solution)/shard_map/ppermute | solution.py:341
  99.5 8.7 %collective-permute-start.7 = (bf16[512,256]{1,0:T(8,128)(2,1)S(1)}, bf16[512,256]{1,0:T(8,128)(2,1)S(1)}, u32[]{:S(2)}, u32[]{:S(2)}) collective-permute-start(bf16[512,256]{1,0:T(8,128)(2,1)S(1)} %bitcast.22), channel_id=1, source_target_pairs={{0,1},{1,0},{2,3},{3,2},{4,5},{5,4},{6,7},{7,6},{8,9},{9,8},{10,11... | collective-permute-start | bytes 786440 | tf_op jit(solution)/shard_map/ppermute | solution.py:341
  105.3 4.1 %collective-permute-start.9 = (bf16[512,256]{1,0:T(8,128)(2,1)S(1)}, bf16[512,256]{1,0:T(8,128)(2,1)S(1)}, u32[]{:S(2)}, u32[]{:S(2)}) collective-permute-start(bf16[512,256]{1,0:T(8,128)(2,1)S(1)} %collective-permute-done.8.n2), channel_id=1, source_target_pairs={{0,1},{1,0},{2,3},{3,2},{4,5},{5,4},{6,7},{7,6},{8,9},{9,8},{10,11... | collective-permute-start | bytes 786440 | tf_op jit(solution)/shard_map/ppermute | solution.py:341

commit v3 on v2

--- a/solution.py
+++ b/solution.py
@@ -223,8 +223,9 @@
         grid_spec=spec,
         out_shape=pltpu.HBM((16, 2, 64, CHEB), F32),
         compiler_params=params(12),
+        cost_estimate=pl.CostEstimate(flops=7 * 10**9, bytes_accessed=10**6, transcendentals=0),
         name="trig",
-    )(place, *near, *near, jnp.asarray(FIRST, BF), jnp.asarray(SECOND, BF))
+    )(place, *near, *near, in_hbm(jnp.asarray(FIRST, BF)), in_hbm(jnp.asarray(SECOND, BF)))
 
 
 def levels_kernel(x_ref, t_ref, trig_ref, enter_ref, turn_ref, leave_ref, out_ref, left, middle, even, odd):
@@ -365,7 +366,6 @@
     near = four(phases.reshape(8, 64, HALF))
     again0, again1 = swap(again0, "z4"), swap(again1, "y4")
     share = sums(keep0, come0, again0, keep1, come1, again1)
-    share, near = lax.optimization_barrier((share, near))
     share = exchange(share.reshape(64, 8, CHEB), ("x4", "x3", "y3", "z3", "y2", "z2"))
     waves = trig(place, near)
     done = levels(share.reshape(2, 256, CHEB), translation, waves)

time: 114 us -> 108 us (0.947)
  waiting for transfers between devices: 24.3 us -> 19.9 us
    all_to_all x2, waiting for transfers between devices: 20.6 us -> 13.9 us  [exchange(): return lax.all_to_all(value, axes, split_axis=0, concat_axis=0, tiled=True)]
    ppermute x10, starting transfers between devices: 21.8 us -> 19.4 us  [swap(): return lax.ppermute(value, axis, [(0, 1), (1, 0)])]
    ppermute x10, waiting for transfers between devices: 3.79 us -> 6.03 us  [swap(): return lax.ppermute(value, axis, [(0, 1), (1, 0)])]
    all_to_all x2, starting transfers between devices: 18.1 us -> 20.1 us  [exchange(): return lax.all_to_all(value, axes, split_axis=0, concat_axis=0, tiled=True)]
  transfers between devices with their start and end apart: 12 -> 12, of which waited for: 5 -> 7; matrix products, arithmetic and copies ran while one was open for 1% -> 1% of each run, Pallas kernels for 9% -> 10%
where the time goes in v3:
time: 108 us
  starting transfers between devices  39.5 us (37%)
  Pallas kernels  25.2 us (23%)
  blocking collectives  22 us (20%)
  waiting for transfers between devices  19.9 us (18%)
    all_to_all x1, blocking collectives, exchange(): return lax.all_to_all(value, axes, split_axis=0, concat_axis=0, tiled=True)  22 us
    all_to_all x2, starting transfers between devices, exchange(): return lax.all_to_all(value, axes, split_axis=0, concat_axis=0, tiled=True)  20.1 us
    ppermute x10, starting transfers between devices, swap(): return lax.ppermute(value, axis, [(0, 1), (1, 0)])  19.4 us
    all_to_all x2, waiting for transfers between devices, exchange(): return lax.all_to_all(value, axes, split_axis=0, concat_axis=0, tiled=True)  13.9 us
    pallas_call x1, Pallas kernels, levels(): pl.pallas_call(levels_kernel, grid=(4,), out_shape=jax.ShapeDtypeStruct((...  7.43 us
    ppermute x10, waiting for transfers between devices, swap(): return lax.ppermute(value, axis, [(0, 1), (1, 0)])  6.03 us
    pallas_call x1, Pallas kernels, trig(): pl.pallas_call(trig_kernel, grid_spec=spec, out_shape=pltpu.HBM((16, 2, 6...  5.42 us
    pallas_call x2, Pallas kernels, rotate(): pl.pallas_call(rotate_kernel, grid_spec=spec, out_shape=[jax.ShapeDtypeSt...  5.41 us
  transfers between devices with their start and end apart: 12, of which 7 were waited for; matrix products, arithmetic and copies ran while one was open for 1% of the time, Pallas kernels for 10%

profile of v3, /device:TPU:1, one launch (start us, length us, event | category | flops | bytes accessed | tf_op | source)
XLA Modules:
  0.0 107.7 jit_solution(3985827310313688563)
XLA Ops:
  0.0 0.1 pad_add_fusion.place
  0.1 2.7 %rotate_sent.1 = (bf16[2,256,512]{2,1,0:T(8,128)(2,1)S(1)}, bf16[2,256,512]{2,1,0:T(8,128)(2,1)S(1)}) custom-call(s32[3]{0:T(128)S(1)} %pad_add_fusion.place, bf16[2,4,256,512]{3,2,1,0:T(8,128)(2,1)} %bitcast.25, bf16[2,4,256,512]{3,2,1,0:T(8,128)(2,1)} %bitcast.26, bf16[2,4,256,512]{3,2,1,0:T(8,128)(2,1)} %bitcast.27, bf16[2,4,256,512]{3,2,1,0:T(8,128)(2,1)} %bitcast.28, ...), custom_call_target="tpu_custom_call" | custom-call | tf_op jit(solution)/shard_map/rotate_sent/pallas_call | solution.py:124
  2.8 3.8 %collective-permute-start.2 = (bf16[2,256,512]{2,1,0:T(8,128)(2,1)S(1)}, bf16[2,256,512]{2,1,0:T(8,128)(2,1)S(1)}, u32[]{:S(2)}, u32[]{:S(2)}) collective-permute-start(bf16[2,256,512]{2,1,0:T(8,128)(2,1)S(1)} %get-tuple-element.13), channel_id=1, source_target_pairs={{0,4},{4,0},{1,5},{5,1},{2,6},{6,2},{3,7},{7,3},{8,12},{12,8},{9,1... | collective-permute-start | bytes 1572872 | tf_op jit(solution)/shard_map/ppermute | solution.py:342
  6.6 2.7 %collective-permute-start = (bf16[2,256,512]{2,1,0:T(8,128)(2,1)S(1)}, bf16[2,256,512]{2,1,0:T(8,128)(2,1)S(1)}, u32[]{:S(2)}, u32[]{:S(2)}) collective-permute-start(bf16[2,256,512]{2,1,0:T(8,128)(2,1)S(1)} %get-tuple-element.11), channel_id=1, source_target_pairs={{0,32},{32,0},{1,33},{33,1},{2,34},{34,2},{3,35},{35,3},{4,36},{36... | collective-permute-start | bytes 1572872 | tf_op jit(solution)/shard_map/ppermute | solution.py:342
  9.4 2.0 %far_phases.1 = bf16[2,4,64,256]{3,2,1,0:T(8,128)(2,1)} custom-call(f32[3,2,4,4,4,512]{5,4,3,2,1,0:T(4,128)} %bitcast.37, f32[3,2,4,4,4,512]{5,4,3,2,1,0:T(4,128)} %bitcast.38, bf16[128,128]{1,0:T(8,128)(2,1)} %constant.35.clone.order_ref), custom_call_target="tpu_custom_call" | custom-call | tf_op jit(solution)/shard_map/far_phases/pallas_call | solution.py:148
  11.4 10.3 %all-to-all-start.1 = ((bf16[64,8,256]{2,1,0:T(8,128)(2,1)}), bf16[64,8,256]{2,1,0:T(8,128)(2,1)S(1)}, u32[]{:S(2)}, u32[]{:S(2)}) async-start(bf16[64,8,256]{2,1,0:T(8,128)(2,1)} %bitcast.9), calls=%async_computation.1 | async-start | bytes 524288 | tf_op jit(solution)/shard_map/all_to_all | solution.py:351
  21.6 2.7 %rotate_kept.1 = (bf16[2,256,512]{2,1,0:T(8,128)(2,1)S(1)}, bf16[2,256,512]{2,1,0:T(8,128)(2,1)S(1)}) custom-call(s32[3]{0:T(128)S(1)} %pad_add_fusion.place, bf16[2,4,256,512]{3,2,1,0:T(8,128)(2,1)} %bitcast.29, bf16[2,4,256,512]{3,2,1,0:T(8,128)(2,1)} %bitcast.30, bf16[2,4,256,512]{3,2,1,0:T(8,128)(2,1)} %bitcast.31, bf16[2,4,256,512]{3,2,1,0:T(8,128)(2,1)} %bitcast.32, ...), custom_call_target="tpu_custom_call" | custom-call | tf_op jit(solution)/shard_map/rotate_kept/pallas_call | solution.py:124
  24.4 0.8 fusion.1
  25.1 2.5 %collective-permute-start.3 = (bf16[256,512]{1,0:T(8,128)(2,1)}, bf16[256,512]{1,0:T(8,128)(2,1)S(1)}, u32[]{:S(2)}, u32[]{:S(2)}) collective-permute-start(bf16[256,512]{1,0:T(8,128)(2,1)} %fusion.1), channel_id=1, source_target_pairs={{0,32},{32,0},{1,33},{33,1},{2,34},{34,2},{3,35},{35,3},{4,36},{36... | collective-permute-start | bytes 786440 | tf_op jit(solution)/shard_map/ppermute | solution.py:342
  27.7 0.1 fusion
  27.7 2.8 %collective-permute-start.1 = (bf16[256,512]{1,0:T(8,128)(2,1)S(1)}, bf16[256,512]{1,0:T(8,128)(2,1)S(1)}, u32[]{:S(2)}, u32[]{:S(2)}) collective-permute-start(bf16[256,512]{1,0:T(8,128)(2,1)S(1)} %fusion), channel_id=1, source_target_pairs={{0,4},{4,0},{1,5},{5,1},{2,6},{6,2},{3,7},{7,3},{8,12},{12,8},{9,1... | collective-permute-start | bytes 786440 | tf_op jit(solution)/shard_map/ppermute | solution.py:342
  30.5 4.5 %all-to-all-done.1 = bf16[64,8,256]{2,1,0:T(8,128)(2,1)S(1)} async-done(((bf16[64,8,256]{2,1,0:T(8,128)(2,1)}), bf16[64,8,256]{2,1,0:T(8,128)(2,1)S(1)}, u32[]{:S(2)}, u32[]{:S(2)}) %all-to-all-start.1) | async-done | bytes 262176 | tf_op jit(solution)/shard_map/all_to_all | solution.py:351
  35.0 0.7 collective-permute-start.5
  35.7 0.9 collective-permute-done.1.again0
  36.5 1.0 sums.1
  37.6 9.9 %all-to-all-start = ((bf16[64,8,512]{2,1,0:T(8,128)(2,1)}), bf16[64,8,512]{2,1,0:T(8,128)(2,1)S(1)}, u32[]{:S(2)}, u32[]{:S(2)}) async-start(bf16[64,8,512]{2,1,0:T(8,128)(2,1)} %bitcast.7), calls=%async_computation | async-start | bytes 1048576 | tf_op jit(solution)/shard_map/all_to_all | solution.py:351
  47.4 0.0 copy-start.2
  47.5 0.0 copy-start.3
  47.5 0.0 copy-start.4
  47.5 0.5 collective-permute-start.4
  48.0 0.1 collective-permute-start.6
  48.1 1.1 collective-permute-done.4.refs_1_.refs_5_
  49.2 0.4 collective-permute-done.6.refs_3_.refs_7_
  49.6 5.4 %trig.1.trig_ref = f32[16,2,64,512]{3,2,1,0:T(8,128)} custom-call(s32[3]{0:T(128)S(1)} %pad_add_fusion.place, bf16[8,64,256]{2,1,0:T(8,128)(2,1)S(1)} %bitcast.23, bf16[8,64,256]{2,1,0:T(8,128)(2,1)S(1)} %collective-permute-done.4.refs_1_.refs_5_, bf16[8,64,256]{2,1,0:T(8,128)(2,1)S(1)} %collective-permute-done.5.refs_2_.refs_6_, ...), custom_call_target="tpu_custom_call" | custom-call | flops 7000000000 | bytes 1000000 | tf_op jit(solution)/shard_map/trig/pallas_call | solution.py:221
  55.0 9.4 %all-to-all-done = bf16[64,8,512]{2,1,0:T(8,128)(2,1)S(1)} async-done(((bf16[64,8,512]{2,1,0:T(8,128)(2,1)}), bf16[64,8,512]{2,1,0:T(8,128)(2,1)S(1)}, u32[]{:S(2)}, u32[]{:S(2)}) %all-to-all-start) | async-done | bytes 524320 | tf_op jit(solution)/shard_map/all_to_all | solution.py:351
  64.5 7.4 %levels.1 = bf16[8,8,8,256]{3,2,1,0:T(8,128)(2,1)S(1)} custom-call(bf16[2,256,512]{2,1,0:T(8,128)(2,1)S(1)} %bitcast.16, bf16[8,512,512]{2,1,0:T(8,128)(2,1)} %t_ref.3, f32[16,2,64,512]{3,2,1,0:T(8,128)} %trig.1.trig_ref, bf16[256,256]{1,0:T(8,128)(2,1)S(1)} %copy-done.3, bf16[256,256]{1,0:T(8,128)(2,1)S(1)} %copy-done.2, bf16[64,64]{1,0:T(8,128)(2,1)S(1)} %copy-done.4), custom_call_target="tpu_custom_call" | custom-call | tf_op jit(solution)/shard_map/levels/pallas_call | solution.py:286
  71.9 22.0 %all_to_all.15 = bf16[64,8,256]{2,1,0:T(8,128)(2,1)S(1)} all-to-all(bf16[64,8,256]{2,1,0:T(8,128)(2,1)S(1)} %bitcast.20), channel_id=1, replica_groups=mesh['x4'=2,'x3'=2,'y4'=2,'y3'=2,'y2'=2,'z4'=2,'z3'=2,'z2'=2] {'y4','z4'..., dimensions={0} | all-to-all | bytes 524288 | tf_op jit(solution)/shard_map/all_to_all | solution.py:351
  93.9 3.3 %collective-permute-start.7 = (bf16[512,256]{1,0:T(8,128)(2,1)S(1)}, bf16[512,256]{1,0:T(8,128)(2,1)S(1)}, u32[]{:S(2)}, u32[]{:S(2)}) collective-permute-start(bf16[512,256]{1,0:T(8,128)(2,1)S(1)} %bitcast.18), channel_id=1, source_target_pairs={{0,1},{1,0},{2,3},{3,2},{4,5},{5,4},{6,7},{7,6},{8,9},{9,8},{10,11... | collective-permute-start | bytes 786440 | tf_op jit(solution)/shard_map/ppermute | solution.py:342
  97.2 2.5 %collective-permute-done.8.n2 = bf16[512,256]{1,0:T(8,128)(2,1)S(1)} collective-permute-done((bf16[512,256]{1,0:T(8,128)(2,1)S(1)}, bf16[512,256]{1,0:T(8,128)(2,1)S(1)}, u32[]{:S(2)}, u32[]{:S(2)}) %collective-permute-start.8) | collective-permute-done | bytes 262176 | tf_op jit(solution)/shard_map/ppermute | solution.py:342
  99.7 2.9 %collective-permute-start.9 = (bf16[512,256]{1,0:T(8,128)(2,1)S(1)}, bf16[512,256]{1,0:T(8,128)(2,1)S(1)}, u32[]{:S(2)}, u32[]{:S(2)}) collective-permute-start(bf16[512,256]{1,0:T(8,128)(2,1)S(1)} %collective-permute-done.8.n2), channel_id=1, source_target_pairs={{0,1},{1,0},{2,3},{3,2},{4,5},{5,4},{6,7},{7,6},{8,9},{9,8},{10,11... | collective-permute-start | bytes 786440 | tf_op jit(solution)/shard_map/ppermute | solution.py:342
  102.7 1.2 %collective-permute-done.9.n3 = bf16[512,256]{1,0:T(8,128)(2,1)S(1)} collective-permute-done((bf16[512,256]{1,0:T(8,128)(2,1)S(1)}, bf16[512,256]{1,0:T(8,128)(2,1)S(1)}, u32[]{:S(2)}, u32[]{:S(2)}) %collective-permute-start.9) | collective-permute-done | bytes 262176 | tf_op jit(solution)/shard_map/ppermute | solution.py:342
  103.8 3.9 %final.1 = bf16[2,4,256,512]{3,2,1,0:T(8,128)(2,1)} custom-call(s32[3]{0:T(128)S(1)} %pad_add_fusion.place, bf16[512,256]{1,0:T(8,128)(2,1)S(1)} %bitcast.19, bf16[512,256]{1,0:T(8,128)(2,1)S(1)} %collective-permute-done.7.n1, bf16[512,256]{1,0:T(8,128)(2,1)S(1)} %collective-permute-done.8.n2, bf16[512,256]{1,0:T(8,128)(2,1)S(1)} %collective-permute-done.9.n3, ...), custom_call_target="tpu_custom_call" | custom-call | tf_op jit(solution)/shard_map/final/pallas_call | solution.py:332
  (13 shorter events, 0.0 us)
Async XLA Ops:
  2.8 21.6 %collective-permute-start.2 = (bf16[2,256,512]{2,1,0:T(8,128)(2,1)S(1)}, bf16[2,256,512]{2,1,0:T(8,128)(2,1)S(1)}, u32[]{:S(2)}, u32[]{:S(2)}) collective-permute-start(bf16[2,256,512]{2,1,0:T(8,128)(2,1)S(1)} %get-tuple-element.13), channel_id=1, source_target_pairs={{0,4},{4,0},{1,5},{5,1},{2,6},{6,2},{3,7},{7,3},{8,12},{12,8},{9,1... | collective-permute-start | bytes 1572872 | tf_op jit(solution)/shard_map/ppermute | solution.py:342
  6.6 21.0 %collective-permute-start = (bf16[2,256,512]{2,1,0:T(8,128)(2,1)S(1)}, bf16[2,256,512]{2,1,0:T(8,128)(2,1)S(1)}, u32[]{:S(2)}, u32[]{:S(2)}) collective-permute-start(bf16[2,256,512]{2,1,0:T(8,128)(2,1)S(1)} %get-tuple-element.11), channel_id=1, source_target_pairs={{0,32},{32,0},{1,33},{33,1},{2,34},{34,2},{3,35},{35,3},{4,36},{36... | collective-permute-start | bytes 1572872 | tf_op jit(solution)/shard_map/ppermute | solution.py:342
  11.4 23.6 %all-to-all-start.1 = ((bf16[64,8,256]{2,1,0:T(8,128)(2,1)}), bf16[64,8,256]{2,1,0:T(8,128)(2,1)S(1)}, u32[]{:S(2)}, u32[]{:S(2)}) async-start(bf16[64,8,256]{2,1,0:T(8,128)(2,1)} %bitcast.9), calls=%async_computation.1 | async-start | bytes 524288 | tf_op jit(solution)/shard_map/all_to_all | solution.py:351
  25.1 10.5 %collective-permute-start.3 = (bf16[256,512]{1,0:T(8,128)(2,1)}, bf16[256,512]{1,0:T(8,128)(2,1)S(1)}, u32[]{:S(2)}, u32[]{:S(2)}) collective-permute-start(bf16[256,512]{1,0:T(8,128)(2,1)} %fusion.1), channel_id=1, source_target_pairs={{0,32},{32,0},{1,33},{33,1},{2,34},{34,2},{3,35},{35,3},{4,36},{36... | collective-permute-start | bytes 786440 | tf_op jit(solution)/shard_map/ppermute | solution.py:342
  27.7 8.8 %collective-permute-start.1 = (bf16[256,512]{1,0:T(8,128)(2,1)S(1)}, bf16[256,512]{1,0:T(8,128)(2,1)S(1)}, u32[]{:S(2)}, u32[]{:S(2)}) collective-permute-start(bf16[256,512]{1,0:T(8,128)(2,1)S(1)} %fusion), channel_id=1, source_target_pairs={{0,4},{4,0},{1,5},{5,1},{2,6},{6,2},{3,7},{7,3},{8,12},{12,8},{9,1... | collective-permute-start | bytes 786440 | tf_op jit(solution)/shard_map/ppermute | solution.py:342
  35.0 13.0 %collective-permute-start.5 = (bf16[8,64,256]{2,1,0:T(8,128)(2,1)S(1)}, bf16[8,64,256]{2,1,0:T(8,128)(2,1)S(1)}, u32[]{:S(2)}, u32[]{:S(2)}) collective-permute-start(bf16[8,64,256]{2,1,0:T(8,128)(2,1)S(1)} %bitcast.21), channel_id=1, source_target_pairs={{0,8},{8,0},{1,9},{9,1},{2,10},{10,2},{3,11},{11,3},{4,12},{12,4},... | collective-permute-start | bytes 786440 | tf_op jit(solution)/shard_map/ppermute | solution.py:342
  37.6 26.8 %all-to-all-start = ((bf16[64,8,512]{2,1,0:T(8,128)(2,1)}), bf16[64,8,512]{2,1,0:T(8,128)(2,1)S(1)}, u32[]{:S(2)}, u32[]{:S(2)}) async-start(bf16[64,8,512]{2,1,0:T(8,128)(2,1)} %bitcast.7), calls=%async_computation | async-start | bytes 1048576 | tf_op jit(solution)/shard_map/all_to_all | solution.py:351
  47.4 17.0 %copy-start.2 = (bf16[256,256]{1,0:T(8,128)(2,1)S(1)}, bf16[256,256]{1,0:T(8,128)(2,1)}, u32[]{:S(2)}) copy-start(bf16[256,256]{1,0:T(8,128)(2,1)} %constant.39.clone.turn_ref) | copy-start | bytes 393220
  47.5 17.0 %copy-start.3 = (bf16[256,256]{1,0:T(8,128)(2,1)S(1)}, bf16[256,256]{1,0:T(8,128)(2,1)}, u32[]{:S(2)}) copy-start(bf16[256,256]{1,0:T(8,128)(2,1)} %constant.38.clone.enter_ref) | copy-start | bytes 393220
  47.5 17.0 %copy-start.4 = (bf16[64,64]{1,0:T(8,128)(2,1)S(1)}, bf16[64,64]{1,0:T(8,128)(2,1)}, u32[]{:S(2)}) copy-start(bf16[64,64]{1,0:T(8,128)(2,1)} %constant.40.clone.leave_ref) | copy-start | bytes 24580
  47.5 1.7 %collective-permute-start.4 = (bf16[8,64,256]{2,1,0:T(8,128)(2,1)S(1)}, bf16[8,64,256]{2,1,0:T(8,128)(2,1)S(1)}, u32[]{:S(2)}, u32[]{:S(2)}) collective-permute-start(bf16[8,64,256]{2,1,0:T(8,128)(2,1)S(1)} %bitcast.22), channel_id=1, source_target_pairs={{0,1},{1,0},{2,3},{3,2},{4,5},{5,4},{6,7},{7,6},{8,9},{9,8},{10,11... | collective-permute-start | bytes 786440 | tf_op jit(solution)/shard_map/ppermute | solution.py:342
  48.0 1.5 %collective-permute-start.6 = (bf16[8,64,256]{2,1,0:T(8,128)(2,1)S(1)}, bf16[8,64,256]{2,1,0:T(8,128)(2,1)S(1)}, u32[]{:S(2)}, u32[]{:S(2)}) collective-permute-start(bf16[8,64,256]{2,1,0:T(8,128)(2,1)S(1)} %collective-permute-done.5.refs_2_.refs_6_), channel_id=1, source_target_pairs={{0,1},{1,0},{2,3},{3,2},{4,5},{5,4},{6,7},{7,6},{8,9},{9,8},{10,11... | collective-permute-start | bytes 786440 | tf_op jit(solution)/shard_map/ppermute | solution.py:342
  64.4 39.4 %copy-start = (bf16[8,512,512]{2,1,0:T(8,128)(2,1)S(1)}, bf16[8,512,512]{2,1,0:T(8,128)(2,1)}, u32[]{:S(2)}) copy-start(bf16[8,512,512]{2,1,0:T(8,128)(2,1)} %t_ref.3) | copy-start | bytes 12582916
  64.4 39.4 %copy-start.1 = (bf16[4,256,256]{2,1,0:T(8,128)(2,1)S(1)}, bf16[4,256,256]{2,1,0:T(8,128)(2,1)}, u32[]{:S(2)}) copy-start(bf16[4,256,256]{2,1,0:T(8,128)(2,1)} %constant.41.clone.pick_ref) | copy-start | bytes 1572868
  93.9 5.8 %collective-permute-start.8 = (bf16[512,256]{1,0:T(8,128)(2,1)S(1)}, bf16[512,256]{1,0:T(8,128)(2,1)S(1)}, u32[]{:S(2)}, u32[]{:S(2)}) collective-permute-start(bf16[512,256]{1,0:T(8,128)(2,1)S(1)} %bitcast.17), channel_id=1, source_target_pairs={{0,8},{8,0},{1,9},{9,1},{2,10},{10,2},{3,11},{11,3},{4,12},{12,4},... | collective-permute-start | bytes 786440 | tf_op jit(solution)/shard_map/ppermute | solution.py:342
  93.9 8.7 %collective-permute-start.7 = (bf16[512,256]{1,0:T(8,128)(2,1)S(1)}, bf16[512,256]{1,0:T(8,128)(2,1)S(1)}, u32[]{:S(2)}, u32[]{:S(2)}) collective-permute-start(bf16[512,256]{1,0:T(8,128)(2,1)S(1)} %bitcast.18), channel_id=1, source_target_pairs={{0,1},{1,0},{2,3},{3,2},{4,5},{5,4},{6,7},{7,6},{8,9},{9,8},{10,11... | collective-permute-start | bytes 786440 | tf_op jit(solution)/shard_map/ppermute | solution.py:342
  99.7 4.1 %collective-permute-start.9 = (bf16[512,256]{1,0:T(8,128)(2,1)S(1)}, bf16[512,256]{1,0:T(8,128)(2,1)S(1)}, u32[]{:S(2)}, u32[]{:S(2)}) collective-permute-start(bf16[512,256]{1,0:T(8,128)(2,1)S(1)} %collective-permute-done.8.n2), channel_id=1, source_target_pairs={{0,1},{1,0},{2,3},{3,2},{4,5},{5,4},{6,7},{7,6},{8,9},{9,8},{10,11... | collective-permute-start | bytes 786440 | tf_op jit(solution)/shard_map/ppermute | solution.py:342

commit v4 on v3

--- a/solution.py
+++ b/solution.py
@@ -81,9 +81,7 @@
     return pltpu.CompilerParams(vmem_limit_bytes=mebibytes * 1024 * 1024)
 
 
-def rotate_kernel(place, *refs):
-    blocks, angles = refs[0:4], refs[4:8]
-    mix_ref, first, second, angle, mixed = refs[8:]
+def rotate_blocks(blocks, angles, mix_ref, first, second, angle, mixed):
     for j in range(4):
         for x2 in range(2):
             for y in range(2):
@@ -99,38 +97,12 @@
         (first, second)[j // 2][j % 2] = dot(mix_ref[...], mixed[j]).astype(BF)
 
 
-def rotate(place, weights, angles, keep):
-    def block(j):
-        y, z = ((1, 0), (1, 1), (0, 1), (1, 1))[j] if keep else ((0, 0), (0, 1), (0, 0), (1, 0))[j]
-        return lambda p: (p[0] ^ (1 - y)) * 2 + (p[1] ^ (1 - z))
-
-    def weight(j):
-        at = block(j)
-        return pl.BlockSpec((2, 1, 128, CHEB), lambda i, p: (0, at(p), j // 2, 0))
-
-    def phase(j):
-        at = block(j)
-        return pl.BlockSpec((1, 2, 1, 2, 4, CHEB), lambda i, p: (0, 0, at(p), j // 2, 0, 0))
-
-    spec = pltpu.PrefetchScalarGridSpec(
-        num_scalar_prefetch=1,
-        grid=(1,),
-        in_specs=[weight(j) for j in range(4)]
-        + [phase(j) for j in range(4)]
-        + [pl.BlockSpec((256, 256), lambda i, p: (0, 0))],
-        out_specs=[pl.BlockSpec((2, 256, CHEB), lambda i, p: (0, 0, 0))] * 2,
-        scratch_shapes=[pltpu.VMEM((4, 2, 8, CHEB), F32), pltpu.VMEM((4, 256, CHEB), BF)],
-    )
-    return pl.pallas_call(
-        rotate_kernel,
-        grid_spec=spec,
-        out_shape=[jax.ShapeDtypeStruct((2, 256, CHEB), BF)] * 2,
-        compiler_params=params(12),
-        name="rotate_kept" if keep else "rotate_sent",
-    )(place, *[weights] * 4, *[angles] * 4, in_hbm(jnp.asarray(MIX, BF)))
-
-
-def phase_kernel(a1_ref, a2_ref, order_ref, phases, far):
+def send_kernel(place, *refs):
+    rotate_blocks(refs[0:4], refs[4:8], *refs[8:])
+
+
+def keep_kernel(place, *refs):
+    mix_ref, a1_ref, a2_ref, order_ref, first, second, phases, angle, mixed, far = refs[8:]
     for block in range(4):
         for level, ref in enumerate((a1_ref, a2_ref)):
             for x2 in range(2):
@@ -142,23 +114,48 @@
         value = dot(order_ref[...], value).astype(BF)
         for high in range(2):
             phases[high, block] = value[64 * high : 64 * high + 64]
-
-
-def far_phases(angles):
-    return pl.pallas_call(
-        phase_kernel,
-        grid=(1,),
-        in_specs=[
-            pl.BlockSpec((1, 2, 4, 4, 4, CHEB), lambda i: (1, 0, 0, 0, 0, 0)),
-            pl.BlockSpec((1, 2, 4, 4, 4, CHEB), lambda i: (2, 0, 0, 0, 0, 0)),
-            pl.BlockSpec((128, 128), lambda i: (0, 0)),
-        ],
-        out_specs=pl.BlockSpec((2, 4, 64, HALF), lambda i: (0, 0, 0, 0)),
-        out_shape=jax.ShapeDtypeStruct((2, 4, 64, HALF), BF),
-        scratch_shapes=[pltpu.VMEM((4, 64, CHEB), F32)],
-        compiler_params=params(8),
-        name="far_phases",
-    )(angles, angles, in_hbm(jnp.asarray(SEND_PHASE, BF)))
+    rotate_blocks(refs[0:4], refs[4:8], mix_ref, first, second, angle, mixed)
+
+
+def rotate(place, weights, angles, keep):
+    def block(j):
+        y, z = ((1, 0), (1, 1), (0, 1), (1, 1))[j] if keep else ((0, 0), (0, 1), (0, 0), (1, 0))[j]
+        return lambda p: (p[0] ^ (1 - y)) * 2 + (p[1] ^ (1 - z))
+
+    def weight(j):
+        at = block(j)
+        return pl.BlockSpec((2, 1, 128, CHEB), lambda i, p: (0, at(p), j // 2, 0))
+
+    def phase(j):
+        at = block(j)
+        return pl.BlockSpec((1, 2, 1, 2, 4, CHEB), lambda i, p: (0, 0, at(p), j // 2, 0, 0))
+
+    in_specs = [weight(j) for j in range(4)] + [phase(j) for j in range(4)]
+    in_specs.append(pl.BlockSpec((256, 256), lambda i, p: (0, 0)))
+    out_specs = [pl.BlockSpec((2, 256, CHEB), lambda i, p: (0, 0, 0))] * 2
+    out_shape = [jax.ShapeDtypeStruct((2, 256, CHEB), BF)] * 2
+    scratch = [pltpu.VMEM((4, 2, 8, CHEB), F32), pltpu.VMEM((4, 256, CHEB), BF)]
+    args = [*[weights] * 4, *[angles] * 4, in_hbm(jnp.asarray(MIX, BF))]
+    if keep:
+        in_specs += [
+            pl.BlockSpec((1, 2, 4, 4, 4, CHEB), lambda i, p: (1, 0, 0, 0, 0, 0)),
+            pl.BlockSpec((1, 2, 4, 4, 4, CHEB), lambda i, p: (2, 0, 0, 0, 0, 0)),
+            pl.BlockSpec((128, 128), lambda i, p: (0, 0)),
+        ]
+        out_specs.append(pl.BlockSpec((2, 4, 64, HALF), lambda i, p: (0, 0, 0, 0)))
+        out_shape.append(jax.ShapeDtypeStruct((2, 4, 64, HALF), BF))
+        scratch.append(pltpu.VMEM((4, 64, CHEB), F32))
+        args += [angles, angles, in_hbm(jnp.asarray(SEND_PHASE, BF))]
+    spec = pltpu.PrefetchScalarGridSpec(
+        num_scalar_prefetch=1, grid=(1,), in_specs=in_specs, out_specs=out_specs, scratch_shapes=scratch
+    )
+    return pl.pallas_call(
+        keep_kernel if keep else send_kernel,
+        grid_spec=spec,
+        out_shape=out_shape,
+        compiler_params=params(14),
+        name="rotate_kept" if keep else "rotate_sent",
+    )(place, *args)
 
 
 def add(a, b):
@@ -307,32 +304,38 @@
     )(share, in_hbm(translation), in_hbm(waves), jnp.asarray(ENTER, BF), jnp.asarray(TURN, BF), jnp.asarray(LEAVE, BF))
 
 
-def final_kernel(place, n0, n1, n2, n3, pick_ref, t_ref, out_ref, left):
-    for high in range(2):
-        held = jnp.concatenate([r[64 * high : 64 * high + 64] for r in (n0, n1, n2, n3)], axis=0)
-        value = dot(pick_ref[0], held)
-        value = jnp.concatenate([value[:128], value[128:]], axis=1)
-        left[128 * high : 128 * high + 128, :] = value.astype(BF)
-    for x2 in range(2):
-        out_ref[x2, 0] = dot(left[...], t_ref[4 * x2 + place[2]]).astype(BF)
+def final_kernel(place, n0, n1, n2, n3, pick_ref, t_ref, out_ref, left, made, sems):
+    own = place[2]
+    copies = []
+    for block in range(4):
+        for high in range(2):
+            at = 128 * block + 64 * high
+            held = jnp.concatenate([r[at : at + 64] for r in (n0, n1, n2, n3)], axis=0)
+            value = dot(pick_ref[own], held)
+            value = jnp.concatenate([value[:128], value[128:]], axis=1)
+            left[block, 128 * high : 128 * high + 128, :] = value.astype(BF)
+        for x2 in range(2):
+            made[x2, block] = dot(left[block], t_ref[4 * x2 + own]).astype(BF)
+            copies.append(
+                pltpu.make_async_copy(made.at[x2, block], out_ref.at[x2, block], sems.at[x2, block])
+            )
+            copies[-1].start()
+    for copy in copies:
+        copy.wait()
 
 
 def final(place, near, translation):
-    spec = pltpu.PrefetchScalarGridSpec(
-        num_scalar_prefetch=1,
-        grid=(4,),
-        in_specs=[pl.BlockSpec((128, HALF), lambda i, p: (i, 0))] * 4
-        + [
-            pl.BlockSpec((1, 256, 256), lambda i, p: (p[2], 0, 0)),
-            pl.BlockSpec(memory_space=pltpu.VMEM),
+    vmem = pl.BlockSpec(memory_space=pltpu.VMEM)
+    return pl.pallas_call(
+        final_kernel,
+        out_shape=jax.ShapeDtypeStruct((2, 4, 256, CHEB), BF),
+        in_specs=[pl.BlockSpec(memory_space=pltpu.SMEM)] + [vmem] * 6,
+        out_specs=pl.BlockSpec(memory_space=pl.ANY),
+        scratch_shapes=[
+            pltpu.VMEM((4, 256, CHEB), BF),
+            pltpu.VMEM((2, 4, 256, CHEB), BF),
+            pltpu.SemaphoreType.DMA((2, 4)),
         ],
-        out_specs=pl.BlockSpec((2, 1, 256, CHEB), lambda i, p: (0, i, 0, 0)),
-        scratch_shapes=[pltpu.VMEM((256, CHEB), BF)],
-    )
-    return pl.pallas_call(
-        final_kernel,
-        grid_spec=spec,
-        out_shape=jax.ShapeDtypeStruct((2, 4, 256, CHEB), BF),
         compiler_params=params(14),
         name="final",
     )(place, *near, jnp.asarray(FINAL, BF), translation)
@@ -359,8 +362,8 @@
     angles = in_hbm(angles.reshape(3, 2, 4, 4, 4, CHEB))
     send0, send1 = rotate(place, weights, angles, False)
     come0, come1 = swap(send0, "y4"), swap(send1, "z4")
-    keep0, keep1 = rotate(place, weights, angles, True)
-    phases = exchange(far_phases(angles).reshape(64, 8, HALF), ("x4", "y4", "z4", "x3", "y3", "z3"))
+    keep0, keep1, phases = rotate(place, weights, angles, True)
+    phases = exchange(phases.reshape(64, 8, HALF), ("x4", "y4", "z4", "x3", "y3", "z3"))
     again0, again1 = add(keep0[0], come0[0]), add(keep1[0], come1[0])
     phases, _, _ = lax.optimization_barrier((phases, again0, again1))
     near = four(phases.reshape(8, 64, HALF))

time: 108 us -> 106 us (0.981)
  Pallas kernels: 25.2 us -> 23 us
  waiting for transfers between devices: 19.9 us -> 21.7 us
    all_to_all x2, waiting for transfers between devices: 13.9 us -> 16.6 us  [exchange(): return lax.all_to_all(value, axes, split_axis=0, concat_axis=0, tiled=True)]
    pallas_call x4 -> x3, Pallas kernels: 11.3 us -> 9.09 us  [the longest x2 5.96 us: rotate(): pl.pallas_call(keep_kernel if keep else send_kernel, grid_spec=spec, out_...]
  transfers between devices with their start and end apart: 12 -> 12, of which waited for: 7 -> 6; matrix products, arithmetic and copies ran while one was open for 1% -> 1% of each run, Pallas kernels for 10% -> 9%
where the time goes in v4:
time: 106 us
  starting transfers between devices  38.5 us (36%)
  Pallas kernels  23 us (22%)
  waiting for transfers between devices  21.7 us (20%)
  blocking collectives  21.7 us (20%)
    all_to_all x1, blocking collectives, exchange(): return lax.all_to_all(value, axes, split_axis=0, concat_axis=0, tiled=True)  21.7 us
    ppermute x10, starting transfers between devices, swap(): return lax.ppermute(value, axis, [(0, 1), (1, 0)])  19.4 us
    all_to_all x2, starting transfers between devices, exchange(): return lax.all_to_all(value, axes, split_axis=0, concat_axis=0, tiled=True)  19.1 us
    all_to_all x2, waiting for transfers between devices, exchange(): return lax.all_to_all(value, axes, split_axis=0, concat_axis=0, tiled=True)  16.6 us
    pallas_call x1, Pallas kernels, levels(): pl.pallas_call(levels_kernel, grid=(4,), out_shape=jax.ShapeDtypeStruct((...  7.43 us
    pallas_call x2, Pallas kernels, rotate(): pl.pallas_call(keep_kernel if keep else send_kernel, grid_spec=spec, out_...  5.96 us
    pallas_call x1, Pallas kernels, trig(): pl.pallas_call(trig_kernel, grid_spec=spec, out_shape=pltpu.HBM((16, 2, 6...  5.42 us
    ppermute x10, waiting for transfers between devices, swap(): return lax.ppermute(value, axis, [(0, 1), (1, 0)])  5.09 us
  transfers between devices with their start and end apart: 12, of which 6 were waited for; matrix products, arithmetic and copies ran while one was open for 1% of the time, Pallas kernels for 9%

profile of v4, /device:TPU:1, one launch (start us, length us, event | category | flops | bytes accessed | tf_op | source)
XLA Modules:
  0.0 106.1 jit_solution(6809286788687957093)
XLA Ops:
  0.0 0.1 pad_add_fusion.place
  0.1 2.7 %rotate_sent.1 = (bf16[2,256,512]{2,1,0:T(8,128)(2,1)S(1)}, bf16[2,256,512]{2,1,0:T(8,128)(2,1)S(1)}) custom-call(s32[3]{0:T(128)S(1)} %pad_add_fusion.place, bf16[2,4,256,512]{3,2,1,0:T(8,128)(2,1)} %bitcast.25, bf16[2,4,256,512]{3,2,1,0:T(8,128)(2,1)} %bitcast.26, bf16[2,4,256,512]{3,2,1,0:T(8,128)(2,1)} %bitcast.27, bf16[2,4,256,512]{3,2,1,0:T(8,128)(2,1)} %bitcast.28, ...), custom_call_target="tpu_custom_call" | custom-call | tf_op jit(solution)/shard_map/rotate_sent/pallas_call | solution.py:152
  2.8 3.8 %collective-permute-start.2 = (bf16[2,256,512]{2,1,0:T(8,128)(2,1)S(1)}, bf16[2,256,512]{2,1,0:T(8,128)(2,1)S(1)}, u32[]{:S(2)}, u32[]{:S(2)}) collective-permute-start(bf16[2,256,512]{2,1,0:T(8,128)(2,1)S(1)} %get-tuple-element.14), channel_id=1, source_target_pairs={{0,4},{4,0},{1,5},{5,1},{2,6},{6,2},{3,7},{7,3},{8,12},{12,8},{9,1... | collective-permute-start | bytes 1572872 | tf_op jit(solution)/shard_map/ppermute | solution.py:345
  6.6 2.8 %collective-permute-start = (bf16[2,256,512]{2,1,0:T(8,128)(2,1)S(1)}, bf16[2,256,512]{2,1,0:T(8,128)(2,1)S(1)}, u32[]{:S(2)}, u32[]{:S(2)}) collective-permute-start(bf16[2,256,512]{2,1,0:T(8,128)(2,1)S(1)} %get-tuple-element.12), channel_id=1, source_target_pairs={{0,32},{32,0},{1,33},{33,1},{2,34},{34,2},{3,35},{35,3},{4,36},{36... | collective-permute-start | bytes 1572872 | tf_op jit(solution)/shard_map/ppermute | solution.py:345
  9.4 3.3 %rotate_kept.1 = (bf16[2,256,512]{2,1,0:T(8,128)(2,1)S(1)}, bf16[2,256,512]{2,1,0:T(8,128)(2,1)S(1)}, bf16[2,4,64,256]{3,2,1,0:T(8,128)(2,1)}) custom-call(s32[3]{0:T(128)S(1)} %pad_add_fusion.place, bf16[2,4,256,512]{3,2,1,0:T(8,128)(2,1)} %bitcast.29, bf16[2,4,256,512]{3,2,1,0:T(8,128)(2,1)} %bitcast.30, bf16[2,4,256,512]{3,2,1,0:T(8,128)(2,1)} %bitcast.31, ...), custom_call_target="tpu_custom_call" | custom-call | tf_op jit(solution)/shard_map/rotate_kept/pallas_call | solution.py:152
  12.6 10.3 %all-to-all-start.1 = ((bf16[64,8,256]{2,1,0:T(8,128)(2,1)}), bf16[64,8,256]{2,1,0:T(8,128)(2,1)S(1)}, u32[]{:S(2)}, u32[]{:S(2)}) async-start(bf16[64,8,256]{2,1,0:T(8,128)(2,1)} %bitcast.9), calls=%async_computation.1 | async-start | bytes 524288 | tf_op jit(solution)/shard_map/all_to_all | solution.py:354
  22.9 0.8 fusion.1
  23.7 2.5 %collective-permute-start.3 = (bf16[256,512]{1,0:T(8,128)(2,1)}, bf16[256,512]{1,0:T(8,128)(2,1)S(1)}, u32[]{:S(2)}, u32[]{:S(2)}) collective-permute-start(bf16[256,512]{1,0:T(8,128)(2,1)} %fusion.1), channel_id=1, source_target_pairs={{0,32},{32,0},{1,33},{33,1},{2,34},{34,2},{3,35},{35,3},{4,36},{36... | collective-permute-start | bytes 786440 | tf_op jit(solution)/shard_map/ppermute | solution.py:345
  26.2 0.1 fusion
  26.3 2.8 %collective-permute-start.1 = (bf16[256,512]{1,0:T(8,128)(2,1)S(1)}, bf16[256,512]{1,0:T(8,128)(2,1)S(1)}, u32[]{:S(2)}, u32[]{:S(2)}) collective-permute-start(bf16[256,512]{1,0:T(8,128)(2,1)S(1)} %fusion), channel_id=1, source_target_pairs={{0,4},{4,0},{1,5},{5,1},{2,6},{6,2},{3,7},{7,3},{8,12},{12,8},{9,1... | collective-permute-start | bytes 786440 | tf_op jit(solution)/shard_map/ppermute | solution.py:345
  29.1 7.2 %all-to-all-done.1 = bf16[64,8,256]{2,1,0:T(8,128)(2,1)S(1)} async-done(((bf16[64,8,256]{2,1,0:T(8,128)(2,1)}), bf16[64,8,256]{2,1,0:T(8,128)(2,1)S(1)}, u32[]{:S(2)}, u32[]{:S(2)}) %all-to-all-start.1) | async-done | bytes 262176 | tf_op jit(solution)/shard_map/all_to_all | solution.py:354
  36.2 0.6 collective-permute-start.5
  36.8 1.0 sums.1
  37.9 8.8 %all-to-all-start = ((bf16[64,8,512]{2,1,0:T(8,128)(2,1)}), bf16[64,8,512]{2,1,0:T(8,128)(2,1)S(1)}, u32[]{:S(2)}, u32[]{:S(2)}) async-start(bf16[64,8,512]{2,1,0:T(8,128)(2,1)} %bitcast.7), calls=%async_computation | async-start | bytes 1048576 | tf_op jit(solution)/shard_map/all_to_all | solution.py:354
  46.7 0.0 copy-start.2
  46.7 0.0 copy-start.3
  46.7 0.0 copy-start.4
  46.7 0.5 collective-permute-start.4
  47.3 0.1 collective-permute-start.6
  47.4 1.1 collective-permute-done.4.refs_1_.refs_5_
  48.4 0.4 collective-permute-done.6.refs_3_.refs_7_
  48.8 5.4 %trig.1.trig_ref = f32[16,2,64,512]{3,2,1,0:T(8,128)} custom-call(s32[3]{0:T(128)S(1)} %pad_add_fusion.place, bf16[8,64,256]{2,1,0:T(8,128)(2,1)S(1)} %bitcast.23, bf16[8,64,256]{2,1,0:T(8,128)(2,1)S(1)} %collective-permute-done.4.refs_1_.refs_5_, bf16[8,64,256]{2,1,0:T(8,128)(2,1)S(1)} %collective-permute-done.5.refs_2_.refs_6_, ...), custom_call_target="tpu_custom_call" | custom-call | flops 7000000000 | bytes 1000000 | tf_op jit(solution)/shard_map/trig/pallas_call | solution.py:218
  54.2 9.4 %all-to-all-done = bf16[64,8,512]{2,1,0:T(8,128)(2,1)S(1)} async-done(((bf16[64,8,512]{2,1,0:T(8,128)(2,1)}), bf16[64,8,512]{2,1,0:T(8,128)(2,1)S(1)}, u32[]{:S(2)}, u32[]{:S(2)}) %all-to-all-start) | async-done | bytes 524320 | tf_op jit(solution)/shard_map/all_to_all | solution.py:354
  63.7 0.0 copy-start
  63.7 0.0 copy-start.1
  63.7 7.4 %levels.1 = bf16[8,8,8,256]{3,2,1,0:T(8,128)(2,1)S(1)} custom-call(bf16[2,256,512]{2,1,0:T(8,128)(2,1)S(1)} %bitcast.16, bf16[8,512,512]{2,1,0:T(8,128)(2,1)} %t_ref.3, f32[16,2,64,512]{3,2,1,0:T(8,128)} %trig.1.trig_ref, bf16[256,256]{1,0:T(8,128)(2,1)S(1)} %copy-done.3, bf16[256,256]{1,0:T(8,128)(2,1)S(1)} %copy-done.2, bf16[64,64]{1,0:T(8,128)(2,1)S(1)} %copy-done.4), custom_call_target="tpu_custom_call" | custom-call | tf_op jit(solution)/shard_map/levels/pallas_call | solution.py:283
  71.2 21.7 %all_to_all.15 = bf16[64,8,256]{2,1,0:T(8,128)(2,1)S(1)} all-to-all(bf16[64,8,256]{2,1,0:T(8,128)(2,1)S(1)} %bitcast.20), channel_id=1, replica_groups=mesh['x4'=2,'x3'=2,'y4'=2,'y3'=2,'y2'=2,'z4'=2,'z3'=2,'z2'=2] {'y4','z4'..., dimensions={0} | all-to-all | bytes 524288 | tf_op jit(solution)/shard_map/all_to_all | solution.py:354
  92.9 3.3 %collective-permute-start.7 = (bf16[512,256]{1,0:T(8,128)(2,1)S(1)}, bf16[512,256]{1,0:T(8,128)(2,1)S(1)}, u32[]{:S(2)}, u32[]{:S(2)}) collective-permute-start(bf16[512,256]{1,0:T(8,128)(2,1)S(1)} %bitcast.18), channel_id=1, source_target_pairs={{0,1},{1,0},{2,3},{3,2},{4,5},{5,4},{6,7},{7,6},{8,9},{9,8},{10,11... | collective-permute-start | bytes 786440 | tf_op jit(solution)/shard_map/ppermute | solution.py:345
  96.2 2.5 %collective-permute-done.8.n2 = bf16[512,256]{1,0:T(8,128)(2,1)S(1)} collective-permute-done((bf16[512,256]{1,0:T(8,128)(2,1)S(1)}, bf16[512,256]{1,0:T(8,128)(2,1)S(1)}, u32[]{:S(2)}, u32[]{:S(2)}) %collective-permute-start.8) | collective-permute-done | bytes 262176 | tf_op jit(solution)/shard_map/ppermute | solution.py:345
  98.7 2.9 %collective-permute-start.9 = (bf16[512,256]{1,0:T(8,128)(2,1)S(1)}, bf16[512,256]{1,0:T(8,128)(2,1)S(1)}, u32[]{:S(2)}, u32[]{:S(2)}) collective-permute-start(bf16[512,256]{1,0:T(8,128)(2,1)S(1)} %collective-permute-done.8.n2), channel_id=1, source_target_pairs={{0,1},{1,0},{2,3},{3,2},{4,5},{5,4},{6,7},{7,6},{8,9},{9,8},{10,11... | collective-permute-start | bytes 786440 | tf_op jit(solution)/shard_map/ppermute | solution.py:345
  101.6 1.2 %collective-permute-done.9.n3 = bf16[512,256]{1,0:T(8,128)(2,1)S(1)} collective-permute-done((bf16[512,256]{1,0:T(8,128)(2,1)S(1)}, bf16[512,256]{1,0:T(8,128)(2,1)S(1)}, u32[]{:S(2)}, u32[]{:S(2)}) %collective-permute-start.9) | collective-permute-done | bytes 262176 | tf_op jit(solution)/shard_map/ppermute | solution.py:345
  102.8 3.1 %final.1 = bf16[2,4,256,512]{3,2,1,0:T(8,128)(2,1)} custom-call(s32[3]{0:T(128)S(1)} %pad_add_fusion.place, bf16[512,256]{1,0:T(8,128)(2,1)S(1)} %bitcast.19, bf16[512,256]{1,0:T(8,128)(2,1)S(1)} %collective-permute-done.7.n1, bf16[512,256]{1,0:T(8,128)(2,1)S(1)} %collective-permute-done.8.n2, bf16[512,256]{1,0:T(8,128)(2,1)S(1)} %collective-permute-done.9.n3, ...), custom_call_target="tpu_custom_call" | custom-call | tf_op jit(solution)/shard_map/final/pallas_call | solution.py:329
  (12 shorter events, 0.0 us)
Async XLA Ops:
  2.8 20.1 %collective-permute-start.2 = (bf16[2,256,512]{2,1,0:T(8,128)(2,1)S(1)}, bf16[2,256,512]{2,1,0:T(8,128)(2,1)S(1)}, u32[]{:S(2)}, u32[]{:S(2)}) collective-permute-start(bf16[2,256,512]{2,1,0:T(8,128)(2,1)S(1)} %get-tuple-element.14), channel_id=1, source_target_pairs={{0,4},{4,0},{1,5},{5,1},{2,6},{6,2},{3,7},{7,3},{8,12},{12,8},{9,1... | collective-permute-start | bytes 1572872 | tf_op jit(solution)/shard_map/ppermute | solution.py:345
  6.6 19.6 %collective-permute-start = (bf16[2,256,512]{2,1,0:T(8,128)(2,1)S(1)}, bf16[2,256,512]{2,1,0:T(8,128)(2,1)S(1)}, u32[]{:S(2)}, u32[]{:S(2)}) collective-permute-start(bf16[2,256,512]{2,1,0:T(8,128)(2,1)S(1)} %get-tuple-element.12), channel_id=1, source_target_pairs={{0,32},{32,0},{1,33},{33,1},{2,34},{34,2},{3,35},{35,3},{4,36},{36... | collective-permute-start | bytes 1572872 | tf_op jit(solution)/shard_map/ppermute | solution.py:345
  12.6 23.6 %all-to-all-start.1 = ((bf16[64,8,256]{2,1,0:T(8,128)(2,1)}), bf16[64,8,256]{2,1,0:T(8,128)(2,1)S(1)}, u32[]{:S(2)}, u32[]{:S(2)}) async-start(bf16[64,8,256]{2,1,0:T(8,128)(2,1)} %bitcast.9), calls=%async_computation.1 | async-start | bytes 524288 | tf_op jit(solution)/shard_map/all_to_all | solution.py:354
  23.7 13.2 %collective-permute-start.3 = (bf16[256,512]{1,0:T(8,128)(2,1)}, bf16[256,512]{1,0:T(8,128)(2,1)S(1)}, u32[]{:S(2)}, u32[]{:S(2)}) collective-permute-start(bf16[256,512]{1,0:T(8,128)(2,1)} %fusion.1), channel_id=1, source_target_pairs={{0,32},{32,0},{1,33},{33,1},{2,34},{34,2},{3,35},{35,3},{4,36},{36... | collective-permute-start | bytes 786440 | tf_op jit(solution)/shard_map/ppermute | solution.py:345
  26.3 10.6 %collective-permute-start.1 = (bf16[256,512]{1,0:T(8,128)(2,1)S(1)}, bf16[256,512]{1,0:T(8,128)(2,1)S(1)}, u32[]{:S(2)}, u32[]{:S(2)}) collective-permute-start(bf16[256,512]{1,0:T(8,128)(2,1)S(1)} %fusion), channel_id=1, source_target_pairs={{0,4},{4,0},{1,5},{5,1},{2,6},{6,2},{3,7},{7,3},{8,12},{12,8},{9,1... | collective-permute-start | bytes 786440 | tf_op jit(solution)/shard_map/ppermute | solution.py:345
  36.2 11.0 %collective-permute-start.5 = (bf16[8,64,256]{2,1,0:T(8,128)(2,1)S(1)}, bf16[8,64,256]{2,1,0:T(8,128)(2,1)S(1)}, u32[]{:S(2)}, u32[]{:S(2)}) collective-permute-start(bf16[8,64,256]{2,1,0:T(8,128)(2,1)S(1)} %bitcast.21), channel_id=1, source_target_pairs={{0,8},{8,0},{1,9},{9,1},{2,10},{10,2},{3,11},{11,3},{4,12},{12,4},... | collective-permute-start | bytes 786440 | tf_op jit(solution)/shard_map/ppermute | solution.py:345
  37.9 25.8 %all-to-all-start = ((bf16[64,8,512]{2,1,0:T(8,128)(2,1)}), bf16[64,8,512]{2,1,0:T(8,128)(2,1)S(1)}, u32[]{:S(2)}, u32[]{:S(2)}) async-start(bf16[64,8,512]{2,1,0:T(8,128)(2,1)} %bitcast.7), calls=%async_computation | async-start | bytes 1048576 | tf_op jit(solution)/shard_map/all_to_all | solution.py:354
  46.7 17.0 %copy-start.2 = (bf16[256,256]{1,0:T(8,128)(2,1)S(1)}, bf16[256,256]{1,0:T(8,128)(2,1)}, u32[]{:S(2)}) copy-start(bf16[256,256]{1,0:T(8,128)(2,1)} %constant.39.clone.turn_ref) | copy-start | bytes 393220
  46.7 17.0 %copy-start.3 = (bf16[256,256]{1,0:T(8,128)(2,1)S(1)}, bf16[256,256]{1,0:T(8,128)(2,1)}, u32[]{:S(2)}) copy-start(bf16[256,256]{1,0:T(8,128)(2,1)} %constant.38.clone.enter_ref) | copy-start | bytes 393220
  46.7 17.0 %copy-start.4 = (bf16[64,64]{1,0:T(8,128)(2,1)S(1)}, bf16[64,64]{1,0:T(8,128)(2,1)}, u32[]{:S(2)}) copy-start(bf16[64,64]{1,0:T(8,128)(2,1)} %constant.40.clone.leave_ref) | copy-start | bytes 24580
  46.7 1.7 %collective-permute-start.4 = (bf16[8,64,256]{2,1,0:T(8,128)(2,1)S(1)}, bf16[8,64,256]{2,1,0:T(8,128)(2,1)S(1)}, u32[]{:S(2)}, u32[]{:S(2)}) collective-permute-start(bf16[8,64,256]{2,1,0:T(8,128)(2,1)S(1)} %bitcast.22), channel_id=1, source_target_pairs={{0,1},{1,0},{2,3},{3,2},{4,5},{5,4},{6,7},{7,6},{8,9},{9,8},{10,11... | collective-permute-start | bytes 786440 | tf_op jit(solution)/shard_map/ppermute | solution.py:345
  47.3 1.5 %collective-permute-start.6 = (bf16[8,64,256]{2,1,0:T(8,128)(2,1)S(1)}, bf16[8,64,256]{2,1,0:T(8,128)(2,1)S(1)}, u32[]{:S(2)}, u32[]{:S(2)}) collective-permute-start(bf16[8,64,256]{2,1,0:T(8,128)(2,1)S(1)} %collective-permute-done.5.refs_2_.refs_6_), channel_id=1, source_target_pairs={{0,1},{1,0},{2,3},{3,2},{4,5},{5,4},{6,7},{7,6},{8,9},{9,8},{10,11... | collective-permute-start | bytes 786440 | tf_op jit(solution)/shard_map/ppermute | solution.py:345
  63.7 39.1 %copy-start = (bf16[8,512,512]{2,1,0:T(8,128)(2,1)S(1)}, bf16[8,512,512]{2,1,0:T(8,128)(2,1)}, u32[]{:S(2)}) copy-start(bf16[8,512,512]{2,1,0:T(8,128)(2,1)} %t_ref.3) | copy-start | bytes 12582916
  63.7 39.1 %copy-start.1 = (bf16[4,256,256]{2,1,0:T(8,128)(2,1)S(1)}, bf16[4,256,256]{2,1,0:T(8,128)(2,1)}, u32[]{:S(2)}) copy-start(bf16[4,256,256]{2,1,0:T(8,128)(2,1)} %constant.41.clone.pick_ref) | copy-start | bytes 1572868
  92.9 5.8 %collective-permute-start.8 = (bf16[512,256]{1,0:T(8,128)(2,1)S(1)}, bf16[512,256]{1,0:T(8,128)(2,1)S(1)}, u32[]{:S(2)}, u32[]{:S(2)}) collective-permute-start(bf16[512,256]{1,0:T(8,128)(2,1)S(1)} %bitcast.17), channel_id=1, source_target_pairs={{0,8},{8,0},{1,9},{9,1},{2,10},{10,2},{3,11},{11,3},{4,12},{12,4},... | collective-permute-start | bytes 786440 | tf_op jit(solution)/shard_map/ppermute | solution.py:345
  92.9 8.7 %collective-permute-start.7 = (bf16[512,256]{1,0:T(8,128)(2,1)S(1)}, bf16[512,256]{1,0:T(8,128)(2,1)S(1)}, u32[]{:S(2)}, u32[]{:S(2)}) collective-permute-start(bf16[512,256]{1,0:T(8,128)(2,1)S(1)} %bitcast.18), channel_id=1, source_target_pairs={{0,1},{1,0},{2,3},{3,2},{4,5},{5,4},{6,7},{7,6},{8,9},{9,8},{10,11... | collective-permute-start | bytes 786440 | tf_op jit(solution)/shard_map/ppermute | solution.py:345
  98.7 4.1 %collective-permute-start.9 = (bf16[512,256]{1,0:T(8,128)(2,1)S(1)}, bf16[512,256]{1,0:T(8,128)(2,1)S(1)}, u32[]{:S(2)}, u32[]{:S(2)}) collective-permute-start(bf16[512,256]{1,0:T(8,128)(2,1)S(1)} %collective-permute-done.8.n2), channel_id=1, source_target_pairs={{0,1},{1,0},{2,3},{3,2},{4,5},{5,4},{6,7},{7,6},{8,9},{9,8},{10,11... | collective-permute-start | bytes 786440 | tf_op jit(solution)/shard_map/ppermute | solution.py:345

commit v5 on v4

--- a/solution.py
+++ b/solution.py
@@ -81,81 +81,86 @@
     return pltpu.CompilerParams(vmem_limit_bytes=mebibytes * 1024 * 1024)
 
 
-def rotate_blocks(blocks, angles, mix_ref, first, second, angle, mixed):
-    for j in range(4):
+def rotate_kernel(place, w_hbm, a_hbm, mix_hbm, order_hbm, send0, send1, keep0, keep1, phases,
+                  w_ref, a_ref, mix_ref, order_ref, waves, mixed, far, w_sems, sems):
+    blocks = []
+    for z, y, high in ((0, 0, 0), (1, 0, 0), (0, 0, 1), (0, 1, 1), (0, 1, 0), (1, 1, 0), (1, 0, 1), (1, 1, 1)):
+        blocks.append(((place[0] ^ (1 - y)) * 2 + (place[1] ^ (1 - z)), high))
+    small = [pltpu.make_async_copy(a_hbm.at[0], a_ref.at[0], sems.at[0])]
+    small.append(pltpu.make_async_copy(mix_hbm, mix_ref, sems.at[1]))
+    small.append(pltpu.make_async_copy(a_hbm.at[1:3], a_ref.at[1:3], sems.at[2]))
+    small.append(pltpu.make_async_copy(order_hbm, order_ref, sems.at[3]))
+    large = [
+        pltpu.make_async_copy(w_hbm.at[:, at, 128 * high : 128 * high + 128], w_ref.at[j], w_sems.at[j])
+        for j, (at, high) in enumerate(blocks)
+    ]
+    small[0].start()
+    large[0].start()
+    small[1].start()
+    for copy in large[1:]:
+        copy.start()
+    small[2].start()
+    small[3].start()
+    small[0].wait()
+    small[2].wait()
+    small[3].wait()
+    for j, (at, high) in enumerate(blocks):
         for x2 in range(2):
             for y in range(2):
-                angle[j, x2, 4 * y : 4 * y + 4, :] = angles[j][0, x2, 0, y]
-            sine, cosine = sin_cos(angle[j, x2])
+                waves[j, x2, 0, 4 * y : 4 * y + 4, :] = a_ref[0, x2, at, 2 * high + y]
+            sine, cosine = sin_cos(waves[j, x2, 0])
+            waves[j, x2, 0] = sine
+            waves[j, x2, 1] = cosine
+    for j, (at, high) in enumerate(blocks):
+        if j == 0:
+            for copy in large:
+                copy.wait()
+            small[1].wait()
+        for x2 in range(2):
+            sine, cosine = waves[j, x2, 0], waves[j, x2, 1]
             for low in range(8):
-                block = blocks[j][x2, 0, 16 * low : 16 * low + 16, :].astype(F32)
+                block = w_ref[j, x2, 16 * low : 16 * low + 16, :].astype(F32)
                 re, im = block[:8], block[8:]
-                s, c = sine[low : low + 1], cosine[low : low + 1]
+                s = sine[low : low + 1]
+                c = cosine[low : low + 1]
                 turned = jnp.concatenate([re * c - im * s, re * s + im * c], axis=0)
-                at = 128 * x2 + 16 * low
-                mixed[j, at : at + 16, :] = turned.astype(BF)
-        (first, second)[j // 2][j % 2] = dot(mix_ref[...], mixed[j]).astype(BF)
-
-
-def send_kernel(place, *refs):
-    rotate_blocks(refs[0:4], refs[4:8], *refs[8:])
-
-
-def keep_kernel(place, *refs):
-    mix_ref, a1_ref, a2_ref, order_ref, first, second, phases, angle, mixed, far = refs[8:]
+                row = 128 * x2 + 16 * low
+                mixed[j, row : row + 16, :] = turned.astype(BF)
+        (send0, send1, keep0, keep1)[j // 2][j % 2] = dot(mix_ref[...], mixed[j]).astype(BF)
     for block in range(4):
-        for level, ref in enumerate((a1_ref, a2_ref)):
+        for level in range(2):
             for x2 in range(2):
                 for y in range(4):
-                    at = 32 * level + 16 * x2 + 4 * y
-                    far[block, at : at + 4, :] = ref[0, x2, block, y]
+                    row = 32 * level + 16 * x2 + 4 * y
+                    far[block, row : row + 4, :] = a_ref[1 + level, x2, block, y]
         value = far[block].astype(BF)
         value = jnp.concatenate([value[:, :HALF], value[:, HALF:]], axis=0)
         value = dot(order_ref[...], value).astype(BF)
         for high in range(2):
             phases[high, block] = value[64 * high : 64 * high + 64]
-    rotate_blocks(refs[0:4], refs[4:8], mix_ref, first, second, angle, mixed)
-
-
-def rotate(place, weights, angles, keep):
-    def block(j):
-        y, z = ((1, 0), (1, 1), (0, 1), (1, 1))[j] if keep else ((0, 0), (0, 1), (0, 0), (1, 0))[j]
-        return lambda p: (p[0] ^ (1 - y)) * 2 + (p[1] ^ (1 - z))
-
-    def weight(j):
-        at = block(j)
-        return pl.BlockSpec((2, 1, 128, CHEB), lambda i, p: (0, at(p), j // 2, 0))
-
-    def phase(j):
-        at = block(j)
-        return pl.BlockSpec((1, 2, 1, 2, 4, CHEB), lambda i, p: (0, 0, at(p), j // 2, 0, 0))
-
-    in_specs = [weight(j) for j in range(4)] + [phase(j) for j in range(4)]
-    in_specs.append(pl.BlockSpec((256, 256), lambda i, p: (0, 0)))
-    out_specs = [pl.BlockSpec((2, 256, CHEB), lambda i, p: (0, 0, 0))] * 2
-    out_shape = [jax.ShapeDtypeStruct((2, 256, CHEB), BF)] * 2
-    scratch = [pltpu.VMEM((4, 2, 8, CHEB), F32), pltpu.VMEM((4, 256, CHEB), BF)]
-    args = [*[weights] * 4, *[angles] * 4, in_hbm(jnp.asarray(MIX, BF))]
-    if keep:
-        in_specs += [
-            pl.BlockSpec((1, 2, 4, 4, 4, CHEB), lambda i, p: (1, 0, 0, 0, 0, 0)),
-            pl.BlockSpec((1, 2, 4, 4, 4, CHEB), lambda i, p: (2, 0, 0, 0, 0, 0)),
-            pl.BlockSpec((128, 128), lambda i, p: (0, 0)),
-        ]
-        out_specs.append(pl.BlockSpec((2, 4, 64, HALF), lambda i, p: (0, 0, 0, 0)))
-        out_shape.append(jax.ShapeDtypeStruct((2, 4, 64, HALF), BF))
-        scratch.append(pltpu.VMEM((4, 64, CHEB), F32))
-        args += [angles, angles, in_hbm(jnp.asarray(SEND_PHASE, BF))]
-    spec = pltpu.PrefetchScalarGridSpec(
-        num_scalar_prefetch=1, grid=(1,), in_specs=in_specs, out_specs=out_specs, scratch_shapes=scratch
-    )
-    return pl.pallas_call(
-        keep_kernel if keep else send_kernel,
-        grid_spec=spec,
-        out_shape=out_shape,
-        compiler_params=params(14),
-        name="rotate_kept" if keep else "rotate_sent",
-    )(place, *args)
+
+
+def rotate(place, weights, angles):
+    piece = jax.ShapeDtypeStruct((2, 256, CHEB), BF)
+    return pl.pallas_call(
+        rotate_kernel,
+        out_shape=[piece] * 4 + [jax.ShapeDtypeStruct((2, 4, 64, HALF), BF)],
+        in_specs=[pl.BlockSpec(memory_space=pltpu.SMEM)] + [pl.BlockSpec(memory_space=pl.ANY)] * 4,
+        out_specs=[pl.BlockSpec(memory_space=pltpu.VMEM)] * 5,
+        scratch_shapes=[
+            pltpu.VMEM((8, 2, 128, CHEB), BF),
+            pltpu.VMEM((3, 2, 4, 4, 4, CHEB), F32),
+            pltpu.VMEM((256, 256), BF),
+            pltpu.VMEM((128, 128), BF),
+            pltpu.VMEM((8, 2, 2, 8, CHEB), F32),
+            pltpu.VMEM((8, 256, CHEB), BF),
+            pltpu.VMEM((4, 64, CHEB), F32),
+            pltpu.SemaphoreType.DMA((8,)),
+            pltpu.SemaphoreType.DMA((4,)),
+        ],
+        compiler_params=params(16),
+        name="rotate",
+    )(place, weights, angles, in_hbm(jnp.asarray(MIX, BF)), in_hbm(jnp.asarray(SEND_PHASE, BF)))
 
 
 def add(a, b):
@@ -360,9 +365,8 @@
     shape = weights.shape
     weights = in_hbm(weights.reshape(2, 4, 256, CHEB))
     angles = in_hbm(angles.reshape(3, 2, 4, 4, 4, CHEB))
-    send0, send1 = rotate(place, weights, angles, False)
+    send0, send1, keep0, keep1, phases = rotate(place, weights, angles)
     come0, come1 = swap(send0, "y4"), swap(send1, "z4")
-    keep0, keep1, phases = rotate(place, weights, angles, True)
     phases = exchange(phases.reshape(64, 8, HALF), ("x4", "y4", "z4", "x3", "y3", "z3"))
     again0, again1 = add(keep0[0], come0[0]), add(keep1[0], come1[0])
     phases, _, _ = lax.optimization_barrier((phases, again0, again1))

time: 106 us -> 105 us (level)
  Pallas kernels: 23 us -> 21.4 us
    pallas_call x2 -> x1, Pallas kernels: 5.96 us -> 4.43 us  [rotate(): pl.pallas_call(rotate_kernel, out_shape=[piece] * 4 + [jax.ShapeDtypeStru...]
  transfers between devices with their start and end apart: 12 -> 12, of which waited for: 6 -> 6; matrix products, arithmetic and copies ran while one was open for 1% -> 1% of each run, Pallas kernels for 9% -> 6%
where the time goes in v5:
time: 105 us
  starting transfers between devices  38.3 us (36%)
  blocking collectives  22.1 us (21%)
  waiting for transfers between devices  21.7 us (21%)
  Pallas kernels  21.4 us (20%)
    all_to_all x1, blocking collectives, exchange(): return lax.all_to_all(value, axes, split_axis=0, concat_axis=0, tiled=True)  22.1 us
    ppermute x10, starting transfers between devices, swap(): return lax.ppermute(value, axis, [(0, 1), (1, 0)])  19.4 us
    all_to_all x2, starting transfers between devices, exchange(): return lax.all_to_all(value, axes, split_axis=0, concat_axis=0, tiled=True)  18.9 us
    all_to_all x2, waiting for transfers between devices, exchange(): return lax.all_to_all(value, axes, split_axis=0, concat_axis=0, tiled=True)  16.6 us
    pallas_call x1, Pallas kernels, levels(): pl.pallas_call(levels_kernel, grid=(4,), out_shape=jax.ShapeDtypeStruct((...  7.43 us
    pallas_call x1, Pallas kernels, trig(): pl.pallas_call(trig_kernel, grid_spec=spec, out_shape=pltpu.HBM((16, 2, 6...  5.41 us
    ppermute x10, waiting for transfers between devices, swap(): return lax.ppermute(value, axis, [(0, 1), (1, 0)])  5.09 us
    pallas_call x1, Pallas kernels, rotate(): pl.pallas_call(rotate_kernel, out_shape=[piece] * 4 + [jax.ShapeDtypeStru...  4.43 us
  transfers between devices with their start and end apart: 12, of which 6 were waited for; matrix products, arithmetic and copies ran while one was open for 1% of the time, Pallas kernels for 6%

profile of v5, /device:TPU:1, one launch (start us, length us, event | category | flops | bytes accessed | tf_op | source)
XLA Modules:
  0.0 104.6 jit_solution(13098372136403792943)
XLA Ops:
  0.0 0.1 pad_add_fusion.place
  0.1 4.4 %rotate.1 = (bf16[2,256,512]{2,1,0:T(8,128)(2,1)S(1)}, bf16[2,256,512]{2,1,0:T(8,128)(2,1)S(1)}, bf16[2,256,512]{2,1,0:T(8,128)(2,1)S(1)}, bf16[2,256,512]{2,1,0:T(8,128)(2,1)S(1)}, bf16[2,4,64,256]{3,2,1,0:T(8,128)(2,1)}) custom-call(s32[3]{0:T(128)S(1)} %pad_add_fusion.place, bf16[2,4,256,512]{3,2,1,0:T(8,128)(2,1)} %bitcast.25, ...), custom_call_target="tpu_custom_call" | custom-call | tf_op jit(solution)/shard_map/rotate/pallas_call | solution.py:145
  4.5 3.7 %collective-permute-start = (bf16[2,256,512]{2,1,0:T(8,128)(2,1)S(1)}, bf16[2,256,512]{2,1,0:T(8,128)(2,1)S(1)}, u32[]{:S(2)}, u32[]{:S(2)}) collective-permute-start(bf16[2,256,512]{2,1,0:T(8,128)(2,1)S(1)} %get-tuple-element.12), channel_id=1, source_target_pairs={{0,32},{32,0},{1,33},{33,1},{2,34},{34,2},{3,35},{35,3},{4,36},{36... | collective-permute-start | bytes 1572872 | tf_op jit(solution)/shard_map/ppermute | solution.py:350
  8.2 2.9 %collective-permute-start.2 = (bf16[2,256,512]{2,1,0:T(8,128)(2,1)S(1)}, bf16[2,256,512]{2,1,0:T(8,128)(2,1)S(1)}, u32[]{:S(2)}, u32[]{:S(2)}) collective-permute-start(bf16[2,256,512]{2,1,0:T(8,128)(2,1)S(1)} %get-tuple-element.14), channel_id=1, source_target_pairs={{0,4},{4,0},{1,5},{5,1},{2,6},{6,2},{3,7},{7,3},{8,12},{12,8},{9,1... | collective-permute-start | bytes 1572872 | tf_op jit(solution)/shard_map/ppermute | solution.py:350
  11.1 10.3 %all-to-all-start.1 = ((bf16[64,8,256]{2,1,0:T(8,128)(2,1)}), bf16[64,8,256]{2,1,0:T(8,128)(2,1)S(1)}, u32[]{:S(2)}, u32[]{:S(2)}) async-start(bf16[64,8,256]{2,1,0:T(8,128)(2,1)} %bitcast.9), calls=%async_computation.1 | async-start | bytes 524288 | tf_op jit(solution)/shard_map/all_to_all | solution.py:359
  21.4 0.0 collective-permute-done.come0
  21.4 0.8 fusion
  22.1 2.5 %collective-permute-start.1 = (bf16[256,512]{1,0:T(8,128)(2,1)}, bf16[256,512]{1,0:T(8,128)(2,1)S(1)}, u32[]{:S(2)}, u32[]{:S(2)}) collective-permute-start(bf16[256,512]{1,0:T(8,128)(2,1)} %fusion), channel_id=1, source_target_pairs={{0,4},{4,0},{1,5},{5,1},{2,6},{6,2},{3,7},{7,3},{8,12},{12,8},{9,1... | collective-permute-start | bytes 786440 | tf_op jit(solution)/shard_map/ppermute | solution.py:350
  24.6 0.1 fusion.1
  24.7 2.8 %collective-permute-start.3 = (bf16[256,512]{1,0:T(8,128)(2,1)S(1)}, bf16[256,512]{1,0:T(8,128)(2,1)S(1)}, u32[]{:S(2)}, u32[]{:S(2)}) collective-permute-start(bf16[256,512]{1,0:T(8,128)(2,1)S(1)} %fusion.1), channel_id=1, source_target_pairs={{0,32},{32,0},{1,33},{33,1},{2,34},{34,2},{3,35},{35,3},{4,36},{36... | collective-permute-start | bytes 786440 | tf_op jit(solution)/shard_map/ppermute | solution.py:350
  27.5 7.2 %all-to-all-done.1 = bf16[64,8,256]{2,1,0:T(8,128)(2,1)S(1)} async-done(((bf16[64,8,256]{2,1,0:T(8,128)(2,1)}), bf16[64,8,256]{2,1,0:T(8,128)(2,1)S(1)}, u32[]{:S(2)}, u32[]{:S(2)}) %all-to-all-start.1) | async-done | bytes 262176 | tf_op jit(solution)/shard_map/all_to_all | solution.py:359
  34.7 0.6 collective-permute-start.5
  35.3 1.0 sums.1
  36.3 8.7 %all-to-all-start = ((bf16[64,8,512]{2,1,0:T(8,128)(2,1)}), bf16[64,8,512]{2,1,0:T(8,128)(2,1)S(1)}, u32[]{:S(2)}, u32[]{:S(2)}) async-start(bf16[64,8,512]{2,1,0:T(8,128)(2,1)} %bitcast.7), calls=%async_computation | async-start | bytes 1048576 | tf_op jit(solution)/shard_map/all_to_all | solution.py:359
  45.0 0.0 copy-start.2
  45.0 0.0 copy-start.3
  45.0 0.0 copy-start.4
  45.0 0.5 collective-permute-start.4
  45.6 0.1 collective-permute-start.6
  45.7 1.1 %collective-permute-done.4.refs_1_.refs_5_ = bf16[8,64,256]{2,1,0:T(8,128)(2,1)S(1)} collective-permute-done((bf16[8,64,256]{2,1,0:T(8,128)(2,1)S(1)}, bf16[8,64,256]{2,1,0:T(8,128)(2,1)S(1)}, u32[]{:S(2)}, u32[]{:S(2)}) %collective-permute-start.4) | collective-permute-done | bytes 262176 | tf_op jit(solution)/shard_map/ppermute | solution.py:350
  46.8 0.4 collective-permute-done.6.refs_3_.refs_7_
  47.1 5.4 %trig.1.trig_ref = f32[16,2,64,512]{3,2,1,0:T(8,128)} custom-call(s32[3]{0:T(128)S(1)} %pad_add_fusion.place, bf16[8,64,256]{2,1,0:T(8,128)(2,1)S(1)} %bitcast.23, bf16[8,64,256]{2,1,0:T(8,128)(2,1)S(1)} %collective-permute-done.4.refs_1_.refs_5_, bf16[8,64,256]{2,1,0:T(8,128)(2,1)S(1)} %collective-permute-done.5.refs_2_.refs_6_, ...), custom_call_target="tpu_custom_call" | custom-call | flops 7000000000 | bytes 1000000 | tf_op jit(solution)/shard_map/trig/pallas_call | solution.py:223
  52.5 9.4 %all-to-all-done = bf16[64,8,512]{2,1,0:T(8,128)(2,1)S(1)} async-done(((bf16[64,8,512]{2,1,0:T(8,128)(2,1)}), bf16[64,8,512]{2,1,0:T(8,128)(2,1)S(1)}, u32[]{:S(2)}, u32[]{:S(2)}) %all-to-all-start) | async-done | bytes 524320 | tf_op jit(solution)/shard_map/all_to_all | solution.py:359
  62.0 0.0 copy-start
  62.0 0.0 copy-start.1
  62.0 7.4 %levels.1 = bf16[8,8,8,256]{3,2,1,0:T(8,128)(2,1)S(1)} custom-call(bf16[2,256,512]{2,1,0:T(8,128)(2,1)S(1)} %bitcast.16, bf16[8,512,512]{2,1,0:T(8,128)(2,1)} %t_ref.3, f32[16,2,64,512]{3,2,1,0:T(8,128)} %trig.1.trig_ref, bf16[256,256]{1,0:T(8,128)(2,1)S(1)} %copy-done.3, bf16[256,256]{1,0:T(8,128)(2,1)S(1)} %copy-done.2, bf16[64,64]{1,0:T(8,128)(2,1)S(1)} %copy-done.4), custom_call_target="tpu_custom_call" | custom-call | tf_op jit(solution)/shard_map/levels/pallas_call | solution.py:288
  69.5 22.1 %all_to_all.15 = bf16[64,8,256]{2,1,0:T(8,128)(2,1)S(1)} all-to-all(bf16[64,8,256]{2,1,0:T(8,128)(2,1)S(1)} %bitcast.20), channel_id=1, replica_groups=mesh['x4'=2,'x3'=2,'y4'=2,'y3'=2,'y2'=2,'z4'=2,'z3'=2,'z2'=2] {'y4','z4'..., dimensions={0} | all-to-all | bytes 524288 | tf_op jit(solution)/shard_map/all_to_all | solution.py:359
  91.6 3.3 %collective-permute-start.7 = (bf16[512,256]{1,0:T(8,128)(2,1)S(1)}, bf16[512,256]{1,0:T(8,128)(2,1)S(1)}, u32[]{:S(2)}, u32[]{:S(2)}) collective-permute-start(bf16[512,256]{1,0:T(8,128)(2,1)S(1)} %bitcast.18), channel_id=1, source_target_pairs={{0,1},{1,0},{2,3},{3,2},{4,5},{5,4},{6,7},{7,6},{8,9},{9,8},{10,11... | collective-permute-start | bytes 786440 | tf_op jit(solution)/shard_map/ppermute | solution.py:350
  94.9 2.5 %collective-permute-done.8.n2 = bf16[512,256]{1,0:T(8,128)(2,1)S(1)} collective-permute-done((bf16[512,256]{1,0:T(8,128)(2,1)S(1)}, bf16[512,256]{1,0:T(8,128)(2,1)S(1)}, u32[]{:S(2)}, u32[]{:S(2)}) %collective-permute-start.8) | collective-permute-done | bytes 262176 | tf_op jit(solution)/shard_map/ppermute | solution.py:350
  97.4 2.9 %collective-permute-start.9 = (bf16[512,256]{1,0:T(8,128)(2,1)S(1)}, bf16[512,256]{1,0:T(8,128)(2,1)S(1)}, u32[]{:S(2)}, u32[]{:S(2)}) collective-permute-start(bf16[512,256]{1,0:T(8,128)(2,1)S(1)} %collective-permute-done.8.n2), channel_id=1, source_target_pairs={{0,1},{1,0},{2,3},{3,2},{4,5},{5,4},{6,7},{7,6},{8,9},{9,8},{10,11... | collective-permute-start | bytes 786440 | tf_op jit(solution)/shard_map/ppermute | solution.py:350
  100.3 1.2 %collective-permute-done.9.n3 = bf16[512,256]{1,0:T(8,128)(2,1)S(1)} collective-permute-done((bf16[512,256]{1,0:T(8,128)(2,1)S(1)}, bf16[512,256]{1,0:T(8,128)(2,1)S(1)}, u32[]{:S(2)}, u32[]{:S(2)}) %collective-permute-start.9) | collective-permute-done | bytes 262176 | tf_op jit(solution)/shard_map/ppermute | solution.py:350
  101.5 3.1 %final.1 = bf16[2,4,256,512]{3,2,1,0:T(8,128)(2,1)} custom-call(s32[3]{0:T(128)S(1)} %pad_add_fusion.place, bf16[512,256]{1,0:T(8,128)(2,1)S(1)} %bitcast.19, bf16[512,256]{1,0:T(8,128)(2,1)S(1)} %collective-permute-done.7.n1, bf16[512,256]{1,0:T(8,128)(2,1)S(1)} %collective-permute-done.8.n2, bf16[512,256]{1,0:T(8,128)(2,1)S(1)} %collective-permute-done.9.n3, ...), custom_call_target="tpu_custom_call" | custom-call | tf_op jit(solution)/shard_map/final/pallas_call | solution.py:334
  (11 shorter events, 0.0 us)
Async XLA Ops:
  4.5 16.8 %collective-permute-start = (bf16[2,256,512]{2,1,0:T(8,128)(2,1)S(1)}, bf16[2,256,512]{2,1,0:T(8,128)(2,1)S(1)}, u32[]{:S(2)}, u32[]{:S(2)}) collective-permute-start(bf16[2,256,512]{2,1,0:T(8,128)(2,1)S(1)} %get-tuple-element.12), channel_id=1, source_target_pairs={{0,32},{32,0},{1,33},{33,1},{2,34},{34,2},{3,35},{35,3},{4,36},{36... | collective-permute-start | bytes 1572872 | tf_op jit(solution)/shard_map/ppermute | solution.py:350
  8.2 16.5 %collective-permute-start.2 = (bf16[2,256,512]{2,1,0:T(8,128)(2,1)S(1)}, bf16[2,256,512]{2,1,0:T(8,128)(2,1)S(1)}, u32[]{:S(2)}, u32[]{:S(2)}) collective-permute-start(bf16[2,256,512]{2,1,0:T(8,128)(2,1)S(1)} %get-tuple-element.14), channel_id=1, source_target_pairs={{0,4},{4,0},{1,5},{5,1},{2,6},{6,2},{3,7},{7,3},{8,12},{12,8},{9,1... | collective-permute-start | bytes 1572872 | tf_op jit(solution)/shard_map/ppermute | solution.py:350
  11.1 23.6 %all-to-all-start.1 = ((bf16[64,8,256]{2,1,0:T(8,128)(2,1)}), bf16[64,8,256]{2,1,0:T(8,128)(2,1)S(1)}, u32[]{:S(2)}, u32[]{:S(2)}) async-start(bf16[64,8,256]{2,1,0:T(8,128)(2,1)} %bitcast.9), calls=%async_computation.1 | async-start | bytes 524288 | tf_op jit(solution)/shard_map/all_to_all | solution.py:359
  22.1 13.2 %collective-permute-start.1 = (bf16[256,512]{1,0:T(8,128)(2,1)}, bf16[256,512]{1,0:T(8,128)(2,1)S(1)}, u32[]{:S(2)}, u32[]{:S(2)}) collective-permute-start(bf16[256,512]{1,0:T(8,128)(2,1)} %fusion), channel_id=1, source_target_pairs={{0,4},{4,0},{1,5},{5,1},{2,6},{6,2},{3,7},{7,3},{8,12},{12,8},{9,1... | collective-permute-start | bytes 786440 | tf_op jit(solution)/shard_map/ppermute | solution.py:350
  24.7 10.6 %collective-permute-start.3 = (bf16[256,512]{1,0:T(8,128)(2,1)S(1)}, bf16[256,512]{1,0:T(8,128)(2,1)S(1)}, u32[]{:S(2)}, u32[]{:S(2)}) collective-permute-start(bf16[256,512]{1,0:T(8,128)(2,1)S(1)} %fusion.1), channel_id=1, source_target_pairs={{0,32},{32,0},{1,33},{33,1},{2,34},{34,2},{3,35},{35,3},{4,36},{36... | collective-permute-start | bytes 786440 | tf_op jit(solution)/shard_map/ppermute | solution.py:350
  34.7 10.9 %collective-permute-start.5 = (bf16[8,64,256]{2,1,0:T(8,128)(2,1)S(1)}, bf16[8,64,256]{2,1,0:T(8,128)(2,1)S(1)}, u32[]{:S(2)}, u32[]{:S(2)}) collective-permute-start(bf16[8,64,256]{2,1,0:T(8,128)(2,1)S(1)} %bitcast.21), channel_id=1, source_target_pairs={{0,8},{8,0},{1,9},{9,1},{2,10},{10,2},{3,11},{11,3},{4,12},{12,4},... | collective-permute-start | bytes 786440 | tf_op jit(solution)/shard_map/ppermute | solution.py:350
  36.3 25.6 %all-to-all-start = ((bf16[64,8,512]{2,1,0:T(8,128)(2,1)}), bf16[64,8,512]{2,1,0:T(8,128)(2,1)S(1)}, u32[]{:S(2)}, u32[]{:S(2)}) async-start(bf16[64,8,512]{2,1,0:T(8,128)(2,1)} %bitcast.7), calls=%async_computation | async-start | bytes 1048576 | tf_op jit(solution)/shard_map/all_to_all | solution.py:359
  45.0 17.0 %copy-start.2 = (bf16[256,256]{1,0:T(8,128)(2,1)S(1)}, bf16[256,256]{1,0:T(8,128)(2,1)}, u32[]{:S(2)}) copy-start(bf16[256,256]{1,0:T(8,128)(2,1)} %constant.39.clone.turn_ref) | copy-start | bytes 393220
  45.0 17.0 %copy-start.3 = (bf16[256,256]{1,0:T(8,128)(2,1)S(1)}, bf16[256,256]{1,0:T(8,128)(2,1)}, u32[]{:S(2)}) copy-start(bf16[256,256]{1,0:T(8,128)(2,1)} %constant.38.clone.enter_ref) | copy-start | bytes 393220
  45.0 17.0 %copy-start.4 = (bf16[64,64]{1,0:T(8,128)(2,1)S(1)}, bf16[64,64]{1,0:T(8,128)(2,1)}, u32[]{:S(2)}) copy-start(bf16[64,64]{1,0:T(8,128)(2,1)} %constant.40.clone.leave_ref) | copy-start | bytes 24580
  45.0 1.7 %collective-permute-start.4 = (bf16[8,64,256]{2,1,0:T(8,128)(2,1)S(1)}, bf16[8,64,256]{2,1,0:T(8,128)(2,1)S(1)}, u32[]{:S(2)}, u32[]{:S(2)}) collective-permute-start(bf16[8,64,256]{2,1,0:T(8,128)(2,1)S(1)} %bitcast.22), channel_id=1, source_target_pairs={{0,1},{1,0},{2,3},{3,2},{4,5},{5,4},{6,7},{7,6},{8,9},{9,8},{10,11... | collective-permute-start | bytes 786440 | tf_op jit(solution)/shard_map/ppermute | solution.py:350
  45.6 1.5 %collective-permute-start.6 = (bf16[8,64,256]{2,1,0:T(8,128)(2,1)S(1)}, bf16[8,64,256]{2,1,0:T(8,128)(2,1)S(1)}, u32[]{:S(2)}, u32[]{:S(2)}) collective-permute-start(bf16[8,64,256]{2,1,0:T(8,128)(2,1)S(1)} %collective-permute-done.5.refs_2_.refs_6_), channel_id=1, source_target_pairs={{0,1},{1,0},{2,3},{3,2},{4,5},{5,4},{6,7},{7,6},{8,9},{9,8},{10,11... | collective-permute-start | bytes 786440 | tf_op jit(solution)/shard_map/ppermute | solution.py:350
  62.0 39.5 %copy-start = (bf16[8,512,512]{2,1,0:T(8,128)(2,1)S(1)}, bf16[8,512,512]{2,1,0:T(8,128)(2,1)}, u32[]{:S(2)}) copy-start(bf16[8,512,512]{2,1,0:T(8,128)(2,1)} %t_ref.3) | copy-start | bytes 12582916
  62.0 39.5 %copy-start.1 = (bf16[4,256,256]{2,1,0:T(8,128)(2,1)S(1)}, bf16[4,256,256]{2,1,0:T(8,128)(2,1)}, u32[]{:S(2)}) copy-start(bf16[4,256,256]{2,1,0:T(8,128)(2,1)} %constant.41.clone.pick_ref) | copy-start | bytes 1572868
  91.6 5.8 %collective-permute-start.8 = (bf16[512,256]{1,0:T(8,128)(2,1)S(1)}, bf16[512,256]{1,0:T(8,128)(2,1)S(1)}, u32[]{:S(2)}, u32[]{:S(2)}) collective-permute-start(bf16[512,256]{1,0:T(8,128)(2,1)S(1)} %bitcast.17), channel_id=1, source_target_pairs={{0,8},{8,0},{1,9},{9,1},{2,10},{10,2},{3,11},{11,3},{4,12},{12,4},... | collective-permute-start | bytes 786440 | tf_op jit(solution)/shard_map/ppermute | solution.py:350
  91.6 8.7 %collective-permute-start.7 = (bf16[512,256]{1,0:T(8,128)(2,1)S(1)}, bf16[512,256]{1,0:T(8,128)(2,1)S(1)}, u32[]{:S(2)}, u32[]{:S(2)}) collective-permute-start(bf16[512,256]{1,0:T(8,128)(2,1)S(1)} %bitcast.18), channel_id=1, source_target_pairs={{0,1},{1,0},{2,3},{3,2},{4,5},{5,4},{6,7},{7,6},{8,9},{9,8},{10,11... | collective-permute-start | bytes 786440 | tf_op jit(solution)/shard_map/ppermute | solution.py:350
  97.4 4.1 %collective-permute-start.9 = (bf16[512,256]{1,0:T(8,128)(2,1)S(1)}, bf16[512,256]{1,0:T(8,128)(2,1)S(1)}, u32[]{:S(2)}, u32[]{:S(2)}) collective-permute-start(bf16[512,256]{1,0:T(8,128)(2,1)S(1)} %collective-permute-done.8.n2), channel_id=1, source_target_pairs={{0,1},{1,0},{2,3},{3,2},{4,5},{5,4},{6,7},{7,6},{8,9},{9,8},{10,11... | collective-permute-start | bytes 786440 | tf_op jit(solution)/shard_map/ppermute | solution.py:350

commit v6 on v5

--- a/solution.py
+++ b/solution.py
@@ -185,10 +185,10 @@
 
 def trig_kernel(place, *refs):
     near1, near2 = refs[0:4], refs[4:8]
-    first_ref, second_ref, out_ref = refs[8:]
+    first_ref, second_ref, out1_ref, out2_ref = refs[8:]
     step = pl.program_id(0)
 
-    def write(t, angle):
+    def write(out_ref, t, angle):
         for half in range(2):
             for at in range(0, 64, 8):
                 sine, cosine = sin_cos(angle[64 * half + at : 64 * half + at + 8])
@@ -199,13 +199,13 @@
     def _():
         for t in range(4):
             held = jnp.concatenate([r[t] for r in near1], axis=0)
-            write(t, dot(first_ref[0], held))
+            write(out1_ref, t, dot(first_ref[0], held))
 
     @pl.when(step >= 2)
     def _():
         for t in range(4):
             held = [r[:, 8 * t : 8 * t + 8, :].astype(F32).reshape(64, HALF) for r in near2]
-            write(t, dot(second_ref[0], jnp.concatenate(held, axis=0).astype(BF)))
+            write(out2_ref, t, dot(second_ref[0], jnp.concatenate(held, axis=0).astype(BF)))
 
 
 def trig(place, near):
@@ -218,35 +218,36 @@
         in_specs=[pl.BlockSpec((4, 64, HALF), lambda i, p: (jnp.minimum(i, 1), 0, 0))] * 4
         + [pl.BlockSpec((8, 32, HALF), lambda i, p: (0, jnp.maximum(i - 2, 0), 0))] * 4
         + [own(128, 256), own(128, 256)],
-        out_specs=pl.BlockSpec((4, 2, 64, CHEB), lambda i, p: (i, 0, 0, 0)),
+        out_specs=[
+            pl.BlockSpec((4, 2, 64, CHEB), lambda i, p: (jnp.minimum(i, 1), 0, 0, 0)),
+            pl.BlockSpec((4, 2, 64, CHEB), lambda i, p: (jnp.maximum(i - 2, 0), 0, 0, 0)),
+        ],
     )
     return pl.pallas_call(
         trig_kernel,
         grid_spec=spec,
-        out_shape=pltpu.HBM((16, 2, 64, CHEB), F32),
-        compiler_params=params(12),
+        out_shape=[jax.ShapeDtypeStruct((8, 2, 64, CHEB), F32), pltpu.HBM((8, 2, 64, CHEB), F32)],
+        compiler_params=params(14),
         cost_estimate=pl.CostEstimate(flops=7 * 10**9, bytes_accessed=10**6, transcendentals=0),
         name="trig",
     )(place, *near, *near, in_hbm(jnp.asarray(FIRST, BF)), in_hbm(jnp.asarray(SECOND, BF)))
 
 
-def levels_kernel(x_ref, t_ref, trig_ref, enter_ref, turn_ref, leave_ref, out_ref, left, middle, even, odd):
-    step = pl.program_id(0)
-
-    @pl.when(step == 0)
-    def _():
-        total = (x_ref[0].astype(F32) + x_ref[1].astype(F32)).astype(BF)
-        left[...] = dot(enter_ref[...], total).astype(BF)
-
-    @pl.when(step == 2)
-    def _():
-        left[...] = dot(turn_ref[...], middle[...]).astype(BF)
-
-    def turn_and_sum(product, at):
+def levels_kernel(place, x_ref, t_hbm, wave1_ref, wave2_hbm, enter_ref, turn_ref, leave_ref, out_ref, last_ref,
+                  t_ref, wave2_ref, left, middle, even, odd, sems):
+    matrices = [pltpu.make_async_copy(t_hbm.at[t], t_ref.at[t], sems.at[t]) for t in range(8)]
+    waves = pltpu.make_async_copy(wave2_hbm, wave2_ref, sems.at[8])
+    for copy in matrices:
+        copy.start()
+    waves.start()
+    total = (x_ref[0].astype(F32) + x_ref[1].astype(F32)).astype(BF)
+    left[...] = dot(enter_ref[...], total).astype(BF)
+
+    def turn_and_sum(product, wave_ref, at):
         total = [jnp.zeros((8, CHEB), F32)] * 4
         for outer in range(8):
-            sine = trig_ref[at, 0, 8 * outer : 8 * outer + 8, :]
-            cosine = trig_ref[at, 1, 8 * outer : 8 * outer + 8, :]
+            sine = wave_ref[at, 0, 8 * outer : 8 * outer + 8, :]
+            cosine = wave_ref[at, 1, 8 * outer : 8 * outer + 8, :]
             for r in range(2):
                 row = 32 * outer + 8 * r
                 re = product[row : row + 8, :]
@@ -255,58 +256,73 @@
                 total[2 + r] = total[2 + r] + (re * sine + im * cosine)
         return jnp.concatenate(total, axis=0).astype(BF)
 
-    def four_orientations(put):
-        even[...] = dot(left[...], t_ref[0])
-        for t in range(4):
-            if t < 3:
-                (odd, even)[t % 2][...] = dot(left[...], t_ref[t + 1])
-            put(t, turn_and_sum((even, odd)[t % 2], t))
-
-    @pl.when(step < 2)
-    def _():
-        def put(t, value):
-            row = pl.multiple_of(128 * step + 32 * t, 32)
-            middle[pl.ds(row, 32), :] = value
-
-        four_orientations(put)
-
-    @pl.when(step >= 2)
-    def _():
-        def put(t, value):
+    slots = (even, odd)
+    for copy in matrices[:2]:
+        copy.wait()
+    even[...] = dot(left[...], t_ref[0])
+    for t in range(8):
+        if t % 2 == 1:
+            for copy in matrices[t + 1 : t + 3]:
+                copy.wait()
+        if t < 7:
+            slots[(t + 1) % 2][...] = dot(left[...], t_ref[t + 1])
+        middle[32 * t : 32 * t + 32, :] = turn_and_sum(slots[t % 2], wave1_ref, t)
+    waves.wait()
+    kept = [
+        pltpu.make_async_copy(t_ref.at[4 * x2 + place[2]], last_ref.at[x2], sems.at[9 + x2]) for x2 in range(2)
+    ]
+    for copy in kept:
+        copy.start()
+    left[...] = dot(turn_ref[...], middle[...]).astype(BF)
+
+    def four_orientations(group, carry):
+        even[...] = dot(left[...], t_ref[4 * group])
+        for i in range(4):
+            if i < 3:
+                slots[(i + 1) % 2][...] = dot(left[...], t_ref[4 * group + i + 1])
+            value = turn_and_sum(slots[i % 2], wave2_ref, 4 * group + i)
             value = jnp.concatenate([value[:, :HALF], value[:, HALF:]], axis=0)
             value = dot(leave_ref[...], value)
             for t4 in range(8):
-                out_ref[t4, t] = value[8 * t4 : 8 * t4 + 8].astype(BF)
-
-        four_orientations(put)
-
-
-def levels(share, translation, waves):
-    def const(*shape):
-        return pl.BlockSpec(shape, lambda i: (0,) * len(shape))
-
+                out_ref[t4, 4 * group + i] = value[8 * t4 : 8 * t4 + 8].astype(BF)
+        return carry
+
+    lax.fori_loop(0, 2, four_orientations, 0)
+    for copy in kept:
+        copy.wait()
+
+
+def levels(place, share, translation, wave1, wave2):
+    vmem, hbm = pl.BlockSpec(memory_space=pltpu.VMEM), pl.BlockSpec(memory_space=pl.ANY)
     return pl.pallas_call(
         levels_kernel,
-        grid=(4,),
-        out_shape=jax.ShapeDtypeStruct((8, 8, 8, HALF), BF),
-        in_specs=[
-            const(2, 256, CHEB),
-            pl.BlockSpec((4, CHEB, CHEB), lambda i: (i % 2, 0, 0)),
-            pl.BlockSpec((4, 2, 64, CHEB), lambda i: (i, 0, 0, 0)),
-            const(256, 256),
-            const(256, 256),
-            const(64, 64),
+        out_shape=[
+            jax.ShapeDtypeStruct((8, 8, 8, HALF), BF),
+            jax.ShapeDtypeStruct((2, CHEB, CHEB), BF),
         ],
-        out_specs=pl.BlockSpec((8, 4, 8, HALF), lambda i: (0, jnp.maximum(i - 2, 0), 0, 0)),
+        in_specs=[pl.BlockSpec(memory_space=pltpu.SMEM), vmem, hbm, vmem, hbm, vmem, vmem, vmem],
+        out_specs=[vmem, vmem],
         scratch_shapes=[
+            pltpu.VMEM((8, CHEB, CHEB), BF),
+            pltpu.VMEM((8, 2, 64, CHEB), F32),
             pltpu.VMEM((256, CHEB), BF),
             pltpu.VMEM((256, CHEB), BF),
             pltpu.VMEM((256, CHEB), F32),
             pltpu.VMEM((256, CHEB), F32),
+            pltpu.SemaphoreType.DMA((11,)),
         ],
         compiler_params=params(20),
         name="levels",
-    )(share, in_hbm(translation), in_hbm(waves), jnp.asarray(ENTER, BF), jnp.asarray(TURN, BF), jnp.asarray(LEAVE, BF))
+    )(
+        place,
+        share,
+        in_hbm(translation),
+        wave1,
+        in_hbm(wave2),
+        jnp.asarray(ENTER, BF),
+        jnp.asarray(TURN, BF),
+        jnp.asarray(LEAVE, BF),
+    )
 
 
 def final_kernel(place, n0, n1, n2, n3, pick_ref, t_ref, out_ref, left, made, sems):
@@ -320,7 +336,7 @@
             value = jnp.concatenate([value[:128], value[128:]], axis=1)
             left[block, 128 * high : 128 * high + 128, :] = value.astype(BF)
         for x2 in range(2):
-            made[x2, block] = dot(left[block], t_ref[4 * x2 + own]).astype(BF)
+            made[x2, block] = dot(left[block], t_ref[x2]).astype(BF)
             copies.append(
                 pltpu.make_async_copy(made.at[x2, block], out_ref.at[x2, block], sems.at[x2, block])
             )
@@ -329,7 +345,7 @@
         copy.wait()
 
 
-def final(place, near, translation):
+def final(place, near, last):
     vmem = pl.BlockSpec(memory_space=pltpu.VMEM)
     return pl.pallas_call(
         final_kernel,
@@ -343,7 +359,7 @@
         ],
         compiler_params=params(14),
         name="final",
-    )(place, *near, jnp.asarray(FINAL, BF), translation)
+    )(place, *near, jnp.asarray(FINAL, BF), last)
 
 
 def swap(value, axis):
@@ -374,11 +390,11 @@
     again0, again1 = swap(again0, "z4"), swap(again1, "y4")
     share = sums(keep0, come0, again0, keep1, come1, again1)
     share = exchange(share.reshape(64, 8, CHEB), ("x4", "x3", "y3", "z3", "y2", "z2"))
-    waves = trig(place, near)
-    done = levels(share.reshape(2, 256, CHEB), translation, waves)
+    wave1, wave2 = trig(place, near)
+    done, last = levels(place, share.reshape(2, 256, CHEB), translation, wave1, wave2)
     done = exchange(done.reshape(64, 8, HALF), ("y4", "z4", "x4", "x3", "y3", "z3"))
     near = four(done.reshape(512, HALF))
-    return final(place, near, translation).reshape(shape)
+    return final(place, near, last).reshape(shape)
 
 
 def solution(mesh):

time: 105 us -> 104 us (level)
  starting transfers between devices: 38.3 us -> 41.7 us
  Pallas kernels: 21.4 us -> 19.6 us
  waiting for transfers between devices: 21.7 us -> 20.4 us
    ppermute x10, starting transfers between devices: 19.4 us -> 21.7 us  [swap(): return lax.ppermute(value, axis, [(0, 1), (1, 0)])]
    pallas_call x2, Pallas kernels: 12.8 us -> 11 us  [the longest x1 5.92 us: levels(): pl.pallas_call(levels_kernel, out_shape=[jax.ShapeDtypeStruct((8, 8, 8, H...]
    ppermute x10, waiting for transfers between devices: 5.09 us -> 3.52 us  [swap(): return lax.ppermute(value, axis, [(0, 1), (1, 0)])]
    all_to_all x2, starting transfers between devices: 18.9 us -> 20 us  [exchange(): return lax.all_to_all(value, axes, split_axis=0, concat_axis=0, tiled=True)]
where the time goes in v6:
time: 104 us
  starting transfers between devices  41.7 us (40%)
  blocking collectives  21.1 us (20%)
  waiting for transfers between devices  20.4 us (20%)
  Pallas kernels  19.6 us (19%)
    ppermute x10, starting transfers between devices, swap(): return lax.ppermute(value, axis, [(0, 1), (1, 0)])  21.7 us
    all_to_all x1, blocking collectives, exchange(): return lax.all_to_all(value, axes, split_axis=0, concat_axis=0, tiled=True)  21.1 us
    all_to_all x2, starting transfers between devices, exchange(): return lax.all_to_all(value, axes, split_axis=0, concat_axis=0, tiled=True)  20 us
    all_to_all x2, waiting for transfers between devices, exchange(): return lax.all_to_all(value, axes, split_axis=0, concat_axis=0, tiled=True)  16.9 us
    pallas_call x1, Pallas kernels, levels(): pl.pallas_call(levels_kernel, out_shape=[jax.ShapeDtypeStruct((8, 8, 8, H...  5.92 us
    pallas_call x1, Pallas kernels, trig(): pl.pallas_call(trig_kernel, grid_spec=spec, out_shape=[jax.ShapeDtypeStru...  5.12 us
    pallas_call x1, Pallas kernels, rotate(): pl.pallas_call(rotate_kernel, out_shape=[piece] * 4 + [jax.ShapeDtypeStru...  4.41 us
    ppermute x10, waiting for transfers between devices, swap(): return lax.ppermute(value, axis, [(0, 1), (1, 0)])  3.52 us
  transfers between devices with their start and end apart: 12, of which 6 were waited for; matrix products, arithmetic and copies ran while one was open for 1% of the time, Pallas kernels for 6%

profile of v6, /device:TPU:1, one launch (start us, length us, event | category | flops | bytes accessed | tf_op | source)
XLA Modules:
  0.0 104.0 jit_solution(11817481626706184228)
XLA Ops:
  0.0 0.1 pad_add_fusion.place
  0.1 4.4 %rotate.1 = (bf16[2,256,512]{2,1,0:T(8,128)(2,1)S(1)}, bf16[2,256,512]{2,1,0:T(8,128)(2,1)}, bf16[2,256,512]{2,1,0:T(8,128)(2,1)S(1)}, bf16[2,256,512]{2,1,0:T(8,128)(2,1)S(1)}, bf16[2,4,64,256]{3,2,1,0:T(8,128)(2,1)}) custom-call(s32[3]{0:T(128)S(1)} %pad_add_fusion.place, bf16[2,4,256,512]{3,2,1,0:T(8,128)(2,1)} %bitcast.25, ...), custom_call_target="tpu_custom_call" | custom-call | tf_op jit(solution)/shard_map/rotate/pallas_call | solution.py:145
  4.5 3.7 %collective-permute-start = (bf16[2,256,512]{2,1,0:T(8,128)(2,1)S(1)}, bf16[2,256,512]{2,1,0:T(8,128)(2,1)S(1)}, u32[]{:S(2)}, u32[]{:S(2)}) collective-permute-start(bf16[2,256,512]{2,1,0:T(8,128)(2,1)S(1)} %get-tuple-element.16), channel_id=1, source_target_pairs={{0,32},{32,0},{1,33},{33,1},{2,34},{34,2},{3,35},{35,3},{4,36},{36... | collective-permute-start | bytes 1572872 | tf_op jit(solution)/shard_map/ppermute | solution.py:366
  8.2 2.9 %collective-permute-start.2 = (bf16[2,256,512]{2,1,0:T(8,128)(2,1)}, bf16[2,256,512]{2,1,0:T(8,128)(2,1)S(1)}, u32[]{:S(2)}, u32[]{:S(2)}) collective-permute-start(bf16[2,256,512]{2,1,0:T(8,128)(2,1)} %get-tuple-element.18), channel_id=1, source_target_pairs={{0,4},{4,0},{1,5},{5,1},{2,6},{6,2},{3,7},{7,3},{8,12},{12,8},{9,1... | collective-permute-start | bytes 1572872 | tf_op jit(solution)/shard_map/ppermute | solution.py:366
  11.1 10.3 %all-to-all-start.1 = ((bf16[64,8,256]{2,1,0:T(8,128)(2,1)}), bf16[64,8,256]{2,1,0:T(8,128)(2,1)S(1)}, u32[]{:S(2)}, u32[]{:S(2)}) async-start(bf16[64,8,256]{2,1,0:T(8,128)(2,1)} %bitcast.9), calls=%async_computation.1 | async-start | bytes 524288 | tf_op jit(solution)/shard_map/all_to_all | solution.py:375
  21.3 0.0 collective-permute-done.come0
  21.4 0.1 fusion
  21.4 2.6 %collective-permute-start.1 = (bf16[256,512]{1,0:T(8,128)(2,1)S(1)}, bf16[256,512]{1,0:T(8,128)(2,1)S(1)}, u32[]{:S(2)}, u32[]{:S(2)}) collective-permute-start(bf16[256,512]{1,0:T(8,128)(2,1)S(1)} %fusion), channel_id=1, source_target_pairs={{0,4},{4,0},{1,5},{5,1},{2,6},{6,2},{3,7},{7,3},{8,12},{12,8},{9,1... | collective-permute-start | bytes 786440 | tf_op jit(solution)/shard_map/ppermute | solution.py:366
  24.0 0.8 fusion.1
  24.8 2.7 %collective-permute-start.3 = (bf16[256,512]{1,0:T(8,128)(2,1)}, bf16[256,512]{1,0:T(8,128)(2,1)S(1)}, u32[]{:S(2)}, u32[]{:S(2)}) collective-permute-start(bf16[256,512]{1,0:T(8,128)(2,1)} %fusion.1), channel_id=1, source_target_pairs={{0,32},{32,0},{1,33},{33,1},{2,34},{34,2},{3,35},{35,3},{4,36},{36... | collective-permute-start | bytes 786440 | tf_op jit(solution)/shard_map/ppermute | solution.py:366
  27.5 7.2 %all-to-all-done.1 = bf16[64,8,256]{2,1,0:T(8,128)(2,1)S(1)} async-done(((bf16[64,8,256]{2,1,0:T(8,128)(2,1)}), bf16[64,8,256]{2,1,0:T(8,128)(2,1)S(1)}, u32[]{:S(2)}, u32[]{:S(2)}) %all-to-all-start.1) | async-done | bytes 262176 | tf_op jit(solution)/shard_map/all_to_all | solution.py:375
  34.7 0.6 collective-permute-start.5
  35.3 1.0 sums.1
  36.4 9.8 %all-to-all-start = ((bf16[64,8,512]{2,1,0:T(8,128)(2,1)}), bf16[64,8,512]{2,1,0:T(8,128)(2,1)S(1)}, u32[]{:S(2)}, u32[]{:S(2)}) async-start(bf16[64,8,512]{2,1,0:T(8,128)(2,1)} %bitcast.7), calls=%async_computation | async-start | bytes 1048576 | tf_op jit(solution)/shard_map/all_to_all | solution.py:375
  46.1 0.0 copy-start.1
  46.1 0.0 copy-start.2
  46.2 0.0 copy-start.3
  46.2 0.5 collective-permute-start.4
  46.7 0.1 collective-permute-start.6
  46.8 1.1 %collective-permute-done.4.refs_1_.refs_5_ = bf16[8,64,256]{2,1,0:T(8,128)(2,1)S(1)} collective-permute-done((bf16[8,64,256]{2,1,0:T(8,128)(2,1)S(1)}, bf16[8,64,256]{2,1,0:T(8,128)(2,1)S(1)}, u32[]{:S(2)}, u32[]{:S(2)}) %collective-permute-start.4) | collective-permute-done | bytes 262176 | tf_op jit(solution)/shard_map/ppermute | solution.py:366
  47.9 0.4 collective-permute-done.6.refs_3_.refs_7_
  48.3 5.1 %trig.1 = (f32[8,2,64,512]{3,2,1,0:T(8,128)S(1)}, f32[8,2,64,512]{3,2,1,0:T(8,128)}) custom-call(s32[3]{0:T(128)S(1)} %pad_add_fusion.place, bf16[8,64,256]{2,1,0:T(8,128)(2,1)S(1)} %bitcast.22, bf16[8,64,256]{2,1,0:T(8,128)(2,1)S(1)} %collective-permute-done.4.refs_1_.refs_5_, bf16[8,64,256]{2,1,0:T(8,128)(2,1)S(1)} %collective-permute-done.5.refs_2_.refs_6_, ...), custom_call_target="tpu_custom_call" | custom-call | flops 7000000000 | bytes 1000000 | tf_op jit(solution)/shard_map/trig/pallas_call | solution.py:226
  53.4 9.7 %all-to-all-done = bf16[64,8,512]{2,1,0:T(8,128)(2,1)S(1)} async-done(((bf16[64,8,512]{2,1,0:T(8,128)(2,1)}), bf16[64,8,512]{2,1,0:T(8,128)(2,1)S(1)}, u32[]{:S(2)}, u32[]{:S(2)}) %all-to-all-start) | async-done | bytes 524320 | tf_op jit(solution)/shard_map/all_to_all | solution.py:375
  63.1 0.0 copy-start
  63.1 5.9 %levels.1 = (bf16[8,8,8,256]{3,2,1,0:T(8,128)(2,1)S(1)}, bf16[2,512,512]{2,1,0:T(8,128)(2,1)S(1)}) custom-call(s32[3]{0:T(128)S(1)} %pad_add_fusion.place, bf16[2,256,512]{2,1,0:T(8,128)(2,1)S(1)} %bitcast.16, bf16[8,512,512]{2,1,0:T(8,128)(2,1)} %t_hbm.1, f32[8,2,64,512]{3,2,1,0:T(8,128)S(1)} %get-tuple-element.21.wave1_ref, ...), custom_call_target="tpu_custom_call" | custom-call | tf_op jit(solution)/shard_map/levels/pallas_call | solution.py:297
  69.1 21.1 %all_to_all.15 = bf16[64,8,256]{2,1,0:T(8,128)(2,1)S(1)} all-to-all(bf16[64,8,256]{2,1,0:T(8,128)(2,1)S(1)} %bitcast.24), channel_id=1, replica_groups=mesh['x4'=2,'x3'=2,'y4'=2,'y3'=2,'y2'=2,'z4'=2,'z3'=2,'z2'=2] {'y4','z4'..., dimensions={0} | all-to-all | bytes 524288 | tf_op jit(solution)/shard_map/all_to_all | solution.py:375
  90.2 1.0 collective-permute-start.8
  91.1 3.4 %collective-permute-start.7 = (bf16[512,256]{1,0:T(8,128)(2,1)S(1)}, bf16[512,256]{1,0:T(8,128)(2,1)S(1)}, u32[]{:S(2)}, u32[]{:S(2)}) collective-permute-start(bf16[512,256]{1,0:T(8,128)(2,1)S(1)} %bitcast.18), channel_id=1, source_target_pairs={{0,1},{1,0},{2,3},{3,2},{4,5},{5,4},{6,7},{7,6},{8,9},{9,8},{10,11... | collective-permute-start | bytes 786440 | tf_op jit(solution)/shard_map/ppermute | solution.py:366
  94.5 0.9 collective-permute-done.8.n2
  95.4 4.2 %collective-permute-start.9 = (bf16[512,256]{1,0:T(8,128)(2,1)S(1)}, bf16[512,256]{1,0:T(8,128)(2,1)S(1)}, u32[]{:S(2)}, u32[]{:S(2)}) collective-permute-start(bf16[512,256]{1,0:T(8,128)(2,1)S(1)} %collective-permute-done.8.n2), channel_id=1, source_target_pairs={{0,1},{1,0},{2,3},{3,2},{4,5},{5,4},{6,7},{7,6},{8,9},{9,8},{10,11... | collective-permute-start | bytes 786440 | tf_op jit(solution)/shard_map/ppermute | solution.py:366
  99.6 1.2 %collective-permute-done.9.n3 = bf16[512,256]{1,0:T(8,128)(2,1)S(1)} collective-permute-done((bf16[512,256]{1,0:T(8,128)(2,1)S(1)}, bf16[512,256]{1,0:T(8,128)(2,1)S(1)}, u32[]{:S(2)}, u32[]{:S(2)}) %collective-permute-start.9) | collective-permute-done | bytes 262176 | tf_op jit(solution)/shard_map/ppermute | solution.py:366
  100.7 3.1 %final.1 = bf16[2,4,256,512]{3,2,1,0:T(8,128)(2,1)} custom-call(s32[3]{0:T(128)S(1)} %pad_add_fusion.place, bf16[512,256]{1,0:T(8,128)(2,1)S(1)} %bitcast.19, bf16[512,256]{1,0:T(8,128)(2,1)S(1)} %collective-permute-done.7.n1, bf16[512,256]{1,0:T(8,128)(2,1)S(1)} %collective-permute-done.8.n2, bf16[512,256]{1,0:T(8,128)(2,1)S(1)} %collective-permute-done.9.n3, ...), custom_call_target="tpu_custom_call" | custom-call | tf_op jit(solution)/shard_map/final/pallas_call | solution.py:350
  (9 shorter events, 0.0 us)
Async XLA Ops:
  4.5 16.8 %collective-permute-start = (bf16[2,256,512]{2,1,0:T(8,128)(2,1)S(1)}, bf16[2,256,512]{2,1,0:T(8,128)(2,1)S(1)}, u32[]{:S(2)}, u32[]{:S(2)}) collective-permute-start(bf16[2,256,512]{2,1,0:T(8,128)(2,1)S(1)} %get-tuple-element.16), channel_id=1, source_target_pairs={{0,32},{32,0},{1,33},{33,1},{2,34},{34,2},{3,35},{35,3},{4,36},{36... | collective-permute-start | bytes 1572872 | tf_op jit(solution)/shard_map/ppermute | solution.py:366
  8.2 15.9 %collective-permute-start.2 = (bf16[2,256,512]{2,1,0:T(8,128)(2,1)}, bf16[2,256,512]{2,1,0:T(8,128)(2,1)S(1)}, u32[]{:S(2)}, u32[]{:S(2)}) collective-permute-start(bf16[2,256,512]{2,1,0:T(8,128)(2,1)} %get-tuple-element.18), channel_id=1, source_target_pairs={{0,4},{4,0},{1,5},{5,1},{2,6},{6,2},{3,7},{7,3},{8,12},{12,8},{9,1... | collective-permute-start | bytes 1572872 | tf_op jit(solution)/shard_map/ppermute | solution.py:366
  11.1 23.6 %all-to-all-start.1 = ((bf16[64,8,256]{2,1,0:T(8,128)(2,1)}), bf16[64,8,256]{2,1,0:T(8,128)(2,1)S(1)}, u32[]{:S(2)}, u32[]{:S(2)}) async-start(bf16[64,8,256]{2,1,0:T(8,128)(2,1)} %bitcast.9), calls=%async_computation.1 | async-start | bytes 524288 | tf_op jit(solution)/shard_map/all_to_all | solution.py:375
  21.4 13.9 %collective-permute-start.1 = (bf16[256,512]{1,0:T(8,128)(2,1)S(1)}, bf16[256,512]{1,0:T(8,128)(2,1)S(1)}, u32[]{:S(2)}, u32[]{:S(2)}) collective-permute-start(bf16[256,512]{1,0:T(8,128)(2,1)S(1)} %fusion), channel_id=1, source_target_pairs={{0,4},{4,0},{1,5},{5,1},{2,6},{6,2},{3,7},{7,3},{8,12},{12,8},{9,1... | collective-permute-start | bytes 786440 | tf_op jit(solution)/shard_map/ppermute | solution.py:366
  24.8 10.5 %collective-permute-start.3 = (bf16[256,512]{1,0:T(8,128)(2,1)}, bf16[256,512]{1,0:T(8,128)(2,1)S(1)}, u32[]{:S(2)}, u32[]{:S(2)}) collective-permute-start(bf16[256,512]{1,0:T(8,128)(2,1)} %fusion.1), channel_id=1, source_target_pairs={{0,32},{32,0},{1,33},{33,1},{2,34},{34,2},{3,35},{35,3},{4,36},{36... | collective-permute-start | bytes 786440 | tf_op jit(solution)/shard_map/ppermute | solution.py:366
  34.7 12.0 %collective-permute-start.5 = (bf16[8,64,256]{2,1,0:T(8,128)(2,1)S(1)}, bf16[8,64,256]{2,1,0:T(8,128)(2,1)S(1)}, u32[]{:S(2)}, u32[]{:S(2)}) collective-permute-start(bf16[8,64,256]{2,1,0:T(8,128)(2,1)S(1)} %bitcast.20), channel_id=1, source_target_pairs={{0,8},{8,0},{1,9},{9,1},{2,10},{10,2},{3,11},{11,3},{4,12},{12,4},... | collective-permute-start | bytes 786440 | tf_op jit(solution)/shard_map/ppermute | solution.py:366
  36.4 26.8 %all-to-all-start = ((bf16[64,8,512]{2,1,0:T(8,128)(2,1)}), bf16[64,8,512]{2,1,0:T(8,128)(2,1)S(1)}, u32[]{:S(2)}, u32[]{:S(2)}) async-start(bf16[64,8,512]{2,1,0:T(8,128)(2,1)} %bitcast.7), calls=%async_computation | async-start | bytes 1048576 | tf_op jit(solution)/shard_map/all_to_all | solution.py:375
  46.1 17.0 %copy-start.1 = (bf16[256,256]{1,0:T(8,128)(2,1)S(1)}, bf16[256,256]{1,0:T(8,128)(2,1)}, u32[]{:S(2)}) copy-start(bf16[256,256]{1,0:T(8,128)(2,1)} %constant.39.clone.turn_ref) | copy-start | bytes 393220
  46.1 17.0 %copy-start.2 = (bf16[256,256]{1,0:T(8,128)(2,1)S(1)}, bf16[256,256]{1,0:T(8,128)(2,1)}, u32[]{:S(2)}) copy-start(bf16[256,256]{1,0:T(8,128)(2,1)} %constant.38.clone.enter_ref) | copy-start | bytes 393220
  46.2 17.0 %copy-start.3 = (bf16[64,64]{1,0:T(8,128)(2,1)S(1)}, bf16[64,64]{1,0:T(8,128)(2,1)}, u32[]{:S(2)}) copy-start(bf16[64,64]{1,0:T(8,128)(2,1)} %constant.40.clone.leave_ref) | copy-start | bytes 24580
  46.2 1.7 %collective-permute-start.4 = (bf16[8,64,256]{2,1,0:T(8,128)(2,1)S(1)}, bf16[8,64,256]{2,1,0:T(8,128)(2,1)S(1)}, u32[]{:S(2)}, u32[]{:S(2)}) collective-permute-start(bf16[8,64,256]{2,1,0:T(8,128)(2,1)S(1)} %bitcast.21), channel_id=1, source_target_pairs={{0,1},{1,0},{2,3},{3,2},{4,5},{5,4},{6,7},{7,6},{8,9},{9,8},{10,11... | collective-permute-start | bytes 786440 | tf_op jit(solution)/shard_map/ppermute | solution.py:366
  46.7 1.5 %collective-permute-start.6 = (bf16[8,64,256]{2,1,0:T(8,128)(2,1)S(1)}, bf16[8,64,256]{2,1,0:T(8,128)(2,1)S(1)}, u32[]{:S(2)}, u32[]{:S(2)}) collective-permute-start(bf16[8,64,256]{2,1,0:T(8,128)(2,1)S(1)} %collective-permute-done.5.refs_2_.refs_6_), channel_id=1, source_target_pairs={{0,1},{1,0},{2,3},{3,2},{4,5},{5,4},{6,7},{7,6},{8,9},{9,8},{10,11... | collective-permute-start | bytes 786440 | tf_op jit(solution)/shard_map/ppermute | solution.py:366
  63.1 37.6 %copy-start = (bf16[4,256,256]{2,1,0:T(8,128)(2,1)S(1)}, bf16[4,256,256]{2,1,0:T(8,128)(2,1)}, u32[]{:S(2)}) copy-start(bf16[4,256,256]{2,1,0:T(8,128)(2,1)} %constant.41.clone.pick_ref) | copy-start | bytes 1572868
  90.2 5.2 %collective-permute-start.8 = (bf16[512,256]{1,0:T(8,128)(2,1)S(1)}, bf16[512,256]{1,0:T(8,128)(2,1)S(1)}, u32[]{:S(2)}, u32[]{:S(2)}) collective-permute-start(bf16[512,256]{1,0:T(8,128)(2,1)S(1)} %bitcast.17), channel_id=1, source_target_pairs={{0,8},{8,0},{1,9},{9,1},{2,10},{10,2},{3,11},{11,3},{4,12},{12,4},... | collective-permute-start | bytes 786440 | tf_op jit(solution)/shard_map/ppermute | solution.py:366
  91.1 8.4 %collective-permute-start.7 = (bf16[512,256]{1,0:T(8,128)(2,1)S(1)}, bf16[512,256]{1,0:T(8,128)(2,1)S(1)}, u32[]{:S(2)}, u32[]{:S(2)}) collective-permute-start(bf16[512,256]{1,0:T(8,128)(2,1)S(1)} %bitcast.18), channel_id=1, source_target_pairs={{0,1},{1,0},{2,3},{3,2},{4,5},{5,4},{6,7},{7,6},{8,9},{9,8},{10,11... | collective-permute-start | bytes 786440 | tf_op jit(solution)/shard_map/ppermute | solution.py:366
  95.4 5.3 %collective-permute-start.9 = (bf16[512,256]{1,0:T(8,128)(2,1)S(1)}, bf16[512,256]{1,0:T(8,128)(2,1)S(1)}, u32[]{:S(2)}, u32[]{:S(2)}) collective-permute-start(bf16[512,256]{1,0:T(8,128)(2,1)S(1)} %collective-permute-done.8.n2), channel_id=1, source_target_pairs={{0,1},{1,0},{2,3},{3,2},{4,5},{5,4},{6,7},{7,6},{8,9},{9,8},{10,11... | collective-permute-start | bytes 786440 | tf_op jit(solution)/shard_map/ppermute | solution.py:366

commit v7 on v6

--- a/solution.py
+++ b/solution.py
@@ -167,6 +167,21 @@
     return (a.astype(F32) + b.astype(F32)).astype(BF)
 
 
+def first_kernel(kept, come, out_ref):
+    out_ref[...] = add(kept[0], come[0])
+
+
+def first_sum(kept, come):
+    return pl.pallas_call(
+        first_kernel,
+        out_shape=jax.ShapeDtypeStruct((256, CHEB), BF),
+        in_specs=[pl.BlockSpec(memory_space=pltpu.VMEM)] * 2,
+        out_specs=pl.BlockSpec(memory_space=pltpu.VMEM),
+        compiler_params=params(8),
+        name="first_sum",
+    )(kept, come)
+
+
 def sum_kernel(keep0, come0, again0, keep1, come1, again1, out_ref):
     for half, (kept, come, again) in enumerate(((keep0, come0, again0), (keep1, come1, again1))):
         out_ref[half] = add(add(kept[1], come[1]), again[...])
@@ -384,11 +399,11 @@
     send0, send1, keep0, keep1, phases = rotate(place, weights, angles)
     come0, come1 = swap(send0, "y4"), swap(send1, "z4")
     phases = exchange(phases.reshape(64, 8, HALF), ("x4", "y4", "z4", "x3", "y3", "z3"))
-    again0, again1 = add(keep0[0], come0[0]), add(keep1[0], come1[0])
-    phases, _, _ = lax.optimization_barrier((phases, again0, again1))
-    near = four(phases.reshape(8, 64, HALF))
+    again0, again1 = first_sum(keep0, come0), first_sum(keep1, come1)
     again0, again1 = swap(again0, "z4"), swap(again1, "y4")
     share = sums(keep0, come0, again0, keep1, come1, again1)
+    phases, _ = lax.optimization_barrier((phases, share))
+    near = four(phases.reshape(8, 64, HALF))
     share = exchange(share.reshape(64, 8, CHEB), ("x4", "x3", "y3", "z3", "y2", "z2"))
     wave1, wave2 = trig(place, near)
     done, last = levels(place, share.reshape(2, 256, CHEB), translation, wave1, wave2)

time: 104 us -> 104 us (level)
    all_to_all x2, waiting for transfers between devices: 16.9 us -> 9.74 us  [exchange(): return lax.all_to_all(value, axes, split_axis=0, concat_axis=0, tiled=True)]
    ppermute x10, waiting for transfers between devices: 3.52 us -> 10.7 us  [swap(): return lax.ppermute(value, axis, [(0, 1), (1, 0)])]
  transfers between devices with their start and end apart: 12 -> 12, of which waited for: 6 -> 7; matrix products, arithmetic and copies ran while one was open for 1% -> 0% of each run, Pallas kernels for 6% -> 6%
where the time goes in v7:
time: 104 us
  starting transfers between devices  42.1 us (40%)
  blocking collectives  21 us (20%)
  waiting for transfers between devices  20.4 us (20%)
  Pallas kernels  19.8 us (19%)
    ppermute x10, starting transfers between devices, swap(): return lax.ppermute(value, axis, [(0, 1), (1, 0)])  21.8 us
    all_to_all x1, blocking collectives, exchange(): return lax.all_to_all(value, axes, split_axis=0, concat_axis=0, tiled=True)  21 us
    all_to_all x2, starting transfers between devices, exchange(): return lax.all_to_all(value, axes, split_axis=0, concat_axis=0, tiled=True)  20.4 us
    ppermute x10, waiting for transfers between devices, swap(): return lax.ppermute(value, axis, [(0, 1), (1, 0)])  10.7 us
    all_to_all x2, waiting for transfers between devices, exchange(): return lax.all_to_all(value, axes, split_axis=0, concat_axis=0, tiled=True)  9.74 us
    pallas_call x1, Pallas kernels, levels(): pl.pallas_call(levels_kernel, out_shape=[jax.ShapeDtypeStruct((8, 8, 8, H...  5.92 us
    pallas_call x1, Pallas kernels, trig(): pl.pallas_call(trig_kernel, grid_spec=spec, out_shape=[jax.ShapeDtypeStru...  5.12 us
    pallas_call x1, Pallas kernels, rotate(): pl.pallas_call(rotate_kernel, out_shape=[piece] * 4 + [jax.ShapeDtypeStru...  4.44 us
  transfers between devices with their start and end apart: 12, of which 7 were waited for; matrix products, arithmetic and copies ran while one was open for 0% of the time, Pallas kernels for 6%

profile of v7, /device:TPU:1, one launch (start us, length us, event | category | flops | bytes accessed | tf_op | source)
XLA Modules:
  0.0 103.7 jit_solution(9041324699212879162)
XLA Ops:
  0.0 0.1 pad_add_fusion.place
  0.1 4.4 %rotate.1 = (bf16[2,256,512]{2,1,0:T(8,128)(2,1)}, bf16[2,256,512]{2,1,0:T(8,128)(2,1)S(1)}, bf16[2,256,512]{2,1,0:T(8,128)(2,1)S(1)}, bf16[2,256,512]{2,1,0:T(8,128)(2,1)S(1)}, bf16[2,4,64,256]{3,2,1,0:T(8,128)(2,1)}) custom-call(s32[3]{0:T(128)S(1)} %pad_add_fusion.place, bf16[2,4,256,512]{3,2,1,0:T(8,128)(2,1)} %bitcast.21, ...), custom_call_target="tpu_custom_call" | custom-call | tf_op jit(solution)/shard_map/rotate/pallas_call | solution.py:145
  4.5 3.7 %collective-permute-start = (bf16[2,256,512]{2,1,0:T(8,128)(2,1)}, bf16[2,256,512]{2,1,0:T(8,128)(2,1)S(1)}, u32[]{:S(2)}, u32[]{:S(2)}) collective-permute-start(bf16[2,256,512]{2,1,0:T(8,128)(2,1)} %get-tuple-element.16), channel_id=1, source_target_pairs={{0,32},{32,0},{1,33},{33,1},{2,34},{34,2},{3,35},{35,3},{4,36},{36... | collective-permute-start | bytes 1572872 | tf_op jit(solution)/shard_map/ppermute | solution.py:381
  8.2 2.9 %collective-permute-start.2 = (bf16[2,256,512]{2,1,0:T(8,128)(2,1)S(1)}, bf16[2,256,512]{2,1,0:T(8,128)(2,1)S(1)}, u32[]{:S(2)}, u32[]{:S(2)}) collective-permute-start(bf16[2,256,512]{2,1,0:T(8,128)(2,1)S(1)} %get-tuple-element.18), channel_id=1, source_target_pairs={{0,4},{4,0},{1,5},{5,1},{2,6},{6,2},{3,7},{7,3},{8,12},{12,8},{9,1... | collective-permute-start | bytes 1572872 | tf_op jit(solution)/shard_map/ppermute | solution.py:381
  11.1 10.3 %all-to-all-start.1 = ((bf16[64,8,256]{2,1,0:T(8,128)(2,1)}), bf16[64,8,256]{2,1,0:T(8,128)(2,1)S(1)}, u32[]{:S(2)}, u32[]{:S(2)}) async-start(bf16[64,8,256]{2,1,0:T(8,128)(2,1)} %bitcast.7), calls=%async_computation.1 | async-start | bytes 524288 | tf_op jit(solution)/shard_map/all_to_all | solution.py:390
  21.4 0.1 first_sum.2
  21.5 2.6 %collective-permute-start.1 = (bf16[256,512]{1,0:T(8,128)(2,1)S(1)}, bf16[256,512]{1,0:T(8,128)(2,1)S(1)}, u32[]{:S(2)}, u32[]{:S(2)}) collective-permute-start(bf16[256,512]{1,0:T(8,128)(2,1)S(1)} %first_sum.2), channel_id=1, source_target_pairs={{0,4},{4,0},{1,5},{5,1},{2,6},{6,2},{3,7},{7,3},{8,12},{12,8},{9,1... | collective-permute-start | bytes 786440 | tf_op jit(solution)/shard_map/ppermute | solution.py:381
  24.1 0.1 first_sum.3
  24.1 2.8 %collective-permute-start.3 = (bf16[256,512]{1,0:T(8,128)(2,1)S(1)}, bf16[256,512]{1,0:T(8,128)(2,1)S(1)}, u32[]{:S(2)}, u32[]{:S(2)}) collective-permute-start(bf16[256,512]{1,0:T(8,128)(2,1)S(1)} %first_sum.3), channel_id=1, source_target_pairs={{0,32},{32,0},{1,33},{33,1},{2,34},{34,2},{3,35},{35,3},{4,36},{36... | collective-permute-start | bytes 786440 | tf_op jit(solution)/shard_map/ppermute | solution.py:381
  26.9 4.3 %collective-permute-done.1.again0 = bf16[256,512]{1,0:T(8,128)(2,1)S(1)} collective-permute-done((bf16[256,512]{1,0:T(8,128)(2,1)S(1)}, bf16[256,512]{1,0:T(8,128)(2,1)S(1)}, u32[]{:S(2)}, u32[]{:S(2)}) %collective-permute-start.1) | collective-permute-done | bytes 262176 | tf_op jit(solution)/shard_map/ppermute | solution.py:381
  31.3 2.9 %collective-permute-done.3.again1 = bf16[256,512]{1,0:T(8,128)(2,1)S(1)} collective-permute-done((bf16[256,512]{1,0:T(8,128)(2,1)S(1)}, bf16[256,512]{1,0:T(8,128)(2,1)S(1)}, u32[]{:S(2)}, u32[]{:S(2)}) %collective-permute-start.3) | collective-permute-done | bytes 262176 | tf_op jit(solution)/shard_map/ppermute | solution.py:381
  34.1 1.0 sums.1
  35.2 0.6 collective-permute-start.5
  35.7 10.1 %all-to-all-start = ((bf16[64,8,512]{2,1,0:T(8,128)(2,1)}), bf16[64,8,512]{2,1,0:T(8,128)(2,1)S(1)}, u32[]{:S(2)}, u32[]{:S(2)}) async-start(bf16[64,8,512]{2,1,0:T(8,128)(2,1)} %bitcast.5), calls=%async_computation | async-start | bytes 1048576 | tf_op jit(solution)/shard_map/all_to_all | solution.py:390
  45.9 0.0 copy-start.1
  45.9 0.0 copy-start.2
  45.9 0.0 copy-start.3
  45.9 0.5 collective-permute-start.4
  46.4 0.1 collective-permute-start.6
  46.5 1.1 %collective-permute-done.4.refs_1_.refs_5_ = bf16[8,64,256]{2,1,0:T(8,128)(2,1)S(1)} collective-permute-done((bf16[8,64,256]{2,1,0:T(8,128)(2,1)S(1)}, bf16[8,64,256]{2,1,0:T(8,128)(2,1)S(1)}, u32[]{:S(2)}, u32[]{:S(2)}) %collective-permute-start.4) | collective-permute-done | bytes 262176 | tf_op jit(solution)/shard_map/ppermute | solution.py:381
  47.6 0.4 collective-permute-done.6.refs_3_.refs_7_
  48.0 5.1 %trig.1 = (f32[8,2,64,512]{3,2,1,0:T(8,128)S(1)}, f32[8,2,64,512]{3,2,1,0:T(8,128)}) custom-call(s32[3]{0:T(128)S(1)} %pad_add_fusion.place, bf16[8,64,256]{2,1,0:T(8,128)(2,1)S(1)} %bitcast.18, bf16[8,64,256]{2,1,0:T(8,128)(2,1)S(1)} %collective-permute-done.4.refs_1_.refs_5_, bf16[8,64,256]{2,1,0:T(8,128)(2,1)S(1)} %collective-permute-done.5.refs_2_.refs_6_, ...), custom_call_target="tpu_custom_call" | custom-call | flops 7000000000 | bytes 1000000 | tf_op jit(solution)/shard_map/trig/pallas_call | solution.py:241
  53.1 9.7 %all-to-all-done = bf16[64,8,512]{2,1,0:T(8,128)(2,1)S(1)} async-done(((bf16[64,8,512]{2,1,0:T(8,128)(2,1)}), bf16[64,8,512]{2,1,0:T(8,128)(2,1)S(1)}, u32[]{:S(2)}, u32[]{:S(2)}) %all-to-all-start) | async-done | bytes 524320 | tf_op jit(solution)/shard_map/all_to_all | solution.py:390
  62.8 0.0 copy-start
  62.9 5.9 %levels.1 = (bf16[8,8,8,256]{3,2,1,0:T(8,128)(2,1)S(1)}, bf16[2,512,512]{2,1,0:T(8,128)(2,1)S(1)}) custom-call(s32[3]{0:T(128)S(1)} %pad_add_fusion.place, bf16[2,256,512]{2,1,0:T(8,128)(2,1)S(1)} %bitcast.12, bf16[8,512,512]{2,1,0:T(8,128)(2,1)} %t_hbm.1, f32[8,2,64,512]{3,2,1,0:T(8,128)S(1)} %get-tuple-element.21.wave1_ref, ...), custom_call_target="tpu_custom_call" | custom-call | tf_op jit(solution)/shard_map/levels/pallas_call | solution.py:312
  68.8 21.0 %all_to_all.15 = bf16[64,8,256]{2,1,0:T(8,128)(2,1)S(1)} all-to-all(bf16[64,8,256]{2,1,0:T(8,128)(2,1)S(1)} %bitcast.20), channel_id=1, replica_groups=mesh['x4'=2,'x3'=2,'y4'=2,'y3'=2,'y2'=2,'z4'=2,'z3'=2,'z2'=2] {'y4','z4'..., dimensions={0} | all-to-all | bytes 524288 | tf_op jit(solution)/shard_map/all_to_all | solution.py:390
  89.8 1.0 collective-permute-start.8
  90.8 3.3 %collective-permute-start.7 = (bf16[512,256]{1,0:T(8,128)(2,1)S(1)}, bf16[512,256]{1,0:T(8,128)(2,1)S(1)}, u32[]{:S(2)}, u32[]{:S(2)}) collective-permute-start(bf16[512,256]{1,0:T(8,128)(2,1)S(1)} %bitcast.14), channel_id=1, source_target_pairs={{0,1},{1,0},{2,3},{3,2},{4,5},{5,4},{6,7},{7,6},{8,9},{9,8},{10,11... | collective-permute-start | bytes 786440 | tf_op jit(solution)/shard_map/ppermute | solution.py:381
  94.2 0.9 collective-permute-done.8.n2
  95.0 4.2 %collective-permute-start.9 = (bf16[512,256]{1,0:T(8,128)(2,1)S(1)}, bf16[512,256]{1,0:T(8,128)(2,1)S(1)}, u32[]{:S(2)}, u32[]{:S(2)}) collective-permute-start(bf16[512,256]{1,0:T(8,128)(2,1)S(1)} %collective-permute-done.8.n2), channel_id=1, source_target_pairs={{0,1},{1,0},{2,3},{3,2},{4,5},{5,4},{6,7},{7,6},{8,9},{9,8},{10,11... | collective-permute-start | bytes 786440 | tf_op jit(solution)/shard_map/ppermute | solution.py:381
  99.3 1.2 %collective-permute-done.9.n3 = bf16[512,256]{1,0:T(8,128)(2,1)S(1)} collective-permute-done((bf16[512,256]{1,0:T(8,128)(2,1)S(1)}, bf16[512,256]{1,0:T(8,128)(2,1)S(1)}, u32[]{:S(2)}, u32[]{:S(2)}) %collective-permute-start.9) | collective-permute-done | bytes 262176 | tf_op jit(solution)/shard_map/ppermute | solution.py:381
  100.4 3.1 %final.1 = bf16[2,4,256,512]{3,2,1,0:T(8,128)(2,1)} custom-call(s32[3]{0:T(128)S(1)} %pad_add_fusion.place, bf16[512,256]{1,0:T(8,128)(2,1)S(1)} %bitcast.15, bf16[512,256]{1,0:T(8,128)(2,1)S(1)} %collective-permute-done.7.n1, bf16[512,256]{1,0:T(8,128)(2,1)S(1)} %collective-permute-done.8.n2, bf16[512,256]{1,0:T(8,128)(2,1)S(1)} %collective-permute-done.9.n3, ...), custom_call_target="tpu_custom_call" | custom-call | tf_op jit(solution)/shard_map/final/pallas_call | solution.py:365
  (9 shorter events, 0.0 us)
Async XLA Ops:
  4.5 16.8 %collective-permute-start = (bf16[2,256,512]{2,1,0:T(8,128)(2,1)}, bf16[2,256,512]{2,1,0:T(8,128)(2,1)S(1)}, u32[]{:S(2)}, u32[]{:S(2)}) collective-permute-start(bf16[2,256,512]{2,1,0:T(8,128)(2,1)} %get-tuple-element.16), channel_id=1, source_target_pairs={{0,32},{32,0},{1,33},{33,1},{2,34},{34,2},{3,35},{35,3},{4,36},{36... | collective-permute-start | bytes 1572872 | tf_op jit(solution)/shard_map/ppermute | solution.py:381
  8.2 15.9 %collective-permute-start.2 = (bf16[2,256,512]{2,1,0:T(8,128)(2,1)S(1)}, bf16[2,256,512]{2,1,0:T(8,128)(2,1)S(1)}, u32[]{:S(2)}, u32[]{:S(2)}) collective-permute-start(bf16[2,256,512]{2,1,0:T(8,128)(2,1)S(1)} %get-tuple-element.18), channel_id=1, source_target_pairs={{0,4},{4,0},{1,5},{5,1},{2,6},{6,2},{3,7},{7,3},{8,12},{12,8},{9,1... | collective-permute-start | bytes 1572872 | tf_op jit(solution)/shard_map/ppermute | solution.py:381
  11.1 24.1 %all-to-all-start.1 = ((bf16[64,8,256]{2,1,0:T(8,128)(2,1)}), bf16[64,8,256]{2,1,0:T(8,128)(2,1)S(1)}, u32[]{:S(2)}, u32[]{:S(2)}) async-start(bf16[64,8,256]{2,1,0:T(8,128)(2,1)} %bitcast.7), calls=%async_computation.1 | async-start | bytes 524288 | tf_op jit(solution)/shard_map/all_to_all | solution.py:390
  21.5 9.8 %collective-permute-start.1 = (bf16[256,512]{1,0:T(8,128)(2,1)S(1)}, bf16[256,512]{1,0:T(8,128)(2,1)S(1)}, u32[]{:S(2)}, u32[]{:S(2)}) collective-permute-start(bf16[256,512]{1,0:T(8,128)(2,1)S(1)} %first_sum.2), channel_id=1, source_target_pairs={{0,4},{4,0},{1,5},{5,1},{2,6},{6,2},{3,7},{7,3},{8,12},{12,8},{9,1... | collective-permute-start | bytes 786440 | tf_op jit(solution)/shard_map/ppermute | solution.py:381
  24.1 10.0 %collective-permute-start.3 = (bf16[256,512]{1,0:T(8,128)(2,1)S(1)}, bf16[256,512]{1,0:T(8,128)(2,1)S(1)}, u32[]{:S(2)}, u32[]{:S(2)}) collective-permute-start(bf16[256,512]{1,0:T(8,128)(2,1)S(1)} %first_sum.3), channel_id=1, source_target_pairs={{0,32},{32,0},{1,33},{33,1},{2,34},{34,2},{3,35},{35,3},{4,36},{36... | collective-permute-start | bytes 786440 | tf_op jit(solution)/shard_map/ppermute | solution.py:381
  35.2 11.3 %collective-permute-start.5 = (bf16[8,64,256]{2,1,0:T(8,128)(2,1)S(1)}, bf16[8,64,256]{2,1,0:T(8,128)(2,1)S(1)}, u32[]{:S(2)}, u32[]{:S(2)}) collective-permute-start(bf16[8,64,256]{2,1,0:T(8,128)(2,1)S(1)} %bitcast.16), channel_id=1, source_target_pairs={{0,8},{8,0},{1,9},{9,1},{2,10},{10,2},{3,11},{11,3},{4,12},{12,4},... | collective-permute-start | bytes 786440 | tf_op jit(solution)/shard_map/ppermute | solution.py:381
  35.7 27.1 %all-to-all-start = ((bf16[64,8,512]{2,1,0:T(8,128)(2,1)}), bf16[64,8,512]{2,1,0:T(8,128)(2,1)S(1)}, u32[]{:S(2)}, u32[]{:S(2)}) async-start(bf16[64,8,512]{2,1,0:T(8,128)(2,1)} %bitcast.5), calls=%async_computation | async-start | bytes 1048576 | tf_op jit(solution)/shard_map/all_to_all | solution.py:390
  45.9 17.0 %copy-start.1 = (bf16[256,256]{1,0:T(8,128)(2,1)S(1)}, bf16[256,256]{1,0:T(8,128)(2,1)}, u32[]{:S(2)}) copy-start(bf16[256,256]{1,0:T(8,128)(2,1)} %constant.39.clone.turn_ref) | copy-start | bytes 393220
  45.9 17.0 %copy-start.2 = (bf16[256,256]{1,0:T(8,128)(2,1)S(1)}, bf16[256,256]{1,0:T(8,128)(2,1)}, u32[]{:S(2)}) copy-start(bf16[256,256]{1,0:T(8,128)(2,1)} %constant.38.clone.enter_ref) | copy-start | bytes 393220
  45.9 17.0 %copy-start.3 = (bf16[64,64]{1,0:T(8,128)(2,1)S(1)}, bf16[64,64]{1,0:T(8,128)(2,1)}, u32[]{:S(2)}) copy-start(bf16[64,64]{1,0:T(8,128)(2,1)} %constant.40.clone.leave_ref) | copy-start | bytes 24580
  45.9 1.7 %collective-permute-start.4 = (bf16[8,64,256]{2,1,0:T(8,128)(2,1)S(1)}, bf16[8,64,256]{2,1,0:T(8,128)(2,1)S(1)}, u32[]{:S(2)}, u32[]{:S(2)}) collective-permute-start(bf16[8,64,256]{2,1,0:T(8,128)(2,1)S(1)} %bitcast.17), channel_id=1, source_target_pairs={{0,1},{1,0},{2,3},{3,2},{4,5},{5,4},{6,7},{7,6},{8,9},{9,8},{10,11... | collective-permute-start | bytes 786440 | tf_op jit(solution)/shard_map/ppermute | solution.py:381
  46.4 1.5 %collective-permute-start.6 = (bf16[8,64,256]{2,1,0:T(8,128)(2,1)S(1)}, bf16[8,64,256]{2,1,0:T(8,128)(2,1)S(1)}, u32[]{:S(2)}, u32[]{:S(2)}) collective-permute-start(bf16[8,64,256]{2,1,0:T(8,128)(2,1)S(1)} %collective-permute-done.5.refs_2_.refs_6_), channel_id=1, source_target_pairs={{0,1},{1,0},{2,3},{3,2},{4,5},{5,4},{6,7},{7,6},{8,9},{9,8},{10,11... | collective-permute-start | bytes 786440 | tf_op jit(solution)/shard_map/ppermute | solution.py:381
  62.8 37.6 %copy-start = (bf16[4,256,256]{2,1,0:T(8,128)(2,1)S(1)}, bf16[4,256,256]{2,1,0:T(8,128)(2,1)}, u32[]{:S(2)}) copy-start(bf16[4,256,256]{2,1,0:T(8,128)(2,1)} %constant.41.clone.pick_ref) | copy-start | bytes 1572868
  89.8 5.2 %collective-permute-start.8 = (bf16[512,256]{1,0:T(8,128)(2,1)S(1)}, bf16[512,256]{1,0:T(8,128)(2,1)S(1)}, u32[]{:S(2)}, u32[]{:S(2)}) collective-permute-start(bf16[512,256]{1,0:T(8,128)(2,1)S(1)} %bitcast.13), channel_id=1, source_target_pairs={{0,8},{8,0},{1,9},{9,1},{2,10},{10,2},{3,11},{11,3},{4,12},{12,4},... | collective-permute-start | bytes 786440 | tf_op jit(solution)/shard_map/ppermute | solution.py:381
  90.8 8.4 %collective-permute-start.7 = (bf16[512,256]{1,0:T(8,128)(2,1)S(1)}, bf16[512,256]{1,0:T(8,128)(2,1)S(1)}, u32[]{:S(2)}, u32[]{:S(2)}) collective-permute-start(bf16[512,256]{1,0:T(8,128)(2,1)S(1)} %bitcast.14), channel_id=1, source_target_pairs={{0,1},{1,0},{2,3},{3,2},{4,5},{5,4},{6,7},{7,6},{8,9},{9,8},{10,11... | collective-permute-start | bytes 786440 | tf_op jit(solution)/shard_map/ppermute | solution.py:381
  95.0 5.4 %collective-permute-start.9 = (bf16[512,256]{1,0:T(8,128)(2,1)S(1)}, bf16[512,256]{1,0:T(8,128)(2,1)S(1)}, u32[]{:S(2)}, u32[]{:S(2)}) collective-permute-start(bf16[512,256]{1,0:T(8,128)(2,1)S(1)} %collective-permute-done.8.n2), channel_id=1, source_target_pairs={{0,1},{1,0},{2,3},{3,2},{4,5},{5,4},{6,7},{7,6},{8,9},{9,8},{10,11... | collective-permute-start | bytes 786440 | tf_op jit(solution)/shard_map/ppermute | solution.py:381

commit v8 on v7

--- a/solution.py
+++ b/solution.py
@@ -290,19 +290,15 @@
         copy.start()
     left[...] = dot(turn_ref[...], middle[...]).astype(BF)
 
-    def four_orientations(group, carry):
-        even[...] = dot(left[...], t_ref[4 * group])
-        for i in range(4):
-            if i < 3:
-                slots[(i + 1) % 2][...] = dot(left[...], t_ref[4 * group + i + 1])
-            value = turn_and_sum(slots[i % 2], wave2_ref, 4 * group + i)
-            value = jnp.concatenate([value[:, :HALF], value[:, HALF:]], axis=0)
-            value = dot(leave_ref[...], value)
-            for t4 in range(8):
-                out_ref[t4, 4 * group + i] = value[8 * t4 : 8 * t4 + 8].astype(BF)
-        return carry
-
-    lax.fori_loop(0, 2, four_orientations, 0)
+    even[...] = dot(left[...], t_ref[0])
+    for t in range(8):
+        if t < 7:
+            slots[(t + 1) % 2][...] = dot(left[...], t_ref[t + 1])
+        value = turn_and_sum(slots[t % 2], wave2_ref, t)
+        value = jnp.concatenate([value[:, :HALF], value[:, HALF:]], axis=0)
+        value = dot(leave_ref[...], value)
+        for t4 in range(8):
+            out_ref[t4, t] = value[8 * t4 : 8 * t4 + 8].astype(BF)
     for copy in kept:
         copy.wait()
 
@@ -343,17 +339,19 @@
 def final_kernel(place, n0, n1, n2, n3, pick_ref, t_ref, out_ref, left, made, sems):
     own = place[2]
     copies = []
-    for block in range(4):
-        for high in range(2):
-            at = 128 * block + 64 * high
-            held = jnp.concatenate([r[at : at + 64] for r in (n0, n1, n2, n3)], axis=0)
-            value = dot(pick_ref[own], held)
-            value = jnp.concatenate([value[:128], value[128:]], axis=1)
-            left[block, 128 * high : 128 * high + 128, :] = value.astype(BF)
+    for group in range(2):
+        for block in range(2 * group, 2 * group + 2):
+            for high in range(2):
+                at = 128 * block + 64 * high
+                held = jnp.concatenate([r[at : at + 64] for r in (n0, n1, n2, n3)], axis=0)
+                value = dot(pick_ref[own], held)
+                value = jnp.concatenate([value[:128], value[128:]], axis=1)
+                left[256 * block + 128 * high : 256 * block + 128 * high + 128, :] = value.astype(BF)
+        rows = slice(512 * group, 512 * group + 512)
         for x2 in range(2):
-            made[x2, block] = dot(left[block], t_ref[x2]).astype(BF)
+            made[x2, rows] = dot(left[rows], t_ref[x2]).astype(BF)
             copies.append(
-                pltpu.make_async_copy(made.at[x2, block], out_ref.at[x2, block], sems.at[x2, block])
+                pltpu.make_async_copy(made.at[x2, rows], out_ref.at[x2, rows], sems.at[x2, group])
             )
             copies[-1].start()
     for copy in copies:
@@ -364,12 +362,12 @@
     vmem = pl.BlockSpec(memory_space=pltpu.VMEM)
     return pl.pallas_call(
         final_kernel,
-        out_shape=jax.ShapeDtypeStruct((2, 4, 256, CHEB), BF),
+        out_shape=jax.ShapeDtypeStruct((2, 1024, CHEB), BF),
         in_specs=[pl.BlockSpec(memory_space=pltpu.SMEM)] + [vmem] * 6,
         out_specs=pl.BlockSpec(memory_space=pl.ANY),
         scratch_shapes=[
-            pltpu.VMEM((4, 256, CHEB), BF),
-            pltpu.VMEM((2, 4, 256, CHEB), BF),
+            pltpu.VMEM((1024, CHEB), BF),
+            pltpu.VMEM((2, 1024, CHEB), BF),
             pltpu.SemaphoreType.DMA((2, 4)),
         ],
         compiler_params=params(14),

time: 104 us -> 104 us (level)
  no operation moved by 1% of the time
where the time goes in v8:
time: 104 us; the launch traced here: 103 us
  starting transfers between devices  42.1 us (40%)
  blocking collectives  21.2 us (20%)
  waiting for transfers between devices  20.4 us (20%)
  Pallas kernels  19.2 us (18%)
    ppermute x10, starting transfers between devices, swap(): return lax.ppermute(value, axis, [(0, 1), (1, 0)])  21.7 us
    all_to_all x1, blocking collectives, exchange(): return lax.all_to_all(value, axes, split_axis=0, concat_axis=0, tiled=True)  21.2 us
    all_to_all x2, starting transfers between devices, exchange(): return lax.all_to_all(value, axes, split_axis=0, concat_axis=0, tiled=True)  20.4 us
    ppermute x10, waiting for transfers between devices, swap(): return lax.ppermute(value, axis, [(0, 1), (1, 0)])  10.7 us
    all_to_all x2, waiting for transfers between devices, exchange(): return lax.all_to_all(value, axes, split_axis=0, concat_axis=0, tiled=True)  9.74 us
    pallas_call x1, Pallas kernels, levels(): pl.pallas_call(levels_kernel, out_shape=[jax.ShapeDtypeStruct((8, 8, 8, H...  5.53 us
    pallas_call x1, Pallas kernels, trig(): pl.pallas_call(trig_kernel, grid_spec=spec, out_shape=[jax.ShapeDtypeStru...  5.12 us
    pallas_call x1, Pallas kernels, rotate(): pl.pallas_call(rotate_kernel, out_shape=[piece] * 4 + [jax.ShapeDtypeStru...  4.44 us
  transfers between devices with their start and end apart: 12, of which 7 were waited for; matrix products, arithmetic and copies ran while one was open for 0% of the time, Pallas kernels for 6%

profile of v8, /device:TPU:1, one launch (start us, length us, event | category | flops | bytes accessed | tf_op | source)
XLA Modules:
  0.0 103.3 jit_solution(12568171864686864506)
XLA Ops:
  0.0 0.1 pad_add_fusion.place
  0.1 4.4 %rotate.1 = (bf16[2,256,512]{2,1,0:T(8,128)(2,1)}, bf16[2,256,512]{2,1,0:T(8,128)(2,1)S(1)}, bf16[2,256,512]{2,1,0:T(8,128)(2,1)S(1)}, bf16[2,256,512]{2,1,0:T(8,128)(2,1)S(1)}, bf16[2,4,64,256]{3,2,1,0:T(8,128)(2,1)}) custom-call(s32[3]{0:T(128)S(1)} %pad_add_fusion.place, bf16[2,4,256,512]{3,2,1,0:T(8,128)(2,1)} %bitcast.21, ...), custom_call_target="tpu_custom_call" | custom-call | tf_op jit(solution)/shard_map/rotate/pallas_call | solution.py:145
  4.5 3.7 %collective-permute-start = (bf16[2,256,512]{2,1,0:T(8,128)(2,1)}, bf16[2,256,512]{2,1,0:T(8,128)(2,1)S(1)}, u32[]{:S(2)}, u32[]{:S(2)}) collective-permute-start(bf16[2,256,512]{2,1,0:T(8,128)(2,1)} %get-tuple-element.16), channel_id=1, source_target_pairs={{0,32},{32,0},{1,33},{33,1},{2,34},{34,2},{3,35},{35,3},{4,36},{36... | collective-permute-start | bytes 1572872 | tf_op jit(solution)/shard_map/ppermute | solution.py:379
  8.2 2.9 %collective-permute-start.2 = (bf16[2,256,512]{2,1,0:T(8,128)(2,1)S(1)}, bf16[2,256,512]{2,1,0:T(8,128)(2,1)S(1)}, u32[]{:S(2)}, u32[]{:S(2)}) collective-permute-start(bf16[2,256,512]{2,1,0:T(8,128)(2,1)S(1)} %get-tuple-element.18), channel_id=1, source_target_pairs={{0,4},{4,0},{1,5},{5,1},{2,6},{6,2},{3,7},{7,3},{8,12},{12,8},{9,1... | collective-permute-start | bytes 1572872 | tf_op jit(solution)/shard_map/ppermute | solution.py:379
  11.1 10.3 %all-to-all-start.1 = ((bf16[64,8,256]{2,1,0:T(8,128)(2,1)}), bf16[64,8,256]{2,1,0:T(8,128)(2,1)S(1)}, u32[]{:S(2)}, u32[]{:S(2)}) async-start(bf16[64,8,256]{2,1,0:T(8,128)(2,1)} %bitcast.7), calls=%async_computation.1 | async-start | bytes 524288 | tf_op jit(solution)/shard_map/all_to_all | solution.py:388
  21.4 0.1 first_sum.2
  21.5 2.6 %collective-permute-start.1 = (bf16[256,512]{1,0:T(8,128)(2,1)S(1)}, bf16[256,512]{1,0:T(8,128)(2,1)S(1)}, u32[]{:S(2)}, u32[]{:S(2)}) collective-permute-start(bf16[256,512]{1,0:T(8,128)(2,1)S(1)} %first_sum.2), channel_id=1, source_target_pairs={{0,4},{4,0},{1,5},{5,1},{2,6},{6,2},{3,7},{7,3},{8,12},{12,8},{9,1... | collective-permute-start | bytes 786440 | tf_op jit(solution)/shard_map/ppermute | solution.py:379
  24.1 0.1 first_sum.3
  24.1 2.8 %collective-permute-start.3 = (bf16[256,512]{1,0:T(8,128)(2,1)S(1)}, bf16[256,512]{1,0:T(8,128)(2,1)S(1)}, u32[]{:S(2)}, u32[]{:S(2)}) collective-permute-start(bf16[256,512]{1,0:T(8,128)(2,1)S(1)} %first_sum.3), channel_id=1, source_target_pairs={{0,32},{32,0},{1,33},{33,1},{2,34},{34,2},{3,35},{35,3},{4,36},{36... | collective-permute-start | bytes 786440 | tf_op jit(solution)/shard_map/ppermute | solution.py:379
  26.9 4.3 %collective-permute-done.1.again0 = bf16[256,512]{1,0:T(8,128)(2,1)S(1)} collective-permute-done((bf16[256,512]{1,0:T(8,128)(2,1)S(1)}, bf16[256,512]{1,0:T(8,128)(2,1)S(1)}, u32[]{:S(2)}, u32[]{:S(2)}) %collective-permute-start.1) | collective-permute-done | bytes 262176 | tf_op jit(solution)/shard_map/ppermute | solution.py:379
  31.3 2.9 %collective-permute-done.3.again1 = bf16[256,512]{1,0:T(8,128)(2,1)S(1)} collective-permute-done((bf16[256,512]{1,0:T(8,128)(2,1)S(1)}, bf16[256,512]{1,0:T(8,128)(2,1)S(1)}, u32[]{:S(2)}, u32[]{:S(2)}) %collective-permute-start.3) | collective-permute-done | bytes 262176 | tf_op jit(solution)/shard_map/ppermute | solution.py:379
  34.1 1.0 sums.1
  35.2 0.6 collective-permute-start.5
  35.7 10.1 %all-to-all-start = ((bf16[64,8,512]{2,1,0:T(8,128)(2,1)}), bf16[64,8,512]{2,1,0:T(8,128)(2,1)S(1)}, u32[]{:S(2)}, u32[]{:S(2)}) async-start(bf16[64,8,512]{2,1,0:T(8,128)(2,1)} %bitcast.5), calls=%async_computation | async-start | bytes 1048576 | tf_op jit(solution)/shard_map/all_to_all | solution.py:388
  45.9 0.0 copy-start.1
  45.9 0.0 copy-start.2
  45.9 0.0 copy-start.3
  45.9 0.5 collective-permute-start.4
  46.4 0.1 collective-permute-start.6
  46.5 1.1 %collective-permute-done.4.refs_1_.refs_5_ = bf16[8,64,256]{2,1,0:T(8,128)(2,1)S(1)} collective-permute-done((bf16[8,64,256]{2,1,0:T(8,128)(2,1)S(1)}, bf16[8,64,256]{2,1,0:T(8,128)(2,1)S(1)}, u32[]{:S(2)}, u32[]{:S(2)}) %collective-permute-start.4) | collective-permute-done | bytes 262176 | tf_op jit(solution)/shard_map/ppermute | solution.py:379
  47.6 0.4 collective-permute-done.6.refs_3_.refs_7_
  48.0 5.1 %trig.1 = (f32[8,2,64,512]{3,2,1,0:T(8,128)S(1)}, f32[8,2,64,512]{3,2,1,0:T(8,128)}) custom-call(s32[3]{0:T(128)S(1)} %pad_add_fusion.place, bf16[8,64,256]{2,1,0:T(8,128)(2,1)S(1)} %bitcast.18, bf16[8,64,256]{2,1,0:T(8,128)(2,1)S(1)} %collective-permute-done.4.refs_1_.refs_5_, bf16[8,64,256]{2,1,0:T(8,128)(2,1)S(1)} %collective-permute-done.5.refs_2_.refs_6_, ...), custom_call_target="tpu_custom_call" | custom-call | flops 7000000000 | bytes 1000000 | tf_op jit(solution)/shard_map/trig/pallas_call | solution.py:241
  53.1 9.7 %all-to-all-done = bf16[64,8,512]{2,1,0:T(8,128)(2,1)S(1)} async-done(((bf16[64,8,512]{2,1,0:T(8,128)(2,1)}), bf16[64,8,512]{2,1,0:T(8,128)(2,1)S(1)}, u32[]{:S(2)}, u32[]{:S(2)}) %all-to-all-start) | async-done | bytes 524320 | tf_op jit(solution)/shard_map/all_to_all | solution.py:388
  62.8 0.0 copy-start
  62.9 5.5 %levels.1 = (bf16[8,8,8,256]{3,2,1,0:T(8,128)(2,1)S(1)}, bf16[2,512,512]{2,1,0:T(8,128)(2,1)S(1)}) custom-call(s32[3]{0:T(128)S(1)} %pad_add_fusion.place, bf16[2,256,512]{2,1,0:T(8,128)(2,1)S(1)} %bitcast.12, bf16[8,512,512]{2,1,0:T(8,128)(2,1)} %t_hbm.1, f32[8,2,64,512]{3,2,1,0:T(8,128)S(1)} %get-tuple-element.21.wave1_ref, ...), custom_call_target="tpu_custom_call" | custom-call | tf_op jit(solution)/shard_map/levels/pallas_call | solution.py:308
  68.4 21.2 %all_to_all.15 = bf16[64,8,256]{2,1,0:T(8,128)(2,1)S(1)} all-to-all(bf16[64,8,256]{2,1,0:T(8,128)(2,1)S(1)} %bitcast.20), channel_id=1, replica_groups=mesh['x4'=2,'x3'=2,'y4'=2,'y3'=2,'y2'=2,'z4'=2,'z3'=2,'z2'=2] {'y4','z4'..., dimensions={0} | all-to-all | bytes 524288 | tf_op jit(solution)/shard_map/all_to_all | solution.py:388
  89.6 1.0 collective-permute-start.8
  90.6 3.3 %collective-permute-start.7 = (bf16[512,256]{1,0:T(8,128)(2,1)S(1)}, bf16[512,256]{1,0:T(8,128)(2,1)S(1)}, u32[]{:S(2)}, u32[]{:S(2)}) collective-permute-start(bf16[512,256]{1,0:T(8,128)(2,1)S(1)} %bitcast.14), channel_id=1, source_target_pairs={{0,1},{1,0},{2,3},{3,2},{4,5},{5,4},{6,7},{7,6},{8,9},{9,8},{10,11... | collective-permute-start | bytes 786440 | tf_op jit(solution)/shard_map/ppermute | solution.py:379
  94.0 0.9 collective-permute-done.8.n2
  94.9 4.2 %collective-permute-start.9 = (bf16[512,256]{1,0:T(8,128)(2,1)S(1)}, bf16[512,256]{1,0:T(8,128)(2,1)S(1)}, u32[]{:S(2)}, u32[]{:S(2)}) collective-permute-start(bf16[512,256]{1,0:T(8,128)(2,1)S(1)} %collective-permute-done.8.n2), channel_id=1, source_target_pairs={{0,1},{1,0},{2,3},{3,2},{4,5},{5,4},{6,7},{7,6},{8,9},{9,8},{10,11... | collective-permute-start | bytes 786440 | tf_op jit(solution)/shard_map/ppermute | solution.py:379
  99.1 1.2 %collective-permute-done.9.n3 = bf16[512,256]{1,0:T(8,128)(2,1)S(1)} collective-permute-done((bf16[512,256]{1,0:T(8,128)(2,1)S(1)}, bf16[512,256]{1,0:T(8,128)(2,1)S(1)}, u32[]{:S(2)}, u32[]{:S(2)}) %collective-permute-start.9) | collective-permute-done | bytes 262176 | tf_op jit(solution)/shard_map/ppermute | solution.py:379
  100.2 2.9 %final.1 = bf16[2,1024,512]{2,1,0:T(8,128)(2,1)} custom-call(s32[3]{0:T(128)S(1)} %pad_add_fusion.place, bf16[512,256]{1,0:T(8,128)(2,1)S(1)} %bitcast.15, bf16[512,256]{1,0:T(8,128)(2,1)S(1)} %collective-permute-done.7.n1, bf16[512,256]{1,0:T(8,128)(2,1)S(1)} %collective-permute-done.8.n2, bf16[512,256]{1,0:T(8,128)(2,1)S(1)} %collective-permute-done.9.n3, ...), custom_call_target="tpu_custom_call" | custom-call | tf_op jit(solution)/shard_map/final/pallas_call | solution.py:363
  (9 shorter events, 0.0 us)
Async XLA Ops:
  4.5 16.8 %collective-permute-start = (bf16[2,256,512]{2,1,0:T(8,128)(2,1)}, bf16[2,256,512]{2,1,0:T(8,128)(2,1)S(1)}, u32[]{:S(2)}, u32[]{:S(2)}) collective-permute-start(bf16[2,256,512]{2,1,0:T(8,128)(2,1)} %get-tuple-element.16), channel_id=1, source_target_pairs={{0,32},{32,0},{1,33},{33,1},{2,34},{34,2},{3,35},{35,3},{4,36},{36... | collective-permute-start | bytes 1572872 | tf_op jit(solution)/shard_map/ppermute | solution.py:379
  8.2 15.9 %collective-permute-start.2 = (bf16[2,256,512]{2,1,0:T(8,128)(2,1)S(1)}, bf16[2,256,512]{2,1,0:T(8,128)(2,1)S(1)}, u32[]{:S(2)}, u32[]{:S(2)}) collective-permute-start(bf16[2,256,512]{2,1,0:T(8,128)(2,1)S(1)} %get-tuple-element.18), channel_id=1, source_target_pairs={{0,4},{4,0},{1,5},{5,1},{2,6},{6,2},{3,7},{7,3},{8,12},{12,8},{9,1... | collective-permute-start | bytes 1572872 | tf_op jit(solution)/shard_map/ppermute | solution.py:379
  11.1 24.1 %all-to-all-start.1 = ((bf16[64,8,256]{2,1,0:T(8,128)(2,1)}), bf16[64,8,256]{2,1,0:T(8,128)(2,1)S(1)}, u32[]{:S(2)}, u32[]{:S(2)}) async-start(bf16[64,8,256]{2,1,0:T(8,128)(2,1)} %bitcast.7), calls=%async_computation.1 | async-start | bytes 524288 | tf_op jit(solution)/shard_map/all_to_all | solution.py:388
  21.5 9.8 %collective-permute-start.1 = (bf16[256,512]{1,0:T(8,128)(2,1)S(1)}, bf16[256,512]{1,0:T(8,128)(2,1)S(1)}, u32[]{:S(2)}, u32[]{:S(2)}) collective-permute-start(bf16[256,512]{1,0:T(8,128)(2,1)S(1)} %first_sum.2), channel_id=1, source_target_pairs={{0,4},{4,0},{1,5},{5,1},{2,6},{6,2},{3,7},{7,3},{8,12},{12,8},{9,1... | collective-permute-start | bytes 786440 | tf_op jit(solution)/shard_map/ppermute | solution.py:379
  24.1 10.0 %collective-permute-start.3 = (bf16[256,512]{1,0:T(8,128)(2,1)S(1)}, bf16[256,512]{1,0:T(8,128)(2,1)S(1)}, u32[]{:S(2)}, u32[]{:S(2)}) collective-permute-start(bf16[256,512]{1,0:T(8,128)(2,1)S(1)} %first_sum.3), channel_id=1, source_target_pairs={{0,32},{32,0},{1,33},{33,1},{2,34},{34,2},{3,35},{35,3},{4,36},{36... | collective-permute-start | bytes 786440 | tf_op jit(solution)/shard_map/ppermute | solution.py:379
  35.2 11.3 %collective-permute-start.5 = (bf16[8,64,256]{2,1,0:T(8,128)(2,1)S(1)}, bf16[8,64,256]{2,1,0:T(8,128)(2,1)S(1)}, u32[]{:S(2)}, u32[]{:S(2)}) collective-permute-start(bf16[8,64,256]{2,1,0:T(8,128)(2,1)S(1)} %bitcast.16), channel_id=1, source_target_pairs={{0,8},{8,0},{1,9},{9,1},{2,10},{10,2},{3,11},{11,3},{4,12},{12,4},... | collective-permute-start | bytes 786440 | tf_op jit(solution)/shard_map/ppermute | solution.py:379
  35.7 27.1 %all-to-all-start = ((bf16[64,8,512]{2,1,0:T(8,128)(2,1)}), bf16[64,8,512]{2,1,0:T(8,128)(2,1)S(1)}, u32[]{:S(2)}, u32[]{:S(2)}) async-start(bf16[64,8,512]{2,1,0:T(8,128)(2,1)} %bitcast.5), calls=%async_computation | async-start | bytes 1048576 | tf_op jit(solution)/shard_map/all_to_all | solution.py:388
  45.9 17.0 %copy-start.1 = (bf16[256,256]{1,0:T(8,128)(2,1)S(1)}, bf16[256,256]{1,0:T(8,128)(2,1)}, u32[]{:S(2)}) copy-start(bf16[256,256]{1,0:T(8,128)(2,1)} %constant.39.clone.turn_ref) | copy-start | bytes 393220
  45.9 17.0 %copy-start.2 = (bf16[256,256]{1,0:T(8,128)(2,1)S(1)}, bf16[256,256]{1,0:T(8,128)(2,1)}, u32[]{:S(2)}) copy-start(bf16[256,256]{1,0:T(8,128)(2,1)} %constant.38.clone.enter_ref) | copy-start | bytes 393220
  45.9 17.0 %copy-start.3 = (bf16[64,64]{1,0:T(8,128)(2,1)S(1)}, bf16[64,64]{1,0:T(8,128)(2,1)}, u32[]{:S(2)}) copy-start(bf16[64,64]{1,0:T(8,128)(2,1)} %constant.40.clone.leave_ref) | copy-start | bytes 24580
  45.9 1.7 %collective-permute-start.4 = (bf16[8,64,256]{2,1,0:T(8,128)(2,1)S(1)}, bf16[8,64,256]{2,1,0:T(8,128)(2,1)S(1)}, u32[]{:S(2)}, u32[]{:S(2)}) collective-permute-start(bf16[8,64,256]{2,1,0:T(8,128)(2,1)S(1)} %bitcast.17), channel_id=1, source_target_pairs={{0,1},{1,0},{2,3},{3,2},{4,5},{5,4},{6,7},{7,6},{8,9},{9,8},{10,11... | collective-permute-start | bytes 786440 | tf_op jit(solution)/shard_map/ppermute | solution.py:379
  46.4 1.5 %collective-permute-start.6 = (bf16[8,64,256]{2,1,0:T(8,128)(2,1)S(1)}, bf16[8,64,256]{2,1,0:T(8,128)(2,1)S(1)}, u32[]{:S(2)}, u32[]{:S(2)}) collective-permute-start(bf16[8,64,256]{2,1,0:T(8,128)(2,1)S(1)} %collective-permute-done.5.refs_2_.refs_6_), channel_id=1, source_target_pairs={{0,1},{1,0},{2,3},{3,2},{4,5},{5,4},{6,7},{7,6},{8,9},{9,8},{10,11... | collective-permute-start | bytes 786440 | tf_op jit(solution)/shard_map/ppermute | solution.py:379
  62.8 37.4 %copy-start = (bf16[4,256,256]{2,1,0:T(8,128)(2,1)S(1)}, bf16[4,256,256]{2,1,0:T(8,128)(2,1)}, u32[]{:S(2)}) copy-start(bf16[4,256,256]{2,1,0:T(8,128)(2,1)} %constant.41.clone.pick_ref) | copy-start | bytes 1572868
  89.6 5.2 %collective-permute-start.8 = (bf16[512,256]{1,0:T(8,128)(2,1)S(1)}, bf16[512,256]{1,0:T(8,128)(2,1)S(1)}, u32[]{:S(2)}, u32[]{:S(2)}) collective-permute-start(bf16[512,256]{1,0:T(8,128)(2,1)S(1)} %bitcast.13), channel_id=1, source_target_pairs={{0,8},{8,0},{1,9},{9,1},{2,10},{10,2},{3,11},{11,3},{4,12},{12,4},... | collective-permute-start | bytes 786440 | tf_op jit(solution)/shard_map/ppermute | solution.py:379
  90.6 8.4 %collective-permute-start.7 = (bf16[512,256]{1,0:T(8,128)(2,1)S(1)}, bf16[512,256]{1,0:T(8,128)(2,1)S(1)}, u32[]{:S(2)}, u32[]{:S(2)}) collective-permute-start(bf16[512,256]{1,0:T(8,128)(2,1)S(1)} %bitcast.14), channel_id=1, source_target_pairs={{0,1},{1,0},{2,3},{3,2},{4,5},{5,4},{6,7},{7,6},{8,9},{9,8},{10,11... | collective-permute-start | bytes 786440 | tf_op jit(solution)/shard_map/ppermute | solution.py:379
  94.9 5.4 %collective-permute-start.9 = (bf16[512,256]{1,0:T(8,128)(2,1)S(1)}, bf16[512,256]{1,0:T(8,128)(2,1)S(1)}, u32[]{:S(2)}, u32[]{:S(2)}) collective-permute-start(bf16[512,256]{1,0:T(8,128)(2,1)S(1)} %collective-permute-done.8.n2), channel_id=1, source_target_pairs={{0,1},{1,0},{2,3},{3,2},{4,5},{5,4},{6,7},{7,6},{8,9},{9,8},{10,11... | collective-permute-start | bytes 786440 | tf_op jit(solution)/shard_map/ppermute | solution.py:379

commit v9 on v8

--- a/solution.py
+++ b/solution.py
@@ -167,31 +167,34 @@
     return (a.astype(F32) + b.astype(F32)).astype(BF)
 
 
-def first_kernel(kept, come, out_ref):
-    out_ref[...] = add(kept[0], come[0])
-
-
-def first_sum(kept, come):
-    return pl.pallas_call(
-        first_kernel,
+def part_kernel(part):
+    def kernel(kept, come, out_ref):
+        out_ref[...] = add(kept[part], come[part])
+
+    return kernel
+
+
+def part_sum(kept, come, part):
+    return pl.pallas_call(
+        part_kernel(part),
         out_shape=jax.ShapeDtypeStruct((256, CHEB), BF),
         in_specs=[pl.BlockSpec(memory_space=pltpu.VMEM)] * 2,
         out_specs=pl.BlockSpec(memory_space=pltpu.VMEM),
         compiler_params=params(8),
-        name="first_sum",
+        name=f"part_sum{part}",
     )(kept, come)
 
 
-def sum_kernel(keep0, come0, again0, keep1, come1, again1, out_ref):
-    for half, (kept, come, again) in enumerate(((keep0, come0, again0), (keep1, come1, again1))):
-        out_ref[half] = add(add(kept[1], come[1]), again[...])
+def sum_kernel(kept0, again0, kept1, again1, out_ref):
+    out_ref[0] = add(kept0[...], again0[...])
+    out_ref[1] = add(kept1[...], again1[...])
 
 
 def sums(*args):
     return pl.pallas_call(
         sum_kernel,
         out_shape=jax.ShapeDtypeStruct((2, 256, CHEB), BF),
-        in_specs=[pl.BlockSpec(memory_space=pltpu.VMEM)] * 6,
+        in_specs=[pl.BlockSpec(memory_space=pltpu.VMEM)] * 4,
         out_specs=pl.BlockSpec(memory_space=pltpu.VMEM),
         compiler_params=params(8),
         name="sums",
@@ -397,9 +400,9 @@
     send0, send1, keep0, keep1, phases = rotate(place, weights, angles)
     come0, come1 = swap(send0, "y4"), swap(send1, "z4")
     phases = exchange(phases.reshape(64, 8, HALF), ("x4", "y4", "z4", "x3", "y3", "z3"))
-    again0, again1 = first_sum(keep0, come0), first_sum(keep1, come1)
+    again0, again1 = part_sum(keep0, come0, 0), part_sum(keep1, come1, 0)
     again0, again1 = swap(again0, "z4"), swap(again1, "y4")
-    share = sums(keep0, come0, again0, keep1, come1, again1)
+    share = sums(part_sum(keep0, come0, 1), again0, part_sum(keep1, come1, 1), again1)
     phases, _ = lax.optimization_barrier((phases, share))
     near = four(phases.reshape(8, 64, HALF))
     share = exchange(share.reshape(64, 8, CHEB), ("x4", "x3", "y3", "z3", "y2", "z2"))

time: 104 us -> 104 us (level)
  no operation moved by 1% of the time
where the time goes in v9:
time: 104 us
  starting transfers between devices  42.3 us (41%)
  blocking collectives  21.5 us (21%)
  waiting for transfers between devices  20.4 us (20%)
  Pallas kernels  19.2 us (18%)
    ppermute x10, starting transfers between devices, swap(): return lax.ppermute(value, axis, [(0, 1), (1, 0)])  21.5 us
    all_to_all x1, blocking collectives, exchange(): return lax.all_to_all(value, axes, split_axis=0, concat_axis=0, tiled=True)  21.5 us
    all_to_all x2, starting transfers between devices, exchange(): return lax.all_to_all(value, axes, split_axis=0, concat_axis=0, tiled=True)  20.8 us
    ppermute x10, waiting for transfers between devices, swap(): return lax.ppermute(value, axis, [(0, 1), (1, 0)])  10.6 us
    all_to_all x2, waiting for transfers between devices, exchange(): return lax.all_to_all(value, axes, split_axis=0, concat_axis=0, tiled=True)  9.74 us
    pallas_call x1, Pallas kernels, levels(): pl.pallas_call(levels_kernel, out_shape=[jax.ShapeDtypeStruct((8, 8, 8, H...  5.53 us
    pallas_call x1, Pallas kernels, trig(): pl.pallas_call(trig_kernel, grid_spec=spec, out_shape=[jax.ShapeDtypeStru...  5.12 us
    pallas_call x1, Pallas kernels, rotate(): pl.pallas_call(rotate_kernel, out_shape=[piece] * 4 + [jax.ShapeDtypeStru...  4.42 us
  transfers between devices with their start and end apart: 12, of which 7 were waited for; matrix products, arithmetic and copies ran while one was open for 0% of the time, Pallas kernels for 6%

profile of v9, /device:TPU:1, one launch (start us, length us, event | category | flops | bytes accessed | tf_op | source)
XLA Modules:
  0.0 103.8 jit_solution(2170309065131538770)
XLA Ops:
  0.0 0.1 pad_add_fusion.place
  0.1 4.4 %rotate.1 = (bf16[2,256,512]{2,1,0:T(8,128)(2,1)S(1)}, bf16[2,256,512]{2,1,0:T(8,128)(2,1)}, bf16[2,256,512]{2,1,0:T(8,128)(2,1)S(1)}, bf16[2,256,512]{2,1,0:T(8,128)(2,1)S(1)}, bf16[2,4,64,256]{3,2,1,0:T(8,128)(2,1)}) custom-call(s32[3]{0:T(128)S(1)} %pad_add_fusion.place, bf16[2,4,256,512]{3,2,1,0:T(8,128)(2,1)} %bitcast.21, ...), custom_call_target="tpu_custom_call" | custom-call | tf_op jit(solution)/shard_map/rotate/pallas_call | solution.py:145
  4.5 3.7 %collective-permute-start = (bf16[2,256,512]{2,1,0:T(8,128)(2,1)S(1)}, bf16[2,256,512]{2,1,0:T(8,128)(2,1)S(1)}, u32[]{:S(2)}, u32[]{:S(2)}) collective-permute-start(bf16[2,256,512]{2,1,0:T(8,128)(2,1)S(1)} %get-tuple-element.16), channel_id=1, source_target_pairs={{0,32},{32,0},{1,33},{33,1},{2,34},{34,2},{3,35},{35,3},{4,36},{36... | collective-permute-start | bytes 1572872 | tf_op jit(solution)/shard_map/ppermute | solution.py:382
  8.2 2.9 %collective-permute-start.2 = (bf16[2,256,512]{2,1,0:T(8,128)(2,1)}, bf16[2,256,512]{2,1,0:T(8,128)(2,1)S(1)}, u32[]{:S(2)}, u32[]{:S(2)}) collective-permute-start(bf16[2,256,512]{2,1,0:T(8,128)(2,1)} %get-tuple-element.18), channel_id=1, source_target_pairs={{0,4},{4,0},{1,5},{5,1},{2,6},{6,2},{3,7},{7,3},{8,12},{12,8},{9,1... | collective-permute-start | bytes 1572872 | tf_op jit(solution)/shard_map/ppermute | solution.py:382
  11.1 10.3 %all-to-all-start.1 = ((bf16[64,8,256]{2,1,0:T(8,128)(2,1)}), bf16[64,8,256]{2,1,0:T(8,128)(2,1)S(1)}, u32[]{:S(2)}, u32[]{:S(2)}) async-start(bf16[64,8,256]{2,1,0:T(8,128)(2,1)} %bitcast.7), calls=%async_computation.1 | async-start | bytes 524288 | tf_op jit(solution)/shard_map/all_to_all | solution.py:391
  21.4 0.1 part_sum0.2
  21.4 2.6 %collective-permute-start.1 = (bf16[256,512]{1,0:T(8,128)(2,1)S(1)}, bf16[256,512]{1,0:T(8,128)(2,1)S(1)}, u32[]{:S(2)}, u32[]{:S(2)}) collective-permute-start(bf16[256,512]{1,0:T(8,128)(2,1)S(1)} %part_sum0.2), channel_id=1, source_target_pairs={{0,4},{4,0},{1,5},{5,1},{2,6},{6,2},{3,7},{7,3},{8,12},{12,8},{9,1... | collective-permute-start | bytes 786440 | tf_op jit(solution)/shard_map/ppermute | solution.py:382
  24.0 0.1 part_sum0.3
  24.1 2.8 %collective-permute-start.3 = (bf16[256,512]{1,0:T(8,128)(2,1)S(1)}, bf16[256,512]{1,0:T(8,128)(2,1)S(1)}, u32[]{:S(2)}, u32[]{:S(2)}) collective-permute-start(bf16[256,512]{1,0:T(8,128)(2,1)S(1)} %part_sum0.3), channel_id=1, source_target_pairs={{0,32},{32,0},{1,33},{33,1},{2,34},{34,2},{3,35},{35,3},{4,36},{36... | collective-permute-start | bytes 786440 | tf_op jit(solution)/shard_map/ppermute | solution.py:382
  26.9 0.1 part_sum1.2.kept0
  27.0 0.1 part_sum1.3.kept1
  27.1 4.2 %collective-permute-done.1.again0 = bf16[256,512]{1,0:T(8,128)(2,1)S(1)} collective-permute-done((bf16[256,512]{1,0:T(8,128)(2,1)S(1)}, bf16[256,512]{1,0:T(8,128)(2,1)S(1)}, u32[]{:S(2)}, u32[]{:S(2)}) %collective-permute-start.1) | collective-permute-done | bytes 262176 | tf_op jit(solution)/shard_map/ppermute | solution.py:382
  31.2 2.9 %collective-permute-done.3.again1 = bf16[256,512]{1,0:T(8,128)(2,1)S(1)} collective-permute-done((bf16[256,512]{1,0:T(8,128)(2,1)S(1)}, bf16[256,512]{1,0:T(8,128)(2,1)S(1)}, u32[]{:S(2)}, u32[]{:S(2)}) %collective-permute-start.3) | collective-permute-done | bytes 262176 | tf_op jit(solution)/shard_map/ppermute | solution.py:382
  34.1 0.9 sums.1
  35.0 0.5 collective-permute-start.5
  35.6 10.5 %all-to-all-start = ((bf16[64,8,512]{2,1,0:T(8,128)(2,1)}), bf16[64,8,512]{2,1,0:T(8,128)(2,1)S(1)}, u32[]{:S(2)}, u32[]{:S(2)}) async-start(bf16[64,8,512]{2,1,0:T(8,128)(2,1)} %bitcast.5), calls=%async_computation | async-start | bytes 1048576 | tf_op jit(solution)/shard_map/all_to_all | solution.py:391
  46.1 0.0 copy-start.1
  46.1 0.0 copy-start.2
  46.1 0.5 collective-permute-start.4
  46.7 0.1 collective-permute-start.6
  46.8 1.1 %collective-permute-done.4.refs_1_.refs_5_ = bf16[8,64,256]{2,1,0:T(8,128)(2,1)S(1)} collective-permute-done((bf16[8,64,256]{2,1,0:T(8,128)(2,1)S(1)}, bf16[8,64,256]{2,1,0:T(8,128)(2,1)S(1)}, u32[]{:S(2)}, u32[]{:S(2)}) %collective-permute-start.4) | collective-permute-done | bytes 262176 | tf_op jit(solution)/shard_map/ppermute | solution.py:382
  47.8 0.4 collective-permute-done.6.refs_3_.refs_7_
  48.2 5.1 %trig.1 = (f32[8,2,64,512]{3,2,1,0:T(8,128)S(1)}, f32[8,2,64,512]{3,2,1,0:T(8,128)}) custom-call(s32[3]{0:T(128)S(1)} %pad_add_fusion.place, bf16[8,64,256]{2,1,0:T(8,128)(2,1)S(1)} %bitcast.18, bf16[8,64,256]{2,1,0:T(8,128)(2,1)S(1)} %collective-permute-done.4.refs_1_.refs_5_, bf16[8,64,256]{2,1,0:T(8,128)(2,1)S(1)} %collective-permute-done.5.refs_2_.refs_6_, ...), custom_call_target="tpu_custom_call" | custom-call | flops 7000000000 | bytes 1000000 | tf_op jit(solution)/shard_map/trig/pallas_call | solution.py:244
  53.3 9.7 %all-to-all-done = bf16[64,8,512]{2,1,0:T(8,128)(2,1)S(1)} async-done(((bf16[64,8,512]{2,1,0:T(8,128)(2,1)}), bf16[64,8,512]{2,1,0:T(8,128)(2,1)S(1)}, u32[]{:S(2)}, u32[]{:S(2)}) %all-to-all-start) | async-done | bytes 524320 | tf_op jit(solution)/shard_map/all_to_all | solution.py:391
  63.1 5.5 %levels.1 = (bf16[8,8,8,256]{3,2,1,0:T(8,128)(2,1)S(1)}, bf16[2,512,512]{2,1,0:T(8,128)(2,1)S(1)}) custom-call(s32[3]{0:T(128)S(1)} %pad_add_fusion.place, bf16[2,256,512]{2,1,0:T(8,128)(2,1)S(1)} %bitcast.12, bf16[8,512,512]{2,1,0:T(8,128)(2,1)} %t_hbm.1, f32[8,2,64,512]{3,2,1,0:T(8,128)S(1)} %get-tuple-element.21.wave1_ref, ...), custom_call_target="tpu_custom_call" | custom-call | tf_op jit(solution)/shard_map/levels/pallas_call | solution.py:311
  68.6 21.5 %all_to_all.15 = bf16[64,8,256]{2,1,0:T(8,128)(2,1)S(1)} all-to-all(bf16[64,8,256]{2,1,0:T(8,128)(2,1)S(1)} %bitcast.20), channel_id=1, replica_groups=mesh['x4'=2,'x3'=2,'y4'=2,'y3'=2,'y2'=2,'z4'=2,'z3'=2,'z2'=2] {'y4','z4'..., dimensions={0} | all-to-all | bytes 524288 | tf_op jit(solution)/shard_map/all_to_all | solution.py:391
  90.2 0.9 collective-permute-start.8
  91.1 3.3 %collective-permute-start.7 = (bf16[512,256]{1,0:T(8,128)(2,1)S(1)}, bf16[512,256]{1,0:T(8,128)(2,1)S(1)}, u32[]{:S(2)}, u32[]{:S(2)}) collective-permute-start(bf16[512,256]{1,0:T(8,128)(2,1)S(1)} %bitcast.14), channel_id=1, source_target_pairs={{0,1},{1,0},{2,3},{3,2},{4,5},{5,4},{6,7},{7,6},{8,9},{9,8},{10,11... | collective-permute-start | bytes 786440 | tf_op jit(solution)/shard_map/ppermute | solution.py:382
  94.4 1.0 collective-permute-done.8.n2
  95.4 4.1 %collective-permute-start.9 = (bf16[512,256]{1,0:T(8,128)(2,1)S(1)}, bf16[512,256]{1,0:T(8,128)(2,1)S(1)}, u32[]{:S(2)}, u32[]{:S(2)}) collective-permute-start(bf16[512,256]{1,0:T(8,128)(2,1)S(1)} %collective-permute-done.8.n2), channel_id=1, source_target_pairs={{0,1},{1,0},{2,3},{3,2},{4,5},{5,4},{6,7},{7,6},{8,9},{9,8},{10,11... | collective-permute-start | bytes 786440 | tf_op jit(solution)/shard_map/ppermute | solution.py:382
  99.5 1.2 %collective-permute-done.9.n3 = bf16[512,256]{1,0:T(8,128)(2,1)S(1)} collective-permute-done((bf16[512,256]{1,0:T(8,128)(2,1)S(1)}, bf16[512,256]{1,0:T(8,128)(2,1)S(1)}, u32[]{:S(2)}, u32[]{:S(2)}) %collective-permute-start.9) | collective-permute-done | bytes 262176 | tf_op jit(solution)/shard_map/ppermute | solution.py:382
  100.7 2.9 %final.1 = bf16[2,1024,512]{2,1,0:T(8,128)(2,1)} custom-call(s32[3]{0:T(128)S(1)} %pad_add_fusion.place, bf16[512,256]{1,0:T(8,128)(2,1)S(1)} %bitcast.15, bf16[512,256]{1,0:T(8,128)(2,1)S(1)} %collective-permute-done.7.n1, bf16[512,256]{1,0:T(8,128)(2,1)S(1)} %collective-permute-done.8.n2, bf16[512,256]{1,0:T(8,128)(2,1)S(1)} %collective-permute-done.9.n3, ...), custom_call_target="tpu_custom_call" | custom-call | tf_op jit(solution)/shard_map/final/pallas_call | solution.py:366
  (11 shorter events, 0.0 us)
Async XLA Ops:
  4.5 16.8 %collective-permute-start = (bf16[2,256,512]{2,1,0:T(8,128)(2,1)S(1)}, bf16[2,256,512]{2,1,0:T(8,128)(2,1)S(1)}, u32[]{:S(2)}, u32[]{:S(2)}) collective-permute-start(bf16[2,256,512]{2,1,0:T(8,128)(2,1)S(1)} %get-tuple-element.16), channel_id=1, source_target_pairs={{0,32},{32,0},{1,33},{33,1},{2,34},{34,2},{3,35},{35,3},{4,36},{36... | collective-permute-start | bytes 1572872 | tf_op jit(solution)/shard_map/ppermute | solution.py:382
  8.2 15.9 %collective-permute-start.2 = (bf16[2,256,512]{2,1,0:T(8,128)(2,1)}, bf16[2,256,512]{2,1,0:T(8,128)(2,1)S(1)}, u32[]{:S(2)}, u32[]{:S(2)}) collective-permute-start(bf16[2,256,512]{2,1,0:T(8,128)(2,1)} %get-tuple-element.18), channel_id=1, source_target_pairs={{0,4},{4,0},{1,5},{5,1},{2,6},{6,2},{3,7},{7,3},{8,12},{12,8},{9,1... | collective-permute-start | bytes 1572872 | tf_op jit(solution)/shard_map/ppermute | solution.py:382
  11.1 24.0 %all-to-all-start.1 = ((bf16[64,8,256]{2,1,0:T(8,128)(2,1)}), bf16[64,8,256]{2,1,0:T(8,128)(2,1)S(1)}, u32[]{:S(2)}, u32[]{:S(2)}) async-start(bf16[64,8,256]{2,1,0:T(8,128)(2,1)} %bitcast.7), calls=%async_computation.1 | async-start | bytes 524288 | tf_op jit(solution)/shard_map/all_to_all | solution.py:391
  21.4 9.8 %collective-permute-start.1 = (bf16[256,512]{1,0:T(8,128)(2,1)S(1)}, bf16[256,512]{1,0:T(8,128)(2,1)S(1)}, u32[]{:S(2)}, u32[]{:S(2)}) collective-permute-start(bf16[256,512]{1,0:T(8,128)(2,1)S(1)} %part_sum0.2), channel_id=1, source_target_pairs={{0,4},{4,0},{1,5},{5,1},{2,6},{6,2},{3,7},{7,3},{8,12},{12,8},{9,1... | collective-permute-start | bytes 786440 | tf_op jit(solution)/shard_map/ppermute | solution.py:382
  24.1 10.0 %collective-permute-start.3 = (bf16[256,512]{1,0:T(8,128)(2,1)S(1)}, bf16[256,512]{1,0:T(8,128)(2,1)S(1)}, u32[]{:S(2)}, u32[]{:S(2)}) collective-permute-start(bf16[256,512]{1,0:T(8,128)(2,1)S(1)} %part_sum0.3), channel_id=1, source_target_pairs={{0,32},{32,0},{1,33},{33,1},{2,34},{34,2},{3,35},{35,3},{4,36},{36... | collective-permute-start | bytes 786440 | tf_op jit(solution)/shard_map/ppermute | solution.py:382
  35.0 11.6 %collective-permute-start.5 = (bf16[8,64,256]{2,1,0:T(8,128)(2,1)S(1)}, bf16[8,64,256]{2,1,0:T(8,128)(2,1)S(1)}, u32[]{:S(2)}, u32[]{:S(2)}) collective-permute-start(bf16[8,64,256]{2,1,0:T(8,128)(2,1)S(1)} %bitcast.16), channel_id=1, source_target_pairs={{0,8},{8,0},{1,9},{9,1},{2,10},{10,2},{3,11},{11,3},{4,12},{12,4},... | collective-permute-start | bytes 786440 | tf_op jit(solution)/shard_map/ppermute | solution.py:382
  35.6 27.5 %all-to-all-start = ((bf16[64,8,512]{2,1,0:T(8,128)(2,1)}), bf16[64,8,512]{2,1,0:T(8,128)(2,1)S(1)}, u32[]{:S(2)}, u32[]{:S(2)}) async-start(bf16[64,8,512]{2,1,0:T(8,128)(2,1)} %bitcast.5), calls=%async_computation | async-start | bytes 1048576 | tf_op jit(solution)/shard_map/all_to_all | solution.py:391
  46.1 17.0 %copy-start.1 = (bf16[256,256]{1,0:T(8,128)(2,1)S(1)}, bf16[256,256]{1,0:T(8,128)(2,1)}, u32[]{:S(2)}) copy-start(bf16[256,256]{1,0:T(8,128)(2,1)} %constant.39.clone.turn_ref) | copy-start | bytes 393220
  46.1 17.0 %copy-start.2 = (bf16[256,256]{1,0:T(8,128)(2,1)S(1)}, bf16[256,256]{1,0:T(8,128)(2,1)}, u32[]{:S(2)}) copy-start(bf16[256,256]{1,0:T(8,128)(2,1)} %constant.38.clone.enter_ref) | copy-start | bytes 393220
  46.1 17.0 %copy-start.3 = (bf16[64,64]{1,0:T(8,128)(2,1)S(1)}, bf16[64,64]{1,0:T(8,128)(2,1)}, u32[]{:S(2)}) copy-start(bf16[64,64]{1,0:T(8,128)(2,1)} %constant.40.clone.leave_ref) | copy-start | bytes 24580
  46.1 1.7 %collective-permute-start.4 = (bf16[8,64,256]{2,1,0:T(8,128)(2,1)S(1)}, bf16[8,64,256]{2,1,0:T(8,128)(2,1)S(1)}, u32[]{:S(2)}, u32[]{:S(2)}) collective-permute-start(bf16[8,64,256]{2,1,0:T(8,128)(2,1)S(1)} %bitcast.17), channel_id=1, source_target_pairs={{0,1},{1,0},{2,3},{3,2},{4,5},{5,4},{6,7},{7,6},{8,9},{9,8},{10,11... | collective-permute-start | bytes 786440 | tf_op jit(solution)/shard_map/ppermute | solution.py:382
  46.7 1.5 %collective-permute-start.6 = (bf16[8,64,256]{2,1,0:T(8,128)(2,1)S(1)}, bf16[8,64,256]{2,1,0:T(8,128)(2,1)S(1)}, u32[]{:S(2)}, u32[]{:S(2)}) collective-permute-start(bf16[8,64,256]{2,1,0:T(8,128)(2,1)S(1)} %collective-permute-done.5.refs_2_.refs_6_), channel_id=1, source_target_pairs={{0,1},{1,0},{2,3},{3,2},{4,5},{5,4},{6,7},{7,6},{8,9},{9,8},{10,11... | collective-permute-start | bytes 786440 | tf_op jit(solution)/shard_map/ppermute | solution.py:382
  63.1 37.6 %copy-start = (bf16[4,256,256]{2,1,0:T(8,128)(2,1)S(1)}, bf16[4,256,256]{2,1,0:T(8,128)(2,1)}, u32[]{:S(2)}) copy-start(bf16[4,256,256]{2,1,0:T(8,128)(2,1)} %constant.41.clone.pick_ref) | copy-start | bytes 1572868
  90.2 5.2 %collective-permute-start.8 = (bf16[512,256]{1,0:T(8,128)(2,1)S(1)}, bf16[512,256]{1,0:T(8,128)(2,1)S(1)}, u32[]{:S(2)}, u32[]{:S(2)}) collective-permute-start(bf16[512,256]{1,0:T(8,128)(2,1)S(1)} %bitcast.13), channel_id=1, source_target_pairs={{0,8},{8,0},{1,9},{9,1},{2,10},{10,2},{3,11},{11,3},{4,12},{12,4},... | collective-permute-start | bytes 786440 | tf_op jit(solution)/shard_map/ppermute | solution.py:382
  91.1 8.4 %collective-permute-start.7 = (bf16[512,256]{1,0:T(8,128)(2,1)S(1)}, bf16[512,256]{1,0:T(8,128)(2,1)S(1)}, u32[]{:S(2)}, u32[]{:S(2)}) collective-permute-start(bf16[512,256]{1,0:T(8,128)(2,1)S(1)} %bitcast.14), channel_id=1, source_target_pairs={{0,1},{1,0},{2,3},{3,2},{4,5},{5,4},{6,7},{7,6},{8,9},{9,8},{10,11... | collective-permute-start | bytes 786440 | tf_op jit(solution)/shard_map/ppermute | solution.py:382
  95.4 5.3 %collective-permute-start.9 = (bf16[512,256]{1,0:T(8,128)(2,1)S(1)}, bf16[512,256]{1,0:T(8,128)(2,1)S(1)}, u32[]{:S(2)}, u32[]{:S(2)}) collective-permute-start(bf16[512,256]{1,0:T(8,128)(2,1)S(1)} %collective-permute-done.8.n2), channel_id=1, source_target_pairs={{0,1},{1,0},{2,3},{3,2},{4,5},{5,4},{6,7},{7,6},{8,9},{9,8},{10,11... | collective-permute-start | bytes 786440 | tf_op jit(solution)/shard_map/ppermute | solution.py:382
